TPU v7x, 512 devices: a whole 4x4x16 slice. The times are simulated.
512 devices in a mesh: tok: 32 (over z, y_lo), feat: 16 (over x, y_hi, core).
Axes of the slice: x: 4, y: 4 (y_hi: 2, y_lo: 2; y = y_hi * 2 + y_lo), z: 16, core: 2. Of those that a mesh axis runs over, the one named last changes fastest.
Arguments:
- tokens: bfloat16 [512, 12288], P('tok', 'feat'), may hold values from -6 to 6
- up_weight: bfloat16 [16, 3072, 5, 768], P('feat', 'tok'), may hold values from -0.09375 to 0.09375
- down_weight: bfloat16 [16, 3072, 5, 768], P('feat', 'tok'), may hold values from -0.046875 to 0.046875
- up_left: bfloat16 [12288, 512], P('feat'), may hold values from -0.0546875 to 0.0546875
- up_right: bfloat16 [16, 3072, 512], P('feat', 'tok'), may hold values from -0.25 to 0.25
- down_left: bfloat16 [16, 3072, 512], P('feat', 'tok'), may hold values from -0.02734375 to 0.02734375
- down_right: bfloat16 [512, 12288], P(None, 'feat'), may hold values from -0.25 to 0.25
Outputs:
- mixed: bfloat16 [512, 12288], P('tok', 'feat')
All inputs are finite; a program needn't handle non-finite values.
Results may differ from a plain program's by a relative error of at most 0.0058.
Values may be sent and summed in bfloat16 or wider, within the bound.
No kernel may reach another device: no remote copies, remote signals or barrier semaphores. Data moves between devices by JAX's collectives and lax.ppermute only.
A program may use at most 64 MiB of HBM per device.

v0:
```python
import jax
import jax.numpy as jnp
from jax import lax
from jax.sharding import PartitionSpec as P


def from_partner(array, axis, bit):
    return lax.ppermute(array, axis, [(i, i ^ 1 << bit) for i in range(lax.axis_size(axis))])


def per_device(tokens, up_weight, down_weight, up_left, up_right, down_left, down_right):
    levels = lax.axis_size("feat").bit_length() - 1
    gathered = lax.all_gather(tokens, "tok", axis=0, tiled=True)
    pieces = [gathered]
    for level in range(levels):
        pieces.append(from_partner(gathered, "feat", level))
    stacked = jnp.stack(pieces, axis=1)
    code_part = jnp.dot(tokens, up_left, preferred_element_type=jnp.float32)
    code = lax.psum(code_part, "feat").astype(jnp.bfloat16)
    code = lax.all_gather(code, "tok", axis=0, tiled=True)
    pre = jnp.einsum("rkd,tkd->rt", up_weight[0], stacked, preferred_element_type=jnp.float32)
    pre = pre + lax.dot_general(
        up_right[0], code, (((1,), (1,)), ((), ())), preferred_element_type=jnp.float32
    )
    hidden = jax.nn.gelu(pre, approximate=False).astype(jnp.bfloat16)
    local_down = down_weight[0]
    terms = jnp.einsum("rt,rkd->tkd", hidden, local_down, preferred_element_type=jnp.float32)
    total = terms[:, 0, :]
    for level in range(levels):
        total = total + from_partner(terms[:, level + 1, :], "feat", level)
    back_part = lax.dot_general(
        hidden, down_left[0], (((0,), (0,)), ((), ())), preferred_element_type=jnp.float32
    )
    total, back = (
        lax.psum_scatter(total, "tok", scatter_dimension=0, tiled=True),
        lax.psum_scatter(back_part, "tok", scatter_dimension=0, tiled=True),
    )
    back = lax.psum(back, "feat")
    mixed = total + jnp.dot(
        back.astype(jnp.bfloat16), down_right, preferred_element_type=jnp.float32
    )
    return mixed.astype(jnp.bfloat16)


def solution(mesh):
    return jax.shard_map(
        per_device,
        mesh=mesh,
        in_specs=(
            P("tok", "feat"),
            P("feat", "tok", None, None),
            P("feat", "tok", None, None),
            P("feat", None),
            P("feat", "tok", None),
            P("feat", "tok", None),
            P(None, "feat"),
        ),
        out_specs=P("tok", "feat"),
        check_vma=False,
    )
```

profile of v0, /device:TPU:6, one launch (start us, length us, event | category | flops | bytes accessed | tf_op | source)
XLA Modules:
  0.0 508.4 jit_solution(7923499260121274680)
XLA Ops:
  6.5 0.0 copy-start
  6.5 0.0 reduce-scatter.5.cloned.1.call-start
  6.5 74.2 %all_gather.6 = bf16[512,768]{1,0:T(8,128)(2,1)S(1)} all-gather(bf16[16,768]{1,0:T(8,128)(2,1)} %param.7), channel_id=1, replica_groups=mesh['tok'=32,'feat'=16] {'tok'}, dimensions={0}, use_global_device_ids=true | all-gather | bytes 811008 | tf_op jit(solution)/shard_map/all_gather | solution.py:13
  80.7 3.2 collective-permute-start.3
  83.9 1.9 collective-permute-start.2
  85.9 4.4 collective-permute-start.1
  90.2 1.9 collective-permute-start
  92.2 1.4 fusion.35
  93.5 62.8 %psum.14 = bf16[16,512]{1,0:T(8,128)(2,1)S(1)} all-reduce(f32[16,512]{1,0:T(8,128)S(1)} %fusion.35), channel_id=1, replica_groups=mesh['tok'=32,'feat'=16] {'feat'}, use_global_device_ids=true, to_apply=%region_0.0 | all-reduce | flops 8192 | bytes 49152 | tf_op jit(solution)/shard_map/psum | solution.py:19
  156.3 61.4 %all_gather.7 = bf16[512,512]{1,0:T(8,128)(2,1)S(1)} all-gather(bf16[16,512]{1,0:T(8,128)(2,1)S(1)} %psum.14), channel_id=1, replica_groups=mesh['tok'=32,'feat'=16] {'tok'}, dimensions={0}, use_global_device_ids=true | all-gather | bytes 540672 | tf_op jit(solution)/shard_map/all_gather | solution.py:20
  217.6 1.2 fusion.31
  218.8 0.0 copy-start.3
  218.8 0.1 bitcast_dynamic-update-slice_fusion.4
  218.9 0.0 collective-permute-done
  218.9 1.2 bitcast_dynamic-update-slice_fusion.3
  220.2 0.0 collective-permute-done.1
  220.2 1.2 bitcast_dynamic-update-slice_fusion.2
  221.4 0.0 collective-permute-done.2
  221.4 0.1 bitcast_dynamic-update-slice_fusion.1
  221.4 0.0 collective-permute-done.3
  221.4 0.1 bitcast_dynamic-update-slice_fusion
  221.5 0.0 copy-done.3
  221.5 0.0 copy-start.2
  221.5 0.0 copy-start.1
  221.5 1.7 fusion.10
  223.2 0.0 copy-done.2
  223.3 1.3 fusion.28
  224.6 0.0 reduce-scatter.5.cloned.1.call-update
  224.6 0.0 reduce-scatter.3.cloned.1.call-start
  224.6 0.0 copy-done.1
  224.6 1.2 fusion.5
  225.8 0.6 slice_bitcast_fusion.3
  226.4 1.9 collective-permute-start.4
  228.4 4.2 collective-permute-start.7
  232.6 6.5 %collective-permute-start.6 = (f32[512,768]{1,0:T(8,128)S(1)}, f32[512,768]{1,0:T(8,128)S(1)}, u32[]{:S(2)}, u32[]{:S(2)}) collective-permute-start(f32[512,768]{1,0:T(8,128)S(1)} %get-tuple-element.7), channel_id=1, source_target_pairs={{0,4},{1,5},{2,6},{3,7},{4,0},{5,1},{6,2},{7,3},{8,12},{9,13},{10,... | collective-permute-start | bytes 4718600 | tf_op jit(solution)/shard_map/ppermute | solution.py:8
  239.0 1.9 collective-permute-start.5
  241.0 0.0 collective-permute-done.4
  241.0 28.1 %collective-permute-done.7 = f32[512,768]{1,0:T(8,128)S(1)} collective-permute-done((f32[512,768]{1,0:T(8,128)S(1)}, f32[512,768]{1,0:T(8,128)S(1)}, u32[]{:S(2)}, u32[]{:S(2)}) %collective-permute-start.7) | collective-permute-done | bytes 1572896 | tf_op jit(solution)/shard_map/ppermute | solution.py:8
  269.0 36.5 %collective-permute-done.6 = f32[512,768]{1,0:T(8,128)S(1)} collective-permute-done((f32[512,768]{1,0:T(8,128)S(1)}, f32[512,768]{1,0:T(8,128)S(1)}, u32[]{:S(2)}, u32[]{:S(2)}) %collective-permute-start.6) | collective-permute-done | bytes 1572896 | tf_op jit(solution)/shard_map/ppermute | solution.py:8
  305.6 0.0 collective-permute-done.5
  305.6 1.8 fusion.3
  307.4 0.0 reduce-scatter.3.cloned.1.call-update
  307.4 53.1 %reduce-scatter.5.cloned.1.call-done = f32[16,512]{1,0:T(8,128)} async-done(((f32[512,512]{1,0:T(8,128)}), f32[16,512]{1,0:T(8,128)}) %reduce-scatter.5.cloned.1.call-update) | async-done | bytes 32784 | tf_op jit(solution)/shard_map/reduce_scatter | solution.py:36
  360.5 56.6 %psum.15 = bf16[16,512]{1,0:T(8,128)(2,1)S(1)} all-reduce(f32[16,512]{1,0:T(8,128)} %reduce-scatter.5.cloned.1.call-done), channel_id=1, replica_groups=mesh['tok'=32,'feat'=16] {'feat'}, use_global_device_ids=true, to_apply=%region_3.0 | all-reduce | flops 8192 | bytes 49152 | tf_op jit(solution)/shard_map/psum | solution.py:38
  417.1 0.0 copy-done
  417.1 0.2 fusion.36
  417.3 82.8 %reduce-scatter.3.cloned.1.call-done = f32[16,768]{1,0:T(8,128)} async-done(((f32[512,768]{1,0:T(8,128)}), f32[16,768]{1,0:T(8,128)}) %reduce-scatter.3.cloned.1.call-update) | async-done | bytes 49168 | tf_op jit(solution)/shard_map/reduce_scatter | solution.py:35
  500.1 1.4 add_convert_fusion
Async XLA Ops:
  6.5 410.6 %copy-start = (bf16[512,768]{1,0:T(8,128)(2,1)S(1)}, bf16[512,768]{1,0:T(8,128)(2,1)}, u32[]{:S(2)}) copy-start(bf16[512,768]{1,0:T(8,128)(2,1)} %param.13) | copy-start | bytes 2359300
  6.5 354.0 %reduce-scatter.5.cloned.1.call-start = ((), (), s32[]{:S(2)}) async-start(), calls=%async_computation.3 | async-start | bytes 1081344 | tf_op jit(solution)/shard_map/reduce_scatter | solution.py:36
  80.7 140.7 %collective-permute-start.3 = (bf16[512,768]{1,0:T(8,128)(2,1)S(1)}, bf16[512,768]{1,0:T(8,128)(2,1)S(1)}, u32[]{:S(2)}, u32[]{:S(2)}) collective-permute-start(bf16[512,768]{1,0:T(8,128)(2,1)S(1)} %all_gather.6), channel_id=1, source_target_pairs={{0,8},{1,9},{2,10},{3,11},{4,12},{5,13},{6,14},{7,15},{8,0},{9,1},... | collective-permute-start | bytes 2359304 | tf_op jit(solution)/shard_map/ppermute | solution.py:8
  83.9 137.4 %collective-permute-start.2 = (bf16[512,768]{1,0:T(8,128)(2,1)S(1)}, bf16[512,768]{1,0:T(8,128)(2,1)S(1)}, u32[]{:S(2)}, u32[]{:S(2)}) collective-permute-start(bf16[512,768]{1,0:T(8,128)(2,1)S(1)} %all_gather.6), channel_id=1, source_target_pairs={{0,4},{1,5},{2,6},{3,7},{4,0},{5,1},{6,2},{7,3},{8,12},{9,13},{10,... | collective-permute-start | bytes 2359304 | tf_op jit(solution)/shard_map/ppermute | solution.py:8
  85.9 134.3 %collective-permute-start.1 = (bf16[512,768]{1,0:T(8,128)(2,1)S(1)}, bf16[512,768]{1,0:T(8,128)(2,1)}, u32[]{:S(2)}, u32[]{:S(2)}) collective-permute-start(bf16[512,768]{1,0:T(8,128)(2,1)S(1)} %all_gather.6), channel_id=1, source_target_pairs={{0,2},{1,3},{2,0},{3,1},{4,6},{5,7},{6,4},{7,5},{8,10},{9,11},{10,... | collective-permute-start | bytes 2359304 | tf_op jit(solution)/shard_map/ppermute | solution.py:8
  90.2 128.7 %collective-permute-start = (bf16[512,768]{1,0:T(8,128)(2,1)S(1)}, bf16[512,768]{1,0:T(8,128)(2,1)}, u32[]{:S(2)}, u32[]{:S(2)}) collective-permute-start(bf16[512,768]{1,0:T(8,128)(2,1)S(1)} %all_gather.6), channel_id=1, source_target_pairs={{0,1},{1,0},{2,3},{3,2},{4,5},{5,4},{6,7},{7,6},{8,9},{9,8},{10,11... | collective-permute-start | bytes 2359304 | tf_op jit(solution)/shard_map/ppermute | solution.py:8
  218.8 2.7 copy-start.3
  221.5 1.7 copy-start.2
  221.5 3.1 copy-start.1
  224.6 275.6 %reduce-scatter.3.cloned.1.call-start = ((), (), s32[]{:S(2)}) async-start(), calls=%async_computation.2 | async-start | bytes 1622016 | tf_op jit(solution)/shard_map/reduce_scatter | solution.py:35
  226.4 14.5 %collective-permute-start.4 = (f32[512,768]{1,0:T(8,128)S(1)}, f32[512,768]{1,0:T(8,128)S(1)}, u32[]{:S(2)}, u32[]{:S(2)}) collective-permute-start(f32[512,768]{1,0:T(8,128)S(1)} %get-tuple-element.5), channel_id=1, source_target_pairs={{0,1},{1,0},{2,3},{3,2},{4,5},{5,4},{6,7},{7,6},{8,9},{9,8},{10,11... | collective-permute-start | bytes 4718600 | tf_op jit(solution)/shard_map/ppermute | solution.py:8
  228.4 40.7 %collective-permute-start.7 = (f32[512,768]{1,0:T(8,128)S(1)}, f32[512,768]{1,0:T(8,128)S(1)}, u32[]{:S(2)}, u32[]{:S(2)}) collective-permute-start(f32[512,768]{1,0:T(8,128)S(1)} %get-tuple-element.6), channel_id=1, source_target_pairs={{0,8},{1,9},{2,10},{3,11},{4,12},{5,13},{6,14},{7,15},{8,0},{9,1},... | collective-permute-start | bytes 4718600 | tf_op jit(solution)/shard_map/ppermute | solution.py:8
  232.6 73.0 %collective-permute-start.6 = (f32[512,768]{1,0:T(8,128)S(1)}, f32[512,768]{1,0:T(8,128)S(1)}, u32[]{:S(2)}, u32[]{:S(2)}) collective-permute-start(f32[512,768]{1,0:T(8,128)S(1)} %get-tuple-element.7), channel_id=1, source_target_pairs={{0,4},{1,5},{2,6},{3,7},{4,0},{5,1},{6,2},{7,3},{8,12},{9,13},{10,... | collective-permute-start | bytes 4718600 | tf_op jit(solution)/shard_map/ppermute | solution.py:8
  239.0 66.5 %collective-permute-start.5 = (f32[512,768]{1,0:T(8,128)S(1)}, f32[512,768]{1,0:T(8,128)S(1)}, u32[]{:S(2)}, u32[]{:S(2)}) collective-permute-start(f32[512,768]{1,0:T(8,128)S(1)} %get-tuple-element.8), channel_id=1, source_target_pairs={{0,2},{1,3},{2,0},{3,1},{4,6},{5,7},{6,4},{7,5},{8,10},{9,11},{10,... | collective-permute-start | bytes 4718600 | tf_op jit(solution)/shard_map/ppermute | solution.py:8
Sparse Core Ops, SparseCore 0:
  224.7 135.7 reduce-scatter.4
  363.3 136.7 reduce-scatter.2
where the time goes:
time: 509 us; the launch traced here: 508 us
  blocking collectives  255 us (50%)
  waiting for transfers between devices  201 us (39%)
  starting transfers between devices  25.9 us (5%)
  between operations  13.6 us (3%)
  matrix products  6.95 us (1%)
    reduce_scatter x1, waiting for transfers between devices, per_device(): lax.psum_scatter(total, 'tok', scatter_dimension=0, tiled=True)  82.8 us
    all_gather x1, blocking collectives, per_device(): gathered = lax.all_gather(tokens, 'tok', axis=0, tiled=True)  74.2 us
    ppermute x8, waiting for transfers between devices, from_partner(): lax.ppermute(array, axis, [(i, i ^ 1 << bit) for i in range(lax.axis_size...  64.6 us
    psum x1, blocking collectives, per_device(): code = lax.psum(code_part, 'feat').astype(jnp.bfloat16)  62.8 us
    all_gather x1, blocking collectives, per_device(): code = lax.all_gather(code, 'tok', axis=0, tiled=True)  61.4 us
    psum x1, blocking collectives, per_device(): back = lax.psum(back, 'feat')  56.6 us
    reduce_scatter x1, waiting for transfers between devices, per_device(): lax.psum_scatter(back_part, 'tok', scatter_dimension=0, tiled=True)  53.1 us
    ppermute x8, starting transfers between devices, from_partner(): lax.ppermute(array, axis, [(i, i ^ 1 << bit) for i in range(lax.axis_size...  25.9 us
  transfers between devices with their start and end apart: 10, of which 4 were waited for; matrix products, arithmetic and copies ran while one was open for 2% of the time, Pallas kernels for 0%

commit v1 on v0

v1 whole, which is shorter than its diff:
```python
import jax
import jax.numpy as jnp
from jax import lax
from jax.sharding import Mesh, PartitionSpec as P


F32 = jnp.float32
BF16 = jnp.bfloat16
FEAT = ("x", "yh", "c")
LEVEL_AXES = (("c", 0), ("yh", 0), ("x", 0), ("x", 1))


def swap(array, axis, bit):
    return lax.ppermute(array, axis, [(i, i ^ (1 << bit)) for i in range(lax.axis_size(axis))])


def dot_nt(a, b):
    return lax.dot_general(a, b, (((1,), (1,)), ((), ())), preferred_element_type=F32)


def dot_nn(a, b):
    return lax.dot_general(a, b, (((1,), (0,)), ((), ())), preferred_element_type=F32)


def share(array, axis):
    n = lax.axis_size(axis)
    return lax.all_to_all(jnp.broadcast_to(array[None], (n,) + array.shape), axis, 0, 0, tiled=True)


def per_device(tokens, up_weight, down_weight, up_left, up_right, down_left, down_right):
    nz = lax.axis_size("z")
    count, db = tokens.shape
    rows, rank = up_right.shape[1:]
    kinds = up_weight.shape[2]
    up = up_weight[0].transpose(1, 0, 2).reshape(kinds * rows, db)
    down = down_weight[0].transpose(1, 0, 2).reshape(kinds * rows, db)

    code_part = dot_nn(tokens, up_left).astype(BF16)
    code = jnp.sum(share(code_part, FEAT).astype(F32), axis=0).astype(BF16)

    head = db - rank
    packed = jnp.concatenate(
        [
            up,
            down,
            jnp.concatenate([up_right[0], down_left[0][:, :head]], axis=1),
            jnp.concatenate([down_left[0][:, head:], jnp.zeros((rows, db - (rank - head)), BF16)], axis=1),
        ],
        axis=0,
    )
    packed, code = lax.optimization_barrier((packed, code))
    other = swap(packed, "yl", 0)
    gathered = lax.all_gather(jnp.concatenate([tokens, code], axis=1), "z", axis=0, tiled=True)
    own = gathered[:, :db]
    codes = gathered[:, db:]
    pieces = [own] + [swap(own, axis, bit) for axis, bit in LEVEL_AXES]

    n = kinds * rows
    up_o, down_o = other[:n], other[n : 2 * n]
    right_o = other[2 * n : 2 * n + rows, :rank]
    left_o = jnp.concatenate([other[2 * n : 2 * n + rows, rank:], other[2 * n + rows :, : rank - head]], axis=1)

    def pre_of(weight, right):
        total = dot_nt(codes, right)
        for k in range(kinds):
            total = total + dot_nt(pieces[k], weight[k * rows : (k + 1) * rows])
        return jax.nn.gelu(total, approximate=False).astype(BF16)

    h_a = pre_of(up, up_right[0])
    h_b = pre_of(up_o, right_o)

    def term(k):
        part = slice(k * rows, (k + 1) * rows)
        return dot_nn(h_a, down[part]) + dot_nn(h_b, down_o[part])

    sent = [swap(term(k + 1).astype(BF16), axis, bit) for k, (axis, bit) in enumerate(LEVEL_AXES)]
    back = (dot_nn(h_a, down_left[0]) + dot_nn(h_b, left_o)).astype(BF16)
    back = lax.all_to_all(back.reshape(nz, count, rank), "z", 0, 0, tiled=True)
    back = jnp.sum(back.astype(F32), axis=0).astype(BF16)
    back = jnp.sum(share(back, FEAT).astype(F32), axis=0).astype(BF16)

    total = term(0)
    for s in sent:
        total = total + s.astype(F32)
    total = lax.all_to_all(total.astype(BF16).reshape(nz, count, db), "z", 0, 0, tiled=True)
    total = jnp.sum(total.astype(F32), axis=0)
    return (total + dot_nn(back, down_right)).astype(BF16)


def solution(mesh):
    tok, feat = ("z", "yl"), FEAT
    inner = Mesh(mesh.devices.reshape(16, 2, 4, 2, 2), tok + feat)
    return jax.shard_map(
        per_device,
        mesh=inner,
        in_specs=(
            P(tok, feat),
            P(feat, tok, None, None),
            P(feat, tok, None, None),
            P(feat, None),
            P(feat, tok, None),
            P(feat, tok, None),
            P(None, feat),
        ),
        out_specs=P(tok, feat),
        check_vma=False,
    )
```

time: 509 us -> 197 us (0.39)
  blocking collectives: 255 us -> 37.7 us
  waiting for transfers between devices: 201 us -> 70.5 us
  starting transfers between devices: 25.9 us -> 60.4 us
  matrix products: 6.95 us -> 20.2 us
  between operations: 13.6 us -> 0.38 us
    reduce_scatter x2 -> x0, waiting for transfers between devices: 136 us -> none  [the longest x1 82.8 us: per_device(): lax.psum_scatter(total, 'tok', scatter_dimension=0, tiled=True)]
    psum x2 -> x0, blocking collectives: 119 us -> none  [the longest x1 62.8 us: per_device(): code = lax.psum(code_part, 'feat').astype(jnp.bfloat16)]
    all_gather x2 -> x1, blocking collectives: 136 us -> 37.7 us  [per_device(): lax.all_gather(jnp.concatenate([tokens, code], axis=1), 'z', axis=0, tile...]
    all_to_all x0 -> x4, starting transfers between devices: none -> 33.9 us  [the longest x2 15.1 us: share(): lax.all_to_all(jnp.broadcast_to(array[None], (n,) + array.shape), axis, 0...]
    all_to_all x0 -> x4, waiting for transfers between devices: none -> 27.6 us  [the longest x1 22.5 us: per_device(): lax.all_to_all(total.astype(BF16).reshape(nz, count, db), 'z', 0, 0, tile...]
    ppermute x8 -> x9, waiting for transfers between devices: 64.6 us -> 42.9 us  [swap(): lax.ppermute(array, axis, [(i, i ^ 1 << bit) for i in range(lax.axis_size...]
    dot_general x6 -> x26, matrix products: 6.95 us -> 20.2 us  [the longest x14 16.7 us: dot_nn(): lax.dot_general(a, b, (((1,), (0,)), ((), ())), preferred_element_type=F32)]
    ppermute x8 -> x9, starting transfers between devices: 25.9 us -> 26.5 us  [swap(): lax.ppermute(array, axis, [(i, i ^ 1 << bit) for i in range(lax.axis_size...]
  transfers between devices with their start and end apart: 10 -> 13, of which waited for: 4 -> 6; matrix products, arithmetic and copies ran while one was open for 2% -> 9% of each run, Pallas kernels for 0% -> 0%
where the time goes in v1:
time: 197 us; the launch traced here: 193 us
  waiting for transfers between devices  70.5 us (36%)
  starting transfers between devices  60.4 us (31%)
  blocking collectives  37.7 us (19%)
  matrix products  20.2 us (10%)
  local copies, waits for them, and re-layouts  2.4 us (1%)
    ppermute x9, waiting for transfers between devices, swap(): lax.ppermute(array, axis, [(i, i ^ 1 << bit) for i in range(lax.axis_size...  42.9 us
    all_gather x1, blocking collectives, per_device(): lax.all_gather(jnp.concatenate([tokens, code], axis=1), 'z', axis=0, tile...  37.7 us
    ppermute x9, starting transfers between devices, swap(): lax.ppermute(array, axis, [(i, i ^ 1 << bit) for i in range(lax.axis_size...  26.5 us
    all_to_all x1, waiting for transfers between devices, per_device(): lax.all_to_all(total.astype(BF16).reshape(nz, count, db), 'z', 0, 0, tile...  22.5 us
    dot_general x14, matrix products, dot_nn(): lax.dot_general(a, b, (((1,), (0,)), ((), ())), preferred_element_type=F32)  16.7 us
    all_to_all x2, starting transfers between devices, share(): lax.all_to_all(jnp.broadcast_to(array[None], (n,) + array.shape), axis, 0...  15.1 us
    all_to_all x1, starting transfers between devices, per_device(): lax.all_to_all(total.astype(BF16).reshape(nz, count, db), 'z', 0, 0, tile...  12 us
    all_to_all x1, starting transfers between devices, per_device(): back = lax.all_to_all(back.reshape(nz, count, rank), 'z', 0, 0, tiled=True)  6.77 us
  transfers between devices with their start and end apart: 13, of which 6 were waited for; matrix products, arithmetic and copies ran while one was open for 9% of the time, Pallas kernels for 0%

profile of v1, /device:TPU:6, one launch (start us, length us, event | category | flops | bytes accessed | tf_op | source)
XLA Modules:
  0.0 193.2 jit_solution(16057825606209016164)
XLA Ops:
  0.0 0.0 copy-start.5
  0.0 1.5 convolution_convert_fusion
  1.5 0.8 broadcast_in_dim.4
  2.3 9.2 %all-to-all-start = ((bf16[16,16,512]{2,1,0:T(8,128)(2,1)}), bf16[16,16,512]{2,1,0:T(8,128)(2,1)S(1)}, u32[]{:S(2)}, u32[]{:S(2)}) async-start(bf16[16,16,512]{2,1,0:T(8,128)(2,1)} %broadcast_in_dim.4), calls=%async_computation | async-start | bytes 524288 | tf_op jit(solution)/shard_map/all_to_all | solution.py:27
  11.5 0.8 fusion.81
  12.3 0.0 copy-done.1
  12.3 0.0 copy-done.5
  12.4 0.0 copy-start.6
  12.4 1.4 fusion.1
  13.7 5.1 %all-to-all-done = bf16[16,16,512]{2,1,0:T(8,128)(2,1)S(1)} async-done(((bf16[16,16,512]{2,1,0:T(8,128)(2,1)}), bf16[16,16,512]{2,1,0:T(8,128)(2,1)S(1)}, u32[]{:S(2)}, u32[]{:S(2)}) %all-to-all-start) | async-done | bytes 262176 | tf_op jit(solution)/shard_map/all_to_all | solution.py:27
  18.9 37.7 %all_gather.3 = bf16[256,1280]{1,0:T(8,128)(2,1)S(1)} all-gather(bf16[16,1280]{1,0:T(8,128)(2,1)S(1)} %pad_maximum_fusion), channel_id=1, replica_groups=mesh['z'=16,'yl'=2,'x'=4,'yh'=2,'c'=2] {'z'}, dimensions={0}, use_global_device_ids=true | all-gather | bytes 696320 | tf_op jit(solution)/shard_map/all_gather | solution.py:53
  56.6 2.7 %collective-permute-start.3 = (bf16[256,768]{1,0:T(8,128)(2,1)S(1)}, bf16[256,768]{1,0:T(8,128)(2,1)S(1)}, u32[]{:S(2)}, u32[]{:S(2)}) collective-permute-start(bf16[256,768]{1,0:T(8,128)(2,1)S(1)} %slice.163), channel_id=1, source_target_pairs={{0,8},{4,12},{8,0},{12,4},{1,9},{5,13},{9,1},{13,5},{2,10},{6,14},... | collective-permute-start | bytes 1179656 | tf_op jit(solution)/shard_map/ppermute | solution.py:14
  59.3 3.4 %collective-permute-start.2 = (bf16[256,768]{1,0:T(8,128)(2,1)S(1)}, bf16[256,768]{1,0:T(8,128)(2,1)S(1)}, u32[]{:S(2)}, u32[]{:S(2)}) collective-permute-start(bf16[256,768]{1,0:T(8,128)(2,1)S(1)} %slice.163), channel_id=1, source_target_pairs={{0,4},{4,0},{8,12},{12,8},{1,5},{5,1},{9,13},{13,9},{2,6},{6,2},{1... | collective-permute-start | bytes 1179656 | tf_op jit(solution)/shard_map/ppermute | solution.py:14
  62.7 2.7 %collective-permute-start.1 = (bf16[256,768]{1,0:T(8,128)(2,1)S(1)}, bf16[256,768]{1,0:T(8,128)(2,1)S(1)}, u32[]{:S(2)}, u32[]{:S(2)}) collective-permute-start(bf16[256,768]{1,0:T(8,128)(2,1)S(1)} %slice.163), channel_id=1, source_target_pairs={{0,2},{2,0},{1,3},{3,1},{4,6},{6,4},{5,7},{7,5},{8,10},{10,8},{9,1... | collective-permute-start | bytes 1179656 | tf_op jit(solution)/shard_map/ppermute | solution.py:14
  65.5 1.9 collective-permute-start
  67.4 2.6 %collective-permute-start.4 = (bf16[1152,768]{1,0:T(8,128)(2,1)}, bf16[1152,768]{1,0:T(8,128)(2,1)S(1)}, u32[]{:S(2)}, u32[]{:S(2)}) collective-permute-start(bf16[1152,768]{1,0:T(8,128)(2,1)} %fusion.1), channel_id=1, source_target_pairs={{0,16},{16,0},{1,17},{17,1},{2,18},{18,2},{3,19},{19,3},{4,20},{20... | collective-permute-start | bytes 5308424 | tf_op jit(solution)/shard_map/ppermute | solution.py:14
  70.0 0.2 fusion.21
  70.2 0.3 convolution_add_fusion.8
  70.5 0.0 collective-permute-done.3
  70.5 0.3 fusion.43
  70.8 0.9 collective-permute-done.2
  71.6 0.3 fusion.44
  71.9 0.0 copy-start.4
  71.9 2.0 %collective-permute-done.1 = bf16[256,768]{1,0:T(8,128)(2,1)S(1)} collective-permute-done((bf16[256,768]{1,0:T(8,128)(2,1)S(1)}, bf16[256,768]{1,0:T(8,128)(2,1)S(1)}, u32[]{:S(2)}, u32[]{:S(2)}) %collective-permute-start.1) | collective-permute-done | bytes 393248 | tf_op jit(solution)/shard_map/ppermute | solution.py:14
  73.9 0.3 fusion.45
  74.2 0.0 collective-permute-done
  74.2 0.5 fusion.48
  74.7 0.2 fusion.75
  74.9 1.2 fusion.30
  76.1 0.3 fusion.28
  76.4 0.3 fusion.26
  76.7 1.2 fusion.24
  77.9 32.6 %collective-permute-done.4 = bf16[1152,768]{1,0:T(8,128)(2,1)S(1)} collective-permute-done((bf16[1152,768]{1,0:T(8,128)(2,1)}, bf16[1152,768]{1,0:T(8,128)(2,1)S(1)}, u32[]{:S(2)}, u32[]{:S(2)}) %collective-permute-start.4) | collective-permute-done | bytes 1769504 | tf_op jit(solution)/shard_map/ppermute | solution.py:14
  110.5 0.3 fusion.32
  110.8 0.3 fusion.34
  111.1 0.3 fusion.36
  111.3 0.3 fusion.38
  111.6 0.3 fusion.40
  111.9 0.4 fusion.51
  112.3 1.0 fusion.11
  113.3 6.8 %all-to-all-start.2 = ((bf16[16,16,512]{2,1,0:T(8,128)(2,1)}), bf16[16,16,512]{2,1,0:T(8,128)(2,1)S(1)}, u32[]{:S(2)}, u32[]{:S(2)}) async-start(bf16[16,16,512]{2,1,0:T(8,128)(2,1)} %bitcast.21), calls=%async_computation.2 | async-start | bytes 524288 | tf_op jit(solution)/shard_map/all_to_all | solution.py:78
  120.1 2.2 %fusion.7 = bf16[256,768]{1,0:T(8,128)(2,1)} fusion(f32[256,768]{1,0:T(8,128)} %fusion.30, bf16[256,96]{0,1:T(8,128)(2,1)S(1)} %fusion.51, bf16[1152,768]{1,0:T(8,128)(2,1)} %copy-done.3), kind=kOutput, calls=%fused_computation.13 | convolution fusion | flops 38141952 | bytes 1376256 | tf_op jit(solution)/shard_map/dot_general | solution.py:22
  122.3 1.9 collective-permute-start.5
  124.2 1.9 %fusion.8 = bf16[256,768]{1,0:T(8,128)(2,1)} fusion(f32[256,768]{1,0:T(8,128)S(1)} %fusion.28, bf16[256,96]{0,1:T(8,128)(2,1)S(1)} %fusion.51, bf16[1152,768]{1,0:T(8,128)(2,1)} %copy-done.3), kind=kOutput, calls=%fused_computation.14 | convolution fusion | flops 38141952 | bytes 1376256 | tf_op jit(solution)/shard_map/dot_general | solution.py:22
  126.2 5.2 %collective-permute-start.6 = (bf16[256,768]{1,0:T(8,128)(2,1)}, bf16[256,768]{1,0:T(8,128)(2,1)}, u32[]{:S(2)}, u32[]{:S(2)}) collective-permute-start(bf16[256,768]{1,0:T(8,128)(2,1)} %fusion.8), channel_id=1, source_target_pairs={{0,2},{2,0},{1,3},{3,1},{4,6},{6,4},{5,7},{7,5},{8,10},{10,8},{9,1... | collective-permute-start | bytes 1179656 | tf_op jit(solution)/shard_map/ppermute | solution.py:14
  131.4 1.2 fusion.9
  132.6 2.1 %collective-permute-start.7 = (bf16[256,768]{1,0:T(8,128)(2,1)S(1)}, bf16[256,768]{1,0:T(8,128)(2,1)S(1)}, u32[]{:S(2)}, u32[]{:S(2)}) collective-permute-start(bf16[256,768]{1,0:T(8,128)(2,1)S(1)} %fusion.9), channel_id=1, source_target_pairs={{0,4},{4,0},{8,12},{12,8},{1,5},{5,1},{9,13},{13,9},{2,6},{6,2},{1... | collective-permute-start | bytes 1179656 | tf_op jit(solution)/shard_map/ppermute | solution.py:14
  134.8 1.2 fusion.10
  136.0 3.9 %collective-permute-start.8 = (bf16[256,768]{1,0:T(8,128)(2,1)S(1)}, bf16[256,768]{1,0:T(8,128)(2,1)}, u32[]{:S(2)}, u32[]{:S(2)}) collective-permute-start(bf16[256,768]{1,0:T(8,128)(2,1)S(1)} %fusion.10), channel_id=1, source_target_pairs={{0,8},{4,12},{8,0},{12,4},{1,9},{5,13},{9,1},{13,5},{2,10},{6,14},... | collective-permute-start | bytes 1179656 | tf_op jit(solution)/shard_map/ppermute | solution.py:14
  139.8 1.2 fusion.42
  141.0 0.0 all-to-all-done.2
  141.1 0.7 broadcast_in_dim.5
  141.8 5.9 %all-to-all-start.3 = ((bf16[16,16,512]{2,1,0:T(8,128)(2,1)}), bf16[16,16,512]{2,1,0:T(8,128)(2,1)S(1)}, u32[]{:S(2)}, u32[]{:S(2)}) async-start(bf16[16,16,512]{2,1,0:T(8,128)(2,1)} %broadcast_in_dim.5), calls=%async_computation.3 | async-start | bytes 524288 | tf_op jit(solution)/shard_map/all_to_all | solution.py:27
  147.7 0.0 collective-permute-done.5
  147.7 0.0 collective-permute-done.6
  147.7 0.0 collective-permute-done.7
  147.8 7.5 %collective-permute-done.8 = bf16[256,768]{1,0:T(8,128)(2,1)} collective-permute-done((bf16[256,768]{1,0:T(8,128)(2,1)S(1)}, bf16[256,768]{1,0:T(8,128)(2,1)}, u32[]{:S(2)}, u32[]{:S(2)}) %collective-permute-start.8) | collective-permute-done | bytes 393248 | tf_op jit(solution)/shard_map/ppermute | solution.py:14
  155.2 2.5 %fusion.6 = bf16[256,768]{1,0:T(8,128)(2,1)} fusion(f32[256,768]{1,0:T(8,128)S(1)} %fusion.42, bf16[256,96]{0,1:T(8,128)(2,1)S(1)} %fusion.51, bf16[256,768]{1,0:T(8,128)(2,1)} %collective-permute-done.8, bf16[256,768]{1,0:T(8,128)(2,1)S(1)} %collective-permute-done.7, bf16[256,768]{1,0:T(8,128)(2,1)} %collective-permute-done.6, ...), kind=kOutput, calls=%fused_computation.12 | convolution fusion | flops 39714816 | bytes 2949120 | tf_op jit(solution)/shard_map/dot_general | solution.py:22
  157.7 0.0 all-to-all-done.3
  157.7 12.0 %all-to-all-start.1 = ((bf16[16,16,768]{2,1,0:T(8,128)(2,1)}), bf16[16,16,768]{2,1,0:T(8,128)(2,1)S(1)}, u32[]{:S(2)}, u32[]{:S(2)}) async-start(bf16[16,16,768]{2,1,0:T(8,128)(2,1)} %bitcast.20), calls=%async_computation.1 | async-start | bytes 786432 | tf_op jit(solution)/shard_map/all_to_all | solution.py:85
  169.8 22.5 %all-to-all-done.1 = bf16[16,16,768]{2,1,0:T(8,128)(2,1)S(1)} async-done(((bf16[16,16,768]{2,1,0:T(8,128)(2,1)}), bf16[16,16,768]{2,1,0:T(8,128)(2,1)S(1)}, u32[]{:S(2)}, u32[]{:S(2)}) %all-to-all-start.1) | async-done | bytes 393248 | tf_op jit(solution)/shard_map/all_to_all | solution.py:85
  192.3 0.1 convert_reduce_fusion
  192.3 0.0 copy-done
  192.3 0.8 fusion.19
  (14 shorter events, 0.2 us)
Async XLA Ops:
  0.0 192.3 %copy-start = (bf16[512,768]{1,0:T(8,128)(2,1)S(1)}, bf16[512,768]{1,0:T(8,128)(2,1)}, u32[]{:S(2)}) copy-start(bf16[512,768]{1,0:T(8,128)(2,1)} %param.13) | copy-start | bytes 2359300
  0.0 12.3 %copy-start.2 = (bf16[1,96,5,768]{3,1,2,0:T(8,128)(2,1)S(1)}, bf16[1,96,5,768]{3,1,2,0:T(8,128)(2,1)}, u32[]{:S(2)}) copy-start(bf16[1,96,5,768]{3,1,2,0:T(8,128)(2,1)} %param.8) | copy-start | bytes 2211844
  0.0 12.3 %copy-start.1 = (bf16[1,96,5,768]{3,1,2,0:T(8,128)(2,1)S(1)}, bf16[1,96,5,768]{3,1,2,0:T(8,128)(2,1)}, u32[]{:S(2)}) copy-start(bf16[1,96,5,768]{3,1,2,0:T(8,128)(2,1)} %param.9) | copy-start | bytes 2211844
  0.0 12.3 %copy-start.5 = (bf16[1,96,512]{2,1,0:T(8,128)(2,1)S(1)}, bf16[1,96,512]{2,1,0:T(8,128)(2,1)}, u32[]{:S(2)}) copy-start(bf16[1,96,512]{2,1,0:T(8,128)(2,1)} %param.11) | copy-start | bytes 294916
  2.3 16.5 %all-to-all-start = ((bf16[16,16,512]{2,1,0:T(8,128)(2,1)}), bf16[16,16,512]{2,1,0:T(8,128)(2,1)S(1)}, u32[]{:S(2)}, u32[]{:S(2)}) async-start(bf16[16,16,512]{2,1,0:T(8,128)(2,1)} %broadcast_in_dim.4), calls=%async_computation | async-start | bytes 524288 | tf_op jit(solution)/shard_map/all_to_all | solution.py:27
  12.4 6.5 %copy-start.6 = (bf16[16,768]{1,0:T(8,128)(2,1)S(1)}, bf16[16,768]{1,0:T(8,128)(2,1)}, u32[]{:S(2)}) copy-start(bf16[16,768]{1,0:T(8,128)(2,1)} %param.7) | copy-start | bytes 73732
  56.6 13.9 %collective-permute-start.3 = (bf16[256,768]{1,0:T(8,128)(2,1)S(1)}, bf16[256,768]{1,0:T(8,128)(2,1)S(1)}, u32[]{:S(2)}, u32[]{:S(2)}) collective-permute-start(bf16[256,768]{1,0:T(8,128)(2,1)S(1)} %slice.163), channel_id=1, source_target_pairs={{0,8},{4,12},{8,0},{12,4},{1,9},{5,13},{9,1},{13,5},{2,10},{6,14},... | collective-permute-start | bytes 1179656 | tf_op jit(solution)/shard_map/ppermute | solution.py:14
  59.3 12.3 %collective-permute-start.2 = (bf16[256,768]{1,0:T(8,128)(2,1)S(1)}, bf16[256,768]{1,0:T(8,128)(2,1)S(1)}, u32[]{:S(2)}, u32[]{:S(2)}) collective-permute-start(bf16[256,768]{1,0:T(8,128)(2,1)S(1)} %slice.163), channel_id=1, source_target_pairs={{0,4},{4,0},{8,12},{12,8},{1,5},{5,1},{9,13},{13,9},{2,6},{6,2},{1... | collective-permute-start | bytes 1179656 | tf_op jit(solution)/shard_map/ppermute | solution.py:14
  62.7 11.2 %collective-permute-start.1 = (bf16[256,768]{1,0:T(8,128)(2,1)S(1)}, bf16[256,768]{1,0:T(8,128)(2,1)S(1)}, u32[]{:S(2)}, u32[]{:S(2)}) collective-permute-start(bf16[256,768]{1,0:T(8,128)(2,1)S(1)} %slice.163), channel_id=1, source_target_pairs={{0,2},{2,0},{1,3},{3,1},{4,6},{6,4},{5,7},{7,5},{8,10},{10,8},{9,1... | collective-permute-start | bytes 1179656 | tf_op jit(solution)/shard_map/ppermute | solution.py:14
  65.5 8.7 %collective-permute-start = (bf16[256,768]{1,0:T(8,128)(2,1)S(1)}, bf16[256,768]{1,0:T(8,128)(2,1)S(1)}, u32[]{:S(2)}, u32[]{:S(2)}) collective-permute-start(bf16[256,768]{1,0:T(8,128)(2,1)S(1)} %slice.163), channel_id=1, source_target_pairs={{0,1},{1,0},{2,3},{3,2},{4,5},{5,4},{6,7},{7,6},{8,9},{9,8},{10,11... | collective-permute-start | bytes 1179656 | tf_op jit(solution)/shard_map/ppermute | solution.py:14
  67.4 43.1 %collective-permute-start.4 = (bf16[1152,768]{1,0:T(8,128)(2,1)}, bf16[1152,768]{1,0:T(8,128)(2,1)S(1)}, u32[]{:S(2)}, u32[]{:S(2)}) collective-permute-start(bf16[1152,768]{1,0:T(8,128)(2,1)} %fusion.1), channel_id=1, source_target_pairs={{0,16},{16,0},{1,17},{17,1},{2,18},{18,2},{3,19},{19,3},{4,20},{20... | collective-permute-start | bytes 5308424 | tf_op jit(solution)/shard_map/ppermute | solution.py:14
  71.9 2.8 %copy-start.4 = (bf16[1,96,512]{2,1,0:T(8,128)(2,1)S(1)}, bf16[1,96,512]{2,1,0:T(8,128)(2,1)}, u32[]{:S(2)}) copy-start(bf16[1,96,512]{2,1,0:T(8,128)(2,1)} %param.12) | copy-start | bytes 294916
  110.5 2.8 %copy-start.3 = (bf16[1152,768]{1,0:T(8,128)(2,1)}, bf16[1152,768]{1,0:T(8,128)(2,1)S(1)}, u32[]{:S(2)}) copy-start(bf16[1152,768]{1,0:T(8,128)(2,1)S(1)} %collective-permute-done.4) | copy-start | bytes 5308420
  113.3 27.8 %all-to-all-start.2 = ((bf16[16,16,512]{2,1,0:T(8,128)(2,1)}), bf16[16,16,512]{2,1,0:T(8,128)(2,1)S(1)}, u32[]{:S(2)}, u32[]{:S(2)}) async-start(bf16[16,16,512]{2,1,0:T(8,128)(2,1)} %bitcast.21), calls=%async_computation.2 | async-start | bytes 524288 | tf_op jit(solution)/shard_map/all_to_all | solution.py:78
  122.3 25.4 %collective-permute-start.5 = (bf16[256,768]{1,0:T(8,128)(2,1)}, bf16[256,768]{1,0:T(8,128)(2,1)}, u32[]{:S(2)}, u32[]{:S(2)}) collective-permute-start(bf16[256,768]{1,0:T(8,128)(2,1)} %fusion.7), channel_id=1, source_target_pairs={{0,1},{1,0},{2,3},{3,2},{4,5},{5,4},{6,7},{7,6},{8,9},{9,8},{10,11... | collective-permute-start | bytes 1179656 | tf_op jit(solution)/shard_map/ppermute | solution.py:14
  126.2 21.6 %collective-permute-start.6 = (bf16[256,768]{1,0:T(8,128)(2,1)}, bf16[256,768]{1,0:T(8,128)(2,1)}, u32[]{:S(2)}, u32[]{:S(2)}) collective-permute-start(bf16[256,768]{1,0:T(8,128)(2,1)} %fusion.8), channel_id=1, source_target_pairs={{0,2},{2,0},{1,3},{3,1},{4,6},{6,4},{5,7},{7,5},{8,10},{10,8},{9,1... | collective-permute-start | bytes 1179656 | tf_op jit(solution)/shard_map/ppermute | solution.py:14
  132.6 15.1 %collective-permute-start.7 = (bf16[256,768]{1,0:T(8,128)(2,1)S(1)}, bf16[256,768]{1,0:T(8,128)(2,1)S(1)}, u32[]{:S(2)}, u32[]{:S(2)}) collective-permute-start(bf16[256,768]{1,0:T(8,128)(2,1)S(1)} %fusion.9), channel_id=1, source_target_pairs={{0,4},{4,0},{8,12},{12,8},{1,5},{5,1},{9,13},{13,9},{2,6},{6,2},{1... | collective-permute-start | bytes 1179656 | tf_op jit(solution)/shard_map/ppermute | solution.py:14
  136.0 19.3 %collective-permute-start.8 = (bf16[256,768]{1,0:T(8,128)(2,1)S(1)}, bf16[256,768]{1,0:T(8,128)(2,1)}, u32[]{:S(2)}, u32[]{:S(2)}) collective-permute-start(bf16[256,768]{1,0:T(8,128)(2,1)S(1)} %fusion.10), channel_id=1, source_target_pairs={{0,8},{4,12},{8,0},{12,4},{1,9},{5,13},{9,1},{13,5},{2,10},{6,14},... | collective-permute-start | bytes 1179656 | tf_op jit(solution)/shard_map/ppermute | solution.py:14
  141.8 15.9 %all-to-all-start.3 = ((bf16[16,16,512]{2,1,0:T(8,128)(2,1)}), bf16[16,16,512]{2,1,0:T(8,128)(2,1)S(1)}, u32[]{:S(2)}, u32[]{:S(2)}) async-start(bf16[16,16,512]{2,1,0:T(8,128)(2,1)} %broadcast_in_dim.5), calls=%async_computation.3 | async-start | bytes 524288 | tf_op jit(solution)/shard_map/all_to_all | solution.py:27
  157.7 34.5 %all-to-all-start.1 = ((bf16[16,16,768]{2,1,0:T(8,128)(2,1)}), bf16[16,16,768]{2,1,0:T(8,128)(2,1)S(1)}, u32[]{:S(2)}, u32[]{:S(2)}) async-start(bf16[16,16,768]{2,1,0:T(8,128)(2,1)} %bitcast.20), calls=%async_computation.1 | async-start | bytes 786432 | tf_op jit(solution)/shard_map/all_to_all | solution.py:85

commit v2 on v1

v2 whole, which is shorter than its diff:
```python
import functools

import jax
import jax.numpy as jnp
from jax import lax
from jax.experimental import pallas as pl
from jax.experimental.pallas import tpu as pltpu
from jax.sharding import Mesh, PartitionSpec as P


F32 = jnp.float32
BF16 = jnp.bfloat16
FEAT = ("x", "yh", "c")
LEVEL_AXES = (("c", 0), ("yh", 0), ("x", 0), ("x", 1))


def swap(array, axis, bit):
    return lax.ppermute(array, axis, [(i, i ^ (1 << bit)) for i in range(lax.axis_size(axis))])


def dot_nt(a, b):
    return lax.dot_general(a, b, (((1,), (1,)), ((), ())), preferred_element_type=F32)


def dot_nn(a, b):
    return lax.dot_general(a, b, (((1,), (0,)), ((), ())), preferred_element_type=F32)


def share(array, axis):
    n = lax.axis_size(axis)
    return lax.all_to_all(jnp.broadcast_to(array[None], (n,) + array.shape), axis, 0, 0, tiled=True)


def total_of(stack):
    return lax.reduce_precision(jnp.sum(stack.astype(F32), axis=0), 8, 7).astype(BF16)


def sum_over_feat(part, n):
    part = lax.all_to_all(part.reshape((n, part.shape[0] // n) + part.shape[1:]), FEAT, 0, 0, tiled=True)
    group = total_of(part)
    whole = share(group, FEAT)
    return whole.reshape((-1,) + group.shape[1:])


def ffn_body(kinds, rows, db, rank, x0, x1, x2, x3, x4, code, up, right, down, left, other, t0, t1, t2, t3, t4, back):
    n = kinds * rows
    head = db - rank
    xs = (x0, x1, x2, x3, x4)

    def pair(ref, base, k):
        lo = k * rows
        return jnp.concatenate([ref[lo : lo + rows, :], other[base + lo : base + lo + rows, :]], axis=0)

    pre = dot_nt(code[...], jnp.concatenate([right[...], other[2 * n : 2 * n + rows, :rank]], axis=0))
    for k in range(kinds):
        pre = pre + dot_nt(xs[k][...], pair(up, 0, k))
    hidden = (0.5 * pre * (1.0 + lax.erf(pre * (0.5**0.5)))).astype(BF16)
    outs = (t0, t1, t2, t3, t4)
    for k in (2, 3, 4, 1, 0):
        outs[k][...] = dot_nn(hidden, pair(down, n, k)).astype(outs[k].dtype)
    low = jnp.concatenate([left[:, :head], other[2 * n : 2 * n + rows, rank:]], axis=0)
    high = jnp.concatenate([left[:, head:], other[2 * n + rows :, : rank - head]], axis=0)
    back[:, :head] = dot_nn(hidden, low).astype(BF16)
    back[:, head:] = dot_nn(hidden, high).astype(BF16)


def ffn_call(pieces, code, up, right, down, left, other):
    count = code.shape[0]
    rows, rank = right.shape
    db = up.shape[1]
    kinds = up.shape[0] // rows
    shapes = [jax.ShapeDtypeStruct((count, db), F32)]
    shapes += [jax.ShapeDtypeStruct((count, db), BF16)] * (kinds - 1)
    shapes += [jax.ShapeDtypeStruct((count, rank), BF16)]
    return pl.pallas_call(
        functools.partial(ffn_body, kinds, rows, db, rank),
        out_shape=shapes,
        compiler_params=pltpu.CompilerParams(vmem_limit_bytes=16 * 2**20),
        name="ffn",
    )(*pieces, code, up, right, down, left, other)


def per_device(tokens, up_weight, down_weight, up_left, up_right, down_left, down_right):
    nz, nf = lax.axis_size("z"), lax.axis_size(FEAT)
    count, db = tokens.shape
    rows, rank = up_right.shape[1:]
    kinds = up_weight.shape[2]
    up = up_weight[0].transpose(1, 0, 2).reshape(kinds * rows, db)
    down = down_weight[0].transpose(1, 0, 2).reshape(kinds * rows, db)

    head = db - rank
    packed = jnp.concatenate(
        [
            up,
            down,
            jnp.concatenate([up_right[0], down_left[0][:, :head]], axis=1),
            jnp.concatenate([down_left[0][:, head:], jnp.zeros((rows, db - (rank - head)), BF16)], axis=1),
        ],
        axis=0,
    )
    other = swap(packed, "yl", 0)
    own = lax.all_gather(tokens, "z", axis=0, tiled=True)
    code = sum_over_feat(dot_nn(own, up_left).astype(BF16), nf)
    pieces = [own]
    for axis, bit in LEVEL_AXES:
        pieces.append(swap(own, axis, bit))

    own_total, *terms, back = ffn_call(pieces, code, up, up_right[0], down, down_left[0], other)
    back = sum_over_feat(back, nf)
    sent = []
    for part, (axis, bit) in zip(terms, LEVEL_AXES):
        sent.append(swap(part, axis, bit))
    total = own_total + dot_nn(back, down_right)
    for s in sent:
        total = total + s.astype(F32)
    total = total.astype(BF16)
    total = lax.all_to_all(total.reshape(nz, count, db), "z", 0, 0, tiled=True)
    return total_of(total)


def solution(mesh):
    tok, feat = ("z", "yl"), FEAT
    inner = Mesh(mesh.devices.reshape(16, 2, 4, 2, 2), tok + feat)
    return jax.shard_map(
        per_device,
        mesh=inner,
        in_specs=(
            P(tok, feat),
            P(feat, tok, None, None),
            P(feat, tok, None, None),
            P(feat, None),
            P(feat, tok, None),
            P(feat, tok, None),
            P(None, feat),
        ),
        out_specs=P(tok, feat),
        check_vma=False,
    )
```

time: 197 us -> 167 us (0.85)
  waiting for transfers between devices: 70.5 us -> 23.3 us
  blocking collectives: 37.7 us -> 79.7 us
  matrix products: 20.2 us -> 1.45 us
  starting transfers between devices: 60.4 us -> 46.9 us
  Pallas kernels: 0 us -> 4.38 us
  local copies, waits for them, and re-layouts: 2.4 us -> 4.76 us
  other arithmetic: 1.56 us -> 3.86 us
    all_to_all x0 -> x2, blocking collectives: none -> 42.1 us  [the longest x1 29.3 us: per_device(): total = lax.all_to_all(total.reshape(nz, count, db), 'z', 0, 0, tiled=True)]
    ppermute x9, waiting for transfers between devices: 42.9 us -> 18.8 us  [swap(): lax.ppermute(array, axis, [(i, i ^ 1 << bit) for i in range(lax.axis_size...]
    all_to_all x2 -> x1, waiting for transfers between devices: 22.5 us -> 0.01 us  [sum_over_feat(): lax.all_to_all(part.reshape((n, part.shape[0] // n) + part.shape[1:]), FE...]
    dot_general x14 -> x2, matrix products: 16.7 us -> 1.45 us  [dot_nn(): lax.dot_general(a, b, (((1,), (0,)), ((), ())), preferred_element_type=F32)]
    all_to_all x2 -> x1, starting transfers between devices: 18.8 us -> 7.13 us  [sum_over_feat(): lax.all_to_all(part.reshape((n, part.shape[0] // n) + part.shape[1:]), FE...]
    pallas_call x0 -> x1, Pallas kernels: none -> 4.38 us  [ffn_call(): pl.pallas_call(functools.partial(ffn_body, kinds, rows, db, rank), out_sh...]
    all_to_all x2, starting transfers between devices: 15.1 us -> 11.4 us  [share(): lax.all_to_all(jnp.broadcast_to(array[None], (n,) + array.shape), axis, 0...]
    dot_general x12 -> x0, matrix products: 3.57 us -> none  [dot_nt(): lax.dot_general(a, b, (((1,), (1,)), ((), ())), preferred_element_type=F32)]
  transfers between devices with their start and end apart: 13 -> 12, of which waited for: 6 -> 5; matrix products, arithmetic and copies ran while one was open for 9% -> 1% of each run, Pallas kernels for 0% -> 0%
where the time goes in v2:
time: 167 us; the launch traced here: 165 us
  blocking collectives  79.7 us (48%)
  starting transfers between devices  46.9 us (28%)
  waiting for transfers between devices  23.3 us (14%)
  local copies, waits for them, and re-layouts  4.76 us (3%)
  Pallas kernels  4.38 us (3%)
  other arithmetic  3.86 us (2%)
    all_gather x1, blocking collectives, per_device(): own = lax.all_gather(tokens, 'z', axis=0, tiled=True)  37.6 us
    all_to_all x1, blocking collectives, per_device(): total = lax.all_to_all(total.reshape(nz, count, db), 'z', 0, 0, tiled=True)  29.3 us
    ppermute x9, starting transfers between devices, swap(): lax.ppermute(array, axis, [(i, i ^ 1 << bit) for i in range(lax.axis_size...  28.4 us
    ppermute x9, waiting for transfers between devices, swap(): lax.ppermute(array, axis, [(i, i ^ 1 << bit) for i in range(lax.axis_size...  18.8 us
    all_to_all x1, blocking collectives, sum_over_feat(): lax.all_to_all(part.reshape((n, part.shape[0] // n) + part.shape[1:]), FE...  12.7 us
    all_to_all x2, starting transfers between devices, share(): lax.all_to_all(jnp.broadcast_to(array[None], (n,) + array.shape), axis, 0...  11.4 us
    all_to_all x1, starting transfers between devices, sum_over_feat(): lax.all_to_all(part.reshape((n, part.shape[0] // n) + part.shape[1:]), FE...  7.13 us
    all_to_all x2, waiting for transfers between devices, share(): lax.all_to_all(jnp.broadcast_to(array[None], (n,) + array.shape), axis, 0...  4.53 us
  transfers between devices with their start and end apart: 12, of which 5 were waited for; matrix products, arithmetic and copies ran while one was open for 1% of the time, Pallas kernels for 0%

profile of v2, /device:TPU:6, one launch (start us, length us, event | category | flops | bytes accessed | tf_op | source)
XLA Modules:
  0.0 164.6 jit_solution(14803292456925347568)
XLA Ops:
  0.0 0.0 copy-start
  0.0 0.9 fusion.2
  0.9 0.0 copy-start.12
  0.9 0.0 copy-start.11
  0.9 2.8 %fusion.1 = bf16[1152,768]{1,0:T(8,128)(2,1)} fusion(bf16[96,256]{1,0:T(8,128)(2,1)S(1)} %get-tuple-element.18, bf16[96,256]{1,0:T(8,128)(2,1)S(1)} %get-tuple-element.17, bf16[96,512]{1,0:T(8,128)(2,1)} %bitcast.28, bf16[480,768]{1,0:T(8,128)(2,1)} %bitcast.23, bf16[480,768]{1,0:T(8,128)(2,1)} %bitcast.21), kind=kLoop, calls=%fused_computation.2 | loop fusion | flops 10616832 | bytes 3440640 | tf_op jit(solution)/shard_map/concatenate | solution.py:92
  3.7 0.0 copy-start.1
  3.7 0.0 copy-start.2
  3.7 0.0 copy-start.5
  3.7 0.0 copy-start.6
  3.8 3.6 %collective-permute-start.4 = (bf16[1152,768]{1,0:T(8,128)(2,1)}, bf16[1152,768]{1,0:T(8,128)(2,1)}, u32[]{:S(2)}, u32[]{:S(2)}) collective-permute-start(bf16[1152,768]{1,0:T(8,128)(2,1)} %fusion.1), channel_id=1, source_target_pairs={{0,16},{16,0},{1,17},{17,1},{2,18},{18,2},{3,19},{19,3},{4,20},{20... | collective-permute-start | bytes 5308424 | tf_op jit(solution)/shard_map/ppermute | solution.py:18
  7.4 0.0 copy-done.12
  7.4 37.6 %all_gather.3.x0 = bf16[256,768]{1,0:T(8,128)(2,1)S(1)} all-gather(bf16[16,768]{1,0:T(8,128)(2,1)S(1)} %copy-done.12), channel_id=1, replica_groups=mesh['z'=16,'yl'=2,'x'=4,'yh'=2,'c'=2] {'z'}, dimensions={0}, use_global_device_ids=true | all-gather | bytes 417792 | tf_op jit(solution)/shard_map/all_gather | solution.py:102
  45.0 0.0 copy-done.11
  45.0 1.1 convolution_convert_fusion
  46.1 7.1 %all-to-all-start = ((bf16[16,16,512]{2,1,0:T(8,128)(2,1)}), bf16[16,16,512]{2,1,0:T(8,128)(2,1)S(1)}, u32[]{:S(2)}, u32[]{:S(2)}) async-start(bf16[16,16,512]{2,1,0:T(8,128)(2,1)} %bitcast), calls=%async_computation | async-start | bytes 524288 | tf_op jit(solution)/shard_map/all_to_all | solution.py:39
  53.2 3.4 %collective-permute-start.3 = (bf16[256,768]{1,0:T(8,128)(2,1)S(1)}, bf16[256,768]{1,0:T(8,128)(2,1)S(1)}, u32[]{:S(2)}, u32[]{:S(2)}) collective-permute-start(bf16[256,768]{1,0:T(8,128)(2,1)S(1)} %all_gather.3.x0), channel_id=1, source_target_pairs={{0,8},{4,12},{8,0},{12,4},{1,9},{5,13},{9,1},{13,5},{2,10},{6,14},... | collective-permute-start | bytes 1179656 | tf_op jit(solution)/shard_map/ppermute | solution.py:18
  56.6 1.9 %collective-permute-start.2 = (bf16[256,768]{1,0:T(8,128)(2,1)S(1)}, bf16[256,768]{1,0:T(8,128)(2,1)}, u32[]{:S(2)}, u32[]{:S(2)}) collective-permute-start(bf16[256,768]{1,0:T(8,128)(2,1)S(1)} %all_gather.3.x0), channel_id=1, source_target_pairs={{0,4},{4,0},{8,12},{12,8},{1,5},{5,1},{9,13},{13,9},{2,6},{6,2},{1... | collective-permute-start | bytes 1179656 | tf_op jit(solution)/shard_map/ppermute | solution.py:18
  58.5 4.9 %collective-permute-start.1 = (bf16[256,768]{1,0:T(8,128)(2,1)S(1)}, bf16[256,768]{1,0:T(8,128)(2,1)}, u32[]{:S(2)}, u32[]{:S(2)}) collective-permute-start(bf16[256,768]{1,0:T(8,128)(2,1)S(1)} %all_gather.3.x0), channel_id=1, source_target_pairs={{0,2},{2,0},{1,3},{3,1},{4,6},{6,4},{5,7},{7,5},{8,10},{10,8},{9,1... | collective-permute-start | bytes 1179656 | tf_op jit(solution)/shard_map/ppermute | solution.py:18
  63.4 1.9 %collective-permute-start = (bf16[256,768]{1,0:T(8,128)(2,1)S(1)}, bf16[256,768]{1,0:T(8,128)(2,1)}, u32[]{:S(2)}, u32[]{:S(2)}) collective-permute-start(bf16[256,768]{1,0:T(8,128)(2,1)S(1)} %all_gather.3.x0), channel_id=1, source_target_pairs={{0,1},{1,0},{2,3},{3,2},{4,5},{5,4},{6,7},{7,6},{8,9},{9,8},{10,11... | collective-permute-start | bytes 1179656 | tf_op jit(solution)/shard_map/ppermute | solution.py:18
  65.3 0.0 all-to-all-done
  65.4 0.7 broadcast_in_dim.4
  66.2 6.1 %all-to-all-start.1 = ((bf16[16,16,512]{2,1,0:T(8,128)(2,1)}), bf16[16,16,512]{2,1,0:T(8,128)(2,1)S(1)}, u32[]{:S(2)}, u32[]{:S(2)}) async-start(bf16[16,16,512]{2,1,0:T(8,128)(2,1)} %broadcast_in_dim.4), calls=%async_computation.1 | async-start | bytes 524288 | tf_op jit(solution)/shard_map/all_to_all | solution.py:31
  72.2 0.0 collective-permute-done.3.x4
  72.2 3.4 %collective-permute-done.2.x3 = bf16[256,768]{1,0:T(8,128)(2,1)} collective-permute-done((bf16[256,768]{1,0:T(8,128)(2,1)S(1)}, bf16[256,768]{1,0:T(8,128)(2,1)}, u32[]{:S(2)}, u32[]{:S(2)}) %collective-permute-start.2) | collective-permute-done | bytes 393248 | tf_op jit(solution)/shard_map/ppermute | solution.py:18
  75.6 0.0 collective-permute-done.1.x2
  75.6 0.0 collective-permute-done.x1
  75.6 4.5 %all-to-all-done.1 = bf16[16,16,512]{2,1,0:T(8,128)(2,1)S(1)} async-done(((bf16[16,16,512]{2,1,0:T(8,128)(2,1)}), bf16[16,16,512]{2,1,0:T(8,128)(2,1)S(1)}, u32[]{:S(2)}, u32[]{:S(2)}) %all-to-all-start.1) | async-done | bytes 262176 | tf_op jit(solution)/shard_map/all_to_all | solution.py:31
  80.1 0.0 collective-permute-done.4.other
  80.1 0.0 copy-done.1
  80.1 0.0 copy-done.2
  80.2 0.0 copy-done.5
  80.2 0.0 copy-done.6
  80.2 4.4 %ffn.1 = (f32[256,768]{1,0:T(8,128)S(1)}, bf16[256,768]{1,0:T(8,128)(2,1)S(1)}, bf16[256,768]{1,0:T(8,128)(2,1)S(1)}, bf16[256,768]{1,0:T(8,128)(2,1)S(1)}, bf16...) custom-call(bf16[256,768]{1,0:T(8,128)(2,1)S(1)} %all_gather.3.x0, bf16[256,768]{1,0:T(8,128)(2,1)} %collective-permute-done.x1, ...), custom_call_target="tpu_custom_call" | custom-call | tf_op jit(solution)/shard_map/ffn/pallas_call | solution.py:75
  84.6 0.0 copy-start.3
  84.6 0.9 copy-done.3
  85.4 0.0 copy-start.9
  85.4 0.7 copy-done.9
  86.2 0.0 copy-start.10
  86.2 0.7 copy-done.10
  86.9 0.0 copy-start.7
  86.9 0.0 copy-start.8
  86.9 0.0 copy-start.4
  86.9 12.7 %all_to_all.25 = bf16[16,16,512]{2,1,0:T(8,128)(2,1)S(1)} all-to-all(bf16[16,16,512]{2,1,0:T(8,128)(2,1)S(1)} %bitcast.30), channel_id=1, replica_groups=mesh['z'=16,'yl'=2,'x'=4,'yh'=2,'c'=2] {'x','yh','c'}, dimensions={0} | all-to-all | bytes 524288 | tf_op jit(solution)/shard_map/all_to_all | solution.py:39
  99.7 0.0 copy-done.7
  99.7 0.0 copy-done.8
  99.7 0.7 broadcast_in_dim.5
  100.5 5.3 %all-to-all-start.3 = ((bf16[16,16,512]{2,1,0:T(8,128)(2,1)}), bf16[16,16,512]{2,1,0:T(8,128)(2,1)S(1)}, u32[]{:S(2)}, u32[]{:S(2)}) async-start(bf16[16,16,512]{2,1,0:T(8,128)(2,1)} %broadcast_in_dim.5), calls=%async_computation.3 | async-start | bytes 524288 | tf_op jit(solution)/shard_map/all_to_all | solution.py:31
  105.8 2.0 %collective-permute-start.5 = (bf16[256,768]{1,0:T(8,128)(2,1)}, bf16[256,768]{1,0:T(8,128)(2,1)S(1)}, u32[]{:S(2)}, u32[]{:S(2)}) collective-permute-start(bf16[256,768]{1,0:T(8,128)(2,1)} %copy-done.10), channel_id=1, source_target_pairs={{0,1},{1,0},{2,3},{3,2},{4,5},{5,4},{6,7},{7,6},{8,9},{9,8},{10,11... | collective-permute-start | bytes 1179656 | tf_op jit(solution)/shard_map/ppermute | solution.py:18
  107.8 4.9 %collective-permute-start.6 = (bf16[256,768]{1,0:T(8,128)(2,1)}, bf16[256,768]{1,0:T(8,128)(2,1)S(1)}, u32[]{:S(2)}, u32[]{:S(2)}) collective-permute-start(bf16[256,768]{1,0:T(8,128)(2,1)} %copy-done.9), channel_id=1, source_target_pairs={{0,2},{2,0},{1,3},{3,1},{4,6},{6,4},{5,7},{7,5},{8,10},{10,8},{9,1... | collective-permute-start | bytes 1179656 | tf_op jit(solution)/shard_map/ppermute | solution.py:18
  112.7 2.7 %collective-permute-start.7 = (bf16[256,768]{1,0:T(8,128)(2,1)}, bf16[256,768]{1,0:T(8,128)(2,1)S(1)}, u32[]{:S(2)}, u32[]{:S(2)}) collective-permute-start(bf16[256,768]{1,0:T(8,128)(2,1)} %copy-done.8), channel_id=1, source_target_pairs={{0,4},{4,0},{8,12},{12,8},{1,5},{5,1},{9,13},{13,9},{2,6},{6,2},{1... | collective-permute-start | bytes 1179656 | tf_op jit(solution)/shard_map/ppermute | solution.py:18
  115.5 3.0 %collective-permute-start.8 = (bf16[256,768]{1,0:T(8,128)(2,1)}, bf16[256,768]{1,0:T(8,128)(2,1)S(1)}, u32[]{:S(2)}, u32[]{:S(2)}) collective-permute-start(bf16[256,768]{1,0:T(8,128)(2,1)} %copy-done.7), channel_id=1, source_target_pairs={{0,8},{4,12},{8,0},{12,4},{1,9},{5,13},{9,1},{13,5},{2,10},{6,14},... | collective-permute-start | bytes 1179656 | tf_op jit(solution)/shard_map/ppermute | solution.py:18
  118.5 0.0 all-to-all-done.3
  118.5 0.0 copy-done
  118.5 0.4 fusion.3
  118.9 0.0 collective-permute-done.5
  118.9 3.9 %collective-permute-done.6 = bf16[256,768]{1,0:T(8,128)(2,1)S(1)} collective-permute-done((bf16[256,768]{1,0:T(8,128)(2,1)}, bf16[256,768]{1,0:T(8,128)(2,1)S(1)}, u32[]{:S(2)}, u32[]{:S(2)}) %collective-permute-start.6) | collective-permute-done | bytes 393248 | tf_op jit(solution)/shard_map/ppermute | solution.py:18
  122.9 4.0 %collective-permute-done.7 = bf16[256,768]{1,0:T(8,128)(2,1)S(1)} collective-permute-done((bf16[256,768]{1,0:T(8,128)(2,1)}, bf16[256,768]{1,0:T(8,128)(2,1)S(1)}, u32[]{:S(2)}, u32[]{:S(2)}) %collective-permute-start.7) | collective-permute-done | bytes 393248 | tf_op jit(solution)/shard_map/ppermute | solution.py:18
  126.8 7.5 %collective-permute-done.8 = bf16[256,768]{1,0:T(8,128)(2,1)S(1)} collective-permute-done((bf16[256,768]{1,0:T(8,128)(2,1)}, bf16[256,768]{1,0:T(8,128)(2,1)S(1)}, u32[]{:S(2)}, u32[]{:S(2)}) %collective-permute-start.8) | collective-permute-done | bytes 393248 | tf_op jit(solution)/shard_map/ppermute | solution.py:18
  134.3 0.0 copy-done.4
  134.3 0.3 add_convert_fusion
  134.6 29.3 %all_to_all.26 = bf16[16,16,768]{2,1,0:T(8,128)(2,1)S(1)} all-to-all(bf16[16,16,768]{2,1,0:T(8,128)(2,1)S(1)} %bitcast.31), channel_id=1, replica_groups=mesh['z'=16,'yl'=2,'x'=4,'yh'=2,'c'=2] {'z'}, dimensions={0} | all-to-all | bytes 786432 | tf_op jit(solution)/shard_map/all_to_all | solution.py:117
  163.9 0.1 convert_reduce_fusion
  164.0 0.6 reduce-precision_convert_fusion
  (4 shorter events, 0.1 us)
Async XLA Ops:
  0.0 118.5 %copy-start = (bf16[512,768]{1,0:T(8,128)(2,1)S(1)}, bf16[512,768]{1,0:T(8,128)(2,1)}, u32[]{:S(2)}) copy-start(bf16[512,768]{1,0:T(8,128)(2,1)} %param.13) | copy-start | bytes 2359300
  0.9 6.5 %copy-start.12 = (bf16[16,768]{1,0:T(8,128)(2,1)S(1)}, bf16[16,768]{1,0:T(8,128)(2,1)}, u32[]{:S(2)}) copy-start(bf16[16,768]{1,0:T(8,128)(2,1)} %param.7) | copy-start | bytes 73732
  0.9 44.1 %copy-start.11 = (bf16[768,512]{1,0:T(8,128)(2,1)S(1)}, bf16[768,512]{1,0:T(8,128)(2,1)}, u32[]{:S(2)}) copy-start(bf16[768,512]{1,0:T(8,128)(2,1)} %param.10) | copy-start | bytes 2359300
  3.7 76.4 %copy-start.1 = (bf16[1,96,5,768]{3,1,2,0:T(8,128)(2,1)S(1)}, bf16[1,96,5,768]{3,1,2,0:T(8,128)(2,1)}, u32[]{:S(2)}) copy-start(bf16[1,96,5,768]{3,1,2,0:T(8,128)(2,1)} %param.8) | copy-start | bytes 2211844
  3.7 76.4 %copy-start.2 = (bf16[1,96,5,768]{3,1,2,0:T(8,128)(2,1)S(1)}, bf16[1,96,5,768]{3,1,2,0:T(8,128)(2,1)}, u32[]{:S(2)}) copy-start(bf16[1,96,5,768]{3,1,2,0:T(8,128)(2,1)} %param.9) | copy-start | bytes 2211844
  3.7 76.4 %copy-start.5 = (bf16[1,96,512]{2,1,0:T(8,128)(2,1)S(1)}, bf16[1,96,512]{2,1,0:T(8,128)(2,1)}, u32[]{:S(2)}) copy-start(bf16[1,96,512]{2,1,0:T(8,128)(2,1)} %param.12) | copy-start | bytes 294916
  3.7 76.4 %copy-start.6 = (bf16[1,96,512]{2,1,0:T(8,128)(2,1)S(1)}, bf16[1,96,512]{2,1,0:T(8,128)(2,1)}, u32[]{:S(2)}) copy-start(bf16[1,96,512]{2,1,0:T(8,128)(2,1)} %param.11) | copy-start | bytes 294916
  3.8 76.4 %collective-permute-start.4 = (bf16[1152,768]{1,0:T(8,128)(2,1)}, bf16[1152,768]{1,0:T(8,128)(2,1)}, u32[]{:S(2)}, u32[]{:S(2)}) collective-permute-start(bf16[1152,768]{1,0:T(8,128)(2,1)} %fusion.1), channel_id=1, source_target_pairs={{0,16},{16,0},{1,17},{17,1},{2,18},{18,2},{3,19},{19,3},{4,20},{20... | collective-permute-start | bytes 5308424 | tf_op jit(solution)/shard_map/ppermute | solution.py:18
  46.1 19.2 %all-to-all-start = ((bf16[16,16,512]{2,1,0:T(8,128)(2,1)}), bf16[16,16,512]{2,1,0:T(8,128)(2,1)S(1)}, u32[]{:S(2)}, u32[]{:S(2)}) async-start(bf16[16,16,512]{2,1,0:T(8,128)(2,1)} %bitcast), calls=%async_computation | async-start | bytes 524288 | tf_op jit(solution)/shard_map/all_to_all | solution.py:39
  53.2 19.0 %collective-permute-start.3 = (bf16[256,768]{1,0:T(8,128)(2,1)S(1)}, bf16[256,768]{1,0:T(8,128)(2,1)S(1)}, u32[]{:S(2)}, u32[]{:S(2)}) collective-permute-start(bf16[256,768]{1,0:T(8,128)(2,1)S(1)} %all_gather.3.x0), channel_id=1, source_target_pairs={{0,8},{4,12},{8,0},{12,4},{1,9},{5,13},{9,1},{13,5},{2,10},{6,14},... | collective-permute-start | bytes 1179656 | tf_op jit(solution)/shard_map/ppermute | solution.py:18
  56.6 19.0 %collective-permute-start.2 = (bf16[256,768]{1,0:T(8,128)(2,1)S(1)}, bf16[256,768]{1,0:T(8,128)(2,1)}, u32[]{:S(2)}, u32[]{:S(2)}) collective-permute-start(bf16[256,768]{1,0:T(8,128)(2,1)S(1)} %all_gather.3.x0), channel_id=1, source_target_pairs={{0,4},{4,0},{8,12},{12,8},{1,5},{5,1},{9,13},{13,9},{2,6},{6,2},{1... | collective-permute-start | bytes 1179656 | tf_op jit(solution)/shard_map/ppermute | solution.py:18
  58.5 17.1 %collective-permute-start.1 = (bf16[256,768]{1,0:T(8,128)(2,1)S(1)}, bf16[256,768]{1,0:T(8,128)(2,1)}, u32[]{:S(2)}, u32[]{:S(2)}) collective-permute-start(bf16[256,768]{1,0:T(8,128)(2,1)S(1)} %all_gather.3.x0), channel_id=1, source_target_pairs={{0,2},{2,0},{1,3},{3,1},{4,6},{6,4},{5,7},{7,5},{8,10},{10,8},{9,1... | collective-permute-start | bytes 1179656 | tf_op jit(solution)/shard_map/ppermute | solution.py:18
  63.4 12.2 %collective-permute-start = (bf16[256,768]{1,0:T(8,128)(2,1)S(1)}, bf16[256,768]{1,0:T(8,128)(2,1)}, u32[]{:S(2)}, u32[]{:S(2)}) collective-permute-start(bf16[256,768]{1,0:T(8,128)(2,1)S(1)} %all_gather.3.x0), channel_id=1, source_target_pairs={{0,1},{1,0},{2,3},{3,2},{4,5},{5,4},{6,7},{7,6},{8,9},{9,8},{10,11... | collective-permute-start | bytes 1179656 | tf_op jit(solution)/shard_map/ppermute | solution.py:18
  66.2 14.0 %all-to-all-start.1 = ((bf16[16,16,512]{2,1,0:T(8,128)(2,1)}), bf16[16,16,512]{2,1,0:T(8,128)(2,1)S(1)}, u32[]{:S(2)}, u32[]{:S(2)}) async-start(bf16[16,16,512]{2,1,0:T(8,128)(2,1)} %broadcast_in_dim.4), calls=%async_computation.1 | async-start | bytes 524288 | tf_op jit(solution)/shard_map/all_to_all | solution.py:31
  84.6 0.9 copy-start.3
  85.4 0.7 copy-start.9
  86.2 0.7 copy-start.10
  86.9 12.7 %copy-start.7 = (bf16[256,768]{1,0:T(8,128)(2,1)}, bf16[256,768]{1,0:T(8,128)(2,1)S(1)}, u32[]{:S(2)}) copy-start(bf16[256,768]{1,0:T(8,128)(2,1)S(1)} %get-tuple-element.16) | copy-start | bytes 1179652
  86.9 12.8 %copy-start.8 = (bf16[256,768]{1,0:T(8,128)(2,1)}, bf16[256,768]{1,0:T(8,128)(2,1)S(1)}, u32[]{:S(2)}) copy-start(bf16[256,768]{1,0:T(8,128)(2,1)S(1)} %get-tuple-element.15) | copy-start | bytes 1179652
  86.9 47.4 %copy-start.4 = (f32[256,768]{1,0:T(8,128)S(1)}, f32[256,768]{1,0:T(8,128)}, u32[]{:S(2)}) copy-start(f32[256,768]{1,0:T(8,128)} %copy-done.3) | copy-start | bytes 2359300
  100.5 18.0 %all-to-all-start.3 = ((bf16[16,16,512]{2,1,0:T(8,128)(2,1)}), bf16[16,16,512]{2,1,0:T(8,128)(2,1)S(1)}, u32[]{:S(2)}, u32[]{:S(2)}) async-start(bf16[16,16,512]{2,1,0:T(8,128)(2,1)} %broadcast_in_dim.5), calls=%async_computation.3 | async-start | bytes 524288 | tf_op jit(solution)/shard_map/all_to_all | solution.py:31
  105.8 13.1 %collective-permute-start.5 = (bf16[256,768]{1,0:T(8,128)(2,1)}, bf16[256,768]{1,0:T(8,128)(2,1)S(1)}, u32[]{:S(2)}, u32[]{:S(2)}) collective-permute-start(bf16[256,768]{1,0:T(8,128)(2,1)} %copy-done.10), channel_id=1, source_target_pairs={{0,1},{1,0},{2,3},{3,2},{4,5},{5,4},{6,7},{7,6},{8,9},{9,8},{10,11... | collective-permute-start | bytes 1179656 | tf_op jit(solution)/shard_map/ppermute | solution.py:18
  107.8 15.0 %collective-permute-start.6 = (bf16[256,768]{1,0:T(8,128)(2,1)}, bf16[256,768]{1,0:T(8,128)(2,1)S(1)}, u32[]{:S(2)}, u32[]{:S(2)}) collective-permute-start(bf16[256,768]{1,0:T(8,128)(2,1)} %copy-done.9), channel_id=1, source_target_pairs={{0,2},{2,0},{1,3},{3,1},{4,6},{6,4},{5,7},{7,5},{8,10},{10,8},{9,1... | collective-permute-start | bytes 1179656 | tf_op jit(solution)/shard_map/ppermute | solution.py:18
  112.7 14.1 %collective-permute-start.7 = (bf16[256,768]{1,0:T(8,128)(2,1)}, bf16[256,768]{1,0:T(8,128)(2,1)S(1)}, u32[]{:S(2)}, u32[]{:S(2)}) collective-permute-start(bf16[256,768]{1,0:T(8,128)(2,1)} %copy-done.8), channel_id=1, source_target_pairs={{0,4},{4,0},{8,12},{12,8},{1,5},{5,1},{9,13},{13,9},{2,6},{6,2},{1... | collective-permute-start | bytes 1179656 | tf_op jit(solution)/shard_map/ppermute | solution.py:18
  115.5 18.8 %collective-permute-start.8 = (bf16[256,768]{1,0:T(8,128)(2,1)}, bf16[256,768]{1,0:T(8,128)(2,1)S(1)}, u32[]{:S(2)}, u32[]{:S(2)}) collective-permute-start(bf16[256,768]{1,0:T(8,128)(2,1)} %copy-done.7), channel_id=1, source_target_pairs={{0,8},{4,12},{8,0},{12,4},{1,9},{5,13},{9,1},{13,5},{2,10},{6,14},... | collective-permute-start | bytes 1179656 | tf_op jit(solution)/shard_map/ppermute | solution.py:18

commit v3 on v2

--- a/solution.py
+++ b/solution.py
@@ -11,6 +11,8 @@
 F32 = jnp.float32
 BF16 = jnp.bfloat16
 FEAT = ("x", "yh", "c")
+UP_MIB = 24
+DOWN_MIB = 60
 LEVEL_AXES = (("c", 0), ("yh", 0), ("x", 0), ("x", 1))
 
 
@@ -42,42 +44,126 @@
     return whole.reshape((-1,) + group.shape[1:])
 
 
-def ffn_body(kinds, rows, db, rank, x0, x1, x2, x3, x4, code, up, right, down, left, other, t0, t1, t2, t3, t4, back):
+def fetch(src, dst, sem, lo, size):
+    part = pl.ds(lo, size)
+    return pltpu.make_async_copy(src.at[part], dst.at[part], sem)
+
+
+def pair(mine, other, rows, base, k):
+    lo = k * rows
+    return jnp.concatenate([mine[lo : lo + rows, :], other[base + lo : base + lo + rows, :]], axis=0)
+
+
+def up_body(kinds, rows, db, rank, *refs):
     n = kinds * rows
     head = db - rank
-    xs = (x0, x1, x2, x3, x4)
-
-    def pair(ref, base, k):
-        lo = k * rows
-        return jnp.concatenate([ref[lo : lo + rows, :], other[base + lo : base + lo + rows, :]], axis=0)
-
-    pre = dot_nt(code[...], jnp.concatenate([right[...], other[2 * n : 2 * n + rows, :rank]], axis=0))
-    for k in range(kinds):
-        pre = pre + dot_nt(xs[k][...], pair(up, 0, k))
+    count = kinds + 4
+    ins, (hidden_out, back) = refs[:count], refs[count : count + 2]
+    bufs, sems = refs[count + 2 : -1], refs[-1]
+    xs, (up, right, left, other) = bufs[:kinds], bufs[kinds:]
+
+    def whole(i):
+        return fetch(ins[i], bufs[i], sems.at[i], 0, ins[i].shape[0])
+
+    last = count - 1
+    first = [
+        whole(0),
+        whole(kinds + 1),
+        fetch(ins[last], other, sems.at[last], 2 * n, 2 * rows),
+        whole(kinds),
+        fetch(ins[last], other, sems.at[last + 1], 0, n),
+    ]
+    partners = [whole(i) for i in range(1, kinds)]
+    late = whole(kinds + 2)
+    for copy in first + partners + [late]:
+        copy.start()
+    for copy in first:
+        copy.wait()
+    pre = dot_nt(xs[0][:, db:], jnp.concatenate([right[...], other[2 * n : 2 * n + rows, :rank]], axis=0))
+    pre = pre + dot_nt(xs[0][:, :db], pair(up, other, rows, 0, 0))
+    for k in range(1, kinds):
+        partners[k - 1].wait()
+        pre = pre + dot_nt(xs[k][...], pair(up, other, rows, 0, k))
     hidden = (0.5 * pre * (1.0 + lax.erf(pre * (0.5**0.5)))).astype(BF16)
-    outs = (t0, t1, t2, t3, t4)
-    for k in (2, 3, 4, 1, 0):
-        outs[k][...] = dot_nn(hidden, pair(down, n, k)).astype(outs[k].dtype)
+    hidden_out[...] = hidden
+    late.wait()
     low = jnp.concatenate([left[:, :head], other[2 * n : 2 * n + rows, rank:]], axis=0)
     high = jnp.concatenate([left[:, head:], other[2 * n + rows :, : rank - head]], axis=0)
     back[:, :head] = dot_nn(hidden, low).astype(BF16)
     back[:, head:] = dot_nn(hidden, high).astype(BF16)
 
 
-def ffn_call(pieces, code, up, right, down, left, other):
-    count = code.shape[0]
+def up_call(gathered, pieces, up, right, left, other):
+    count = gathered.shape[0]
     rows, rank = right.shape
     db = up.shape[1]
     kinds = up.shape[0] // rows
+    args = (gathered, *pieces, up, right, left, other)
+    return pl.pallas_call(
+        functools.partial(up_body, kinds, rows, db, rank),
+        out_shape=[jax.ShapeDtypeStruct((count, 2 * rows), BF16), jax.ShapeDtypeStruct((count, rank), BF16)],
+        in_specs=[pl.BlockSpec(memory_space=pl.ANY)] * len(args),
+        scratch_shapes=[pltpu.VMEM(a.shape, BF16) for a in args] + [pltpu.SemaphoreType.DMA((len(args) + 1,))],
+        compiler_params=pltpu.CompilerParams(vmem_limit_bytes=UP_MIB * 2**20),
+        name="ffn_up",
+    )(*args)
+
+
+def down_body(kinds, rows, hidden_in, down_in, other_in, *refs):
+    n = kinds * rows
+    outs, (hidden, down, other) = refs[:kinds], refs[kinds : kinds + 3]
+    stage, (in_sems, out_sems) = refs[kinds + 3 : -2], refs[-2:]
+    head = fetch(hidden_in, hidden, in_sems.at[2 * kinds], 0, hidden.shape[0])
+    head.start()
+    order = (2, 4, 3, 1, 0)
+    loads = {}
+    for k in order:
+        loads[k] = (
+            fetch(down_in, down, in_sems.at[2 * k], k * rows, rows),
+            fetch(other_in, other, in_sems.at[2 * k + 1], n + k * rows, rows),
+        )
+        for copy in loads[k]:
+            copy.start()
+    head.wait()
+    stores = []
+    for k in order:
+        for copy in loads[k]:
+            copy.wait()
+        stage[k][...] = dot_nn(hidden[...], pair(down, other, rows, n, k)).astype(outs[k].dtype)
+        stores.append(pltpu.make_async_copy(stage[k], outs[k], out_sems.at[k]))
+        stores[-1].start()
+    for copy in stores:
+        copy.wait()
+
+
+def down_call(hidden, down, other):
+    count, db = hidden.shape[0], down.shape[1]
+    rows = hidden.shape[1] // 2
+    kinds = down.shape[0] // rows
     shapes = [jax.ShapeDtypeStruct((count, db), F32)]
     shapes += [jax.ShapeDtypeStruct((count, db), BF16)] * (kinds - 1)
-    shapes += [jax.ShapeDtypeStruct((count, rank), BF16)]
     return pl.pallas_call(
-        functools.partial(ffn_body, kinds, rows, db, rank),
+        functools.partial(down_body, kinds, rows),
         out_shape=shapes,
-        compiler_params=pltpu.CompilerParams(vmem_limit_bytes=16 * 2**20),
-        name="ffn",
-    )(*pieces, code, up, right, down, left, other)
+        in_specs=[pl.BlockSpec(memory_space=pl.ANY)] * 3,
+        out_specs=[pl.BlockSpec(memory_space=pl.ANY)] * kinds,
+        scratch_shapes=[pltpu.VMEM(a.shape, BF16) for a in (hidden, down, other)]
+        + [pltpu.VMEM(a.shape, a.dtype) for a in shapes]
+        + [pltpu.SemaphoreType.DMA((2 * kinds + 1,)), pltpu.SemaphoreType.DMA((kinds,))],
+        compiler_params=pltpu.CompilerParams(vmem_limit_bytes=DOWN_MIB * 2**20),
+        name="ffn_down",
+    )(hidden, down, other)
+
+
+def code_body(x, w, stack):
+    part = dot_nn(x[...], w[...]).astype(BF16)
+    for i in range(stack.shape[0]):
+        stack[i] = part
+
+
+def code_call(tokens, up_left, n):
+    shape = jax.ShapeDtypeStruct((n, tokens.shape[0], up_left.shape[1]), BF16)
+    return pl.pallas_call(code_body, out_shape=shape, name="code_part", compiler_params=pltpu.CompilerParams(vmem_limit_bytes=8 * 2**20))(tokens, up_left)
 
 
 def per_device(tokens, up_weight, down_weight, up_left, up_right, down_left, down_right):
@@ -98,15 +184,19 @@
         ],
         axis=0,
     )
+    stack = code_call(tokens, up_left, nf)
+    stack = lax.all_to_all(stack, FEAT, 0, 0, tiled=True)
     other = swap(packed, "yl", 0)
-    own = lax.all_gather(tokens, "z", axis=0, tiled=True)
-    code = sum_over_feat(dot_nn(own, up_left).astype(BF16), nf)
-    pieces = [own]
+    mine = jnp.concatenate([tokens, total_of(stack)], axis=1)
+    gathered = lax.all_gather(mine, "z", axis=0, tiled=True)
+    own = gathered[:, :db]
+    pieces = []
     for axis, bit in LEVEL_AXES:
         pieces.append(swap(own, axis, bit))
 
-    own_total, *terms, back = ffn_call(pieces, code, up, up_right[0], down, down_left[0], other)
+    hidden, back = up_call(gathered, pieces, up, up_right[0], down_left[0], other)
     back = sum_over_feat(back, nf)
+    own_total, *terms = down_call(hidden, down, other)
     sent = []
     for part, (axis, bit) in zip(terms, LEVEL_AXES):
         sent.append(swap(part, axis, bit))

time: 167 us -> 204 us (1.22)
  blocking collectives: 79.7 us -> 126 us
  starting transfers between devices: 46.9 us -> 32.5 us
  waiting for transfers between devices: 23.3 us -> 31.1 us
  Pallas kernels: 4.38 us -> 7.53 us
  local copies, waits for them, and re-layouts: 4.76 us -> 1.7 us
    all_to_all x0 -> x1, blocking collectives: none -> 43.6 us  [per_device(): stack = lax.all_to_all(stack, FEAT, 0, 0, tiled=True)]
    ppermute x9, waiting for transfers between devices: 18.8 us -> 31.1 us  [swap(): lax.ppermute(array, axis, [(i, i ^ 1 << bit) for i in range(lax.axis_size...]
    all_to_all x1 -> x0, starting transfers between devices: 7.13 us -> none  [sum_over_feat(): lax.all_to_all(part.reshape((n, part.shape[0] // n) + part.shape[1:]), FE...]
    all_to_all x2 -> x1, starting transfers between devices: 11.4 us -> 5.34 us  [share(): lax.all_to_all(jnp.broadcast_to(array[None], (n,) + array.shape), axis, 0...]
    all_to_all x2 -> x1, waiting for transfers between devices: 4.53 us -> 0.01 us  [share(): lax.all_to_all(jnp.broadcast_to(array[None], (n,) + array.shape), axis, 0...]
    pallas_call x1 -> x3, Pallas kernels: 4.38 us -> 7.53 us  [the longest x1 3.8 us: up_call(): pl.pallas_call(functools.partial(up_body, kinds, rows, db, rank), out_sha...]
    unnamed x26 -> x18, local copies, waits for them, and re-layouts: 2.39 us -> 0.05 us
  transfers between devices with their start and end apart: 12 -> 10, of which waited for: 5 -> 6; matrix products, arithmetic and copies ran while one was open for 1% -> 0% of each run, Pallas kernels for 0% -> 2%
where the time goes in v3:
time: 204 us; the launch traced here: 202 us
  blocking collectives  126 us (62%)
  starting transfers between devices  32.5 us (16%)
  waiting for transfers between devices  31.1 us (15%)
  Pallas kernels  7.53 us (4%)
  other arithmetic  2.61 us (1%)
    all_to_all x1, blocking collectives, per_device(): stack = lax.all_to_all(stack, FEAT, 0, 0, tiled=True)  43.6 us
    all_gather x1, blocking collectives, per_device(): gathered = lax.all_gather(mine, 'z', axis=0, tiled=True)  38.9 us
    ppermute x9, waiting for transfers between devices, swap(): lax.ppermute(array, axis, [(i, i ^ 1 << bit) for i in range(lax.axis_size...  31.1 us
    all_to_all x1, blocking collectives, per_device(): total = lax.all_to_all(total.reshape(nz, count, db), 'z', 0, 0, tiled=True)  29.8 us
    ppermute x9, starting transfers between devices, swap(): lax.ppermute(array, axis, [(i, i ^ 1 << bit) for i in range(lax.axis_size...  27.2 us
    all_to_all x1, blocking collectives, sum_over_feat(): lax.all_to_all(part.reshape((n, part.shape[0] // n) + part.shape[1:]), FE...  13.8 us
    all_to_all x1, starting transfers between devices, share(): lax.all_to_all(jnp.broadcast_to(array[None], (n,) + array.shape), axis, 0...  5.34 us
  transfers between devices with their start and end apart: 10, of which 6 were waited for; matrix products, arithmetic and copies ran while one was open for 0% of the time, Pallas kernels for 2%

profile of v3, /device:TPU:6, one launch (start us, length us, event | category | flops | bytes accessed | tf_op | source)
XLA Modules:
  0.0 202.2 jit_solution(2820889133730493540)
XLA Ops:
  0.0 0.0 copy-start
  0.0 0.9 fusion.2
  0.9 0.0 copy-start.3
  0.9 0.0 copy-start.7
  0.9 1.6 fusion.1
  2.5 0.0 copy-start.2
  2.5 0.0 copy-start.4
  2.5 0.0 copy-start.5
  2.5 3.6 %collective-permute-start.4 = (bf16[1152,768]{1,0:T(8,128)(2,1)S(1)}, bf16[1152,768]{1,0:T(8,128)(2,1)S(1)}, u32[]{:S(2)}, u32[]{:S(2)}) collective-permute-start(bf16[1152,768]{1,0:T(8,128)(2,1)S(1)} %fusion.1), channel_id=1, source_target_pairs={{0,16},{16,0},{1,17},{17,1},{2,18},{18,2},{3,19},{19,3},{4,20},{20... | collective-permute-start | bytes 5308424 | tf_op jit(solution)/shard_map/ppermute | solution.py:20
  6.2 0.0 copy-done.3
  6.2 0.0 copy-done.7
  6.2 0.2 code_part.1
  6.4 43.6 %all_to_all.20 = bf16[16,16,512]{2,1,0:T(8,128)(2,1)S(1)} all-to-all(bf16[16,16,512]{2,1,0:T(8,128)(2,1)S(1)} %code_part.1), channel_id=1, replica_groups=mesh['z'=16,'yl'=2,'x'=4,'yh'=2,'c'=2] {'x','yh','c'}, dimensions={0} | all-to-all | bytes 524288 | tf_op jit(solution)/shard_map/all_to_all | solution.py:188
  50.1 38.9 %all_gather.3.refs_0_ = bf16[256,1280]{1,0:T(8,128)(2,1)S(1)} all-gather(bf16[16,1280]{1,0:T(8,128)(2,1)S(1)} %pad_maximum_fusion), channel_id=1, replica_groups=mesh['z'=16,'yl'=2,'x'=4,'yh'=2,'c'=2] {'z'}, dimensions={0}, use_global_device_ids=true | all-gather | bytes 696320 | tf_op jit(solution)/shard_map/all_gather | solution.py:191
  89.0 1.9 collective-permute-start
  91.0 3.1 %collective-permute-start.1 = (bf16[256,768]{1,0:T(8,128)(2,1)S(1)}, bf16[256,768]{1,0:T(8,128)(2,1)S(1)}, u32[]{:S(2)}, u32[]{:S(2)}) collective-permute-start(bf16[256,768]{1,0:T(8,128)(2,1)S(1)} %slice.12), channel_id=1, source_target_pairs={{0,2},{2,0},{1,3},{3,1},{4,6},{6,4},{5,7},{7,5},{8,10},{10,8},{9,1... | collective-permute-start | bytes 1179656 | tf_op jit(solution)/shard_map/ppermute | solution.py:20
  94.0 2.7 %collective-permute-start.2 = (bf16[256,768]{1,0:T(8,128)(2,1)S(1)}, bf16[256,768]{1,0:T(8,128)(2,1)S(1)}, u32[]{:S(2)}, u32[]{:S(2)}) collective-permute-start(bf16[256,768]{1,0:T(8,128)(2,1)S(1)} %slice.12), channel_id=1, source_target_pairs={{0,4},{4,0},{8,12},{12,8},{1,5},{5,1},{9,13},{13,9},{2,6},{6,2},{1... | collective-permute-start | bytes 1179656 | tf_op jit(solution)/shard_map/ppermute | solution.py:20
  96.8 3.0 %collective-permute-start.3 = (bf16[256,768]{1,0:T(8,128)(2,1)S(1)}, bf16[256,768]{1,0:T(8,128)(2,1)S(1)}, u32[]{:S(2)}, u32[]{:S(2)}) collective-permute-start(bf16[256,768]{1,0:T(8,128)(2,1)S(1)} %slice.12), channel_id=1, source_target_pairs={{0,8},{4,12},{8,0},{12,4},{1,9},{5,13},{9,1},{13,5},{2,10},{6,14},... | collective-permute-start | bytes 1179656 | tf_op jit(solution)/shard_map/ppermute | solution.py:20
  99.8 0.0 collective-permute-done.refs_1_
  99.8 6.1 %collective-permute-done.1.refs_2_ = bf16[256,768]{1,0:T(8,128)(2,1)S(1)} collective-permute-done((bf16[256,768]{1,0:T(8,128)(2,1)S(1)}, bf16[256,768]{1,0:T(8,128)(2,1)S(1)}, u32[]{:S(2)}, u32[]{:S(2)}) %collective-permute-start.1) | collective-permute-done | bytes 393248 | tf_op jit(solution)/shard_map/ppermute | solution.py:20
  105.9 2.0 %collective-permute-done.2.refs_3_ = bf16[256,768]{1,0:T(8,128)(2,1)S(1)} collective-permute-done((bf16[256,768]{1,0:T(8,128)(2,1)S(1)}, bf16[256,768]{1,0:T(8,128)(2,1)S(1)}, u32[]{:S(2)}, u32[]{:S(2)}) %collective-permute-start.2) | collective-permute-done | bytes 393248 | tf_op jit(solution)/shard_map/ppermute | solution.py:20
  107.9 7.6 %collective-permute-done.3.refs_4_ = bf16[256,768]{1,0:T(8,128)(2,1)S(1)} collective-permute-done((bf16[256,768]{1,0:T(8,128)(2,1)S(1)}, bf16[256,768]{1,0:T(8,128)(2,1)S(1)}, u32[]{:S(2)}, u32[]{:S(2)}) %collective-permute-start.3) | collective-permute-done | bytes 393248 | tf_op jit(solution)/shard_map/ppermute | solution.py:20
  115.5 0.0 collective-permute-done.4.refs_8_.other_in
  115.5 0.0 copy-done.2
  115.5 0.0 copy-done.4
  115.5 0.0 copy-done.5
  115.5 0.0 copy-start.1
  115.5 3.8 %ffn_up.1 = (bf16[256,192]{1,0:T(8,128)(2,1)S(1)}, bf16[256,512]{1,0:T(8,128)(2,1)S(1)}) custom-call(bf16[256,1280]{1,0:T(8,128)(2,1)S(1)} %all_gather.3.refs_0_, bf16[256,768]{1,0:T(8,128)(2,1)S(1)} %collective-permute-done.refs_1_, bf16[256,768]{1,0:T(8,128)(2,1)S(1)} %collective-permute-done.1.refs_2_, ...), custom_call_target="tpu_custom_call" | custom-call | tf_op jit(solution)/shard_map/ffn_up/pallas_call | solution.py:102
  119.4 0.0 copy-done.1
  119.4 0.0 copy-start.6
  119.4 13.8 %all_to_all.21 = bf16[16,16,512]{2,1,0:T(8,128)(2,1)S(1)} all-to-all(bf16[16,16,512]{2,1,0:T(8,128)(2,1)S(1)} %bitcast.23), channel_id=1, replica_groups=mesh['z'=16,'yl'=2,'x'=4,'yh'=2,'c'=2] {'x','yh','c'}, dimensions={0} | all-to-all | bytes 524288 | tf_op jit(solution)/shard_map/all_to_all | solution.py:41
  133.1 0.0 copy-done.6
  133.2 0.7 broadcast_in_dim.2
  133.9 5.3 %all-to-all-start.2 = ((bf16[16,16,512]{2,1,0:T(8,128)(2,1)}), bf16[16,16,512]{2,1,0:T(8,128)(2,1)S(1)}, u32[]{:S(2)}, u32[]{:S(2)}) async-start(bf16[16,16,512]{2,1,0:T(8,128)(2,1)} %broadcast_in_dim.2), calls=%async_computation.2 | async-start | bytes 524288 | tf_op jit(solution)/shard_map/all_to_all | solution.py:33
  139.3 3.5 %ffn_down.1 = (f32[256,768]{1,0:T(8,128)}, bf16[256,768]{1,0:T(8,128)(2,1)}, bf16[256,768]{1,0:T(8,128)(2,1)}, bf16[256,768]{1,0:T(8,128)(2,1)}, bf16[256,768]{1,0:T(8,128)(2,1)}) custom-call(bf16[256,192]{1,0:T(8,128)(2,1)} %copy-done.6, bf16[480,768]{1,0:T(8,128)(2,1)} %bitcast.25, bf16[1152,768]{1,0:T(8,128)(2,1)} %copy-done.1), custom_call_target="tpu_custom_call" | custom-call | tf_op jit(solution)/shard_map/ffn_down/pallas_call | solution.py:145
  142.8 0.0 copy-start.8
  142.8 2.2 %collective-permute-start.5 = (bf16[256,768]{1,0:T(8,128)(2,1)}, bf16[256,768]{1,0:T(8,128)(2,1)S(1)}, u32[]{:S(2)}, u32[]{:S(2)}) collective-permute-start(bf16[256,768]{1,0:T(8,128)(2,1)} %get-tuple-element.15), channel_id=1, source_target_pairs={{0,1},{1,0},{2,3},{3,2},{4,5},{5,4},{6,7},{7,6},{8,9},{9,8},{10,11... | collective-permute-start | bytes 1179656 | tf_op jit(solution)/shard_map/ppermute | solution.py:20
  145.0 4.9 %collective-permute-start.6 = (bf16[256,768]{1,0:T(8,128)(2,1)}, bf16[256,768]{1,0:T(8,128)(2,1)S(1)}, u32[]{:S(2)}, u32[]{:S(2)}) collective-permute-start(bf16[256,768]{1,0:T(8,128)(2,1)} %get-tuple-element.16), channel_id=1, source_target_pairs={{0,2},{2,0},{1,3},{3,1},{4,6},{6,4},{5,7},{7,5},{8,10},{10,8},{9,1... | collective-permute-start | bytes 1179656 | tf_op jit(solution)/shard_map/ppermute | solution.py:20
  149.8 2.7 %collective-permute-start.7 = (bf16[256,768]{1,0:T(8,128)(2,1)}, bf16[256,768]{1,0:T(8,128)(2,1)S(1)}, u32[]{:S(2)}, u32[]{:S(2)}) collective-permute-start(bf16[256,768]{1,0:T(8,128)(2,1)} %get-tuple-element.17), channel_id=1, source_target_pairs={{0,4},{4,0},{8,12},{12,8},{1,5},{5,1},{9,13},{13,9},{2,6},{6,2},{1... | collective-permute-start | bytes 1179656 | tf_op jit(solution)/shard_map/ppermute | solution.py:20
  152.6 3.0 %collective-permute-start.8 = (bf16[256,768]{1,0:T(8,128)(2,1)}, bf16[256,768]{1,0:T(8,128)(2,1)S(1)}, u32[]{:S(2)}, u32[]{:S(2)}) collective-permute-start(bf16[256,768]{1,0:T(8,128)(2,1)} %get-tuple-element.18), channel_id=1, source_target_pairs={{0,8},{4,12},{8,0},{12,4},{1,9},{5,13},{9,1},{13,5},{2,10},{6,14},... | collective-permute-start | bytes 1179656 | tf_op jit(solution)/shard_map/ppermute | solution.py:20
  155.6 0.0 all-to-all-done.2
  155.6 0.0 copy-done
  155.6 0.4 fusion.3
  156.0 0.0 collective-permute-done.5
  156.0 3.9 %collective-permute-done.6 = bf16[256,768]{1,0:T(8,128)(2,1)S(1)} collective-permute-done((bf16[256,768]{1,0:T(8,128)(2,1)}, bf16[256,768]{1,0:T(8,128)(2,1)S(1)}, u32[]{:S(2)}, u32[]{:S(2)}) %collective-permute-start.6) | collective-permute-done | bytes 393248 | tf_op jit(solution)/shard_map/ppermute | solution.py:20
  160.0 4.0 %collective-permute-done.7 = bf16[256,768]{1,0:T(8,128)(2,1)S(1)} collective-permute-done((bf16[256,768]{1,0:T(8,128)(2,1)}, bf16[256,768]{1,0:T(8,128)(2,1)S(1)}, u32[]{:S(2)}, u32[]{:S(2)}) %collective-permute-start.7) | collective-permute-done | bytes 393248 | tf_op jit(solution)/shard_map/ppermute | solution.py:20
  163.9 7.5 %collective-permute-done.8 = bf16[256,768]{1,0:T(8,128)(2,1)S(1)} collective-permute-done((bf16[256,768]{1,0:T(8,128)(2,1)}, bf16[256,768]{1,0:T(8,128)(2,1)S(1)}, u32[]{:S(2)}, u32[]{:S(2)}) %collective-permute-start.8) | collective-permute-done | bytes 393248 | tf_op jit(solution)/shard_map/ppermute | solution.py:20
  171.4 0.0 copy-done.8
  171.4 0.3 add_convert_fusion
  171.7 29.8 %all_to_all.22 = bf16[16,16,768]{2,1,0:T(8,128)(2,1)S(1)} all-to-all(bf16[16,16,768]{2,1,0:T(8,128)(2,1)S(1)} %bitcast.26), channel_id=1, replica_groups=mesh['z'=16,'yl'=2,'x'=4,'yh'=2,'c'=2] {'z'}, dimensions={0} | all-to-all | bytes 786432 | tf_op jit(solution)/shard_map/all_to_all | solution.py:207
  201.5 0.1 convert_reduce_fusion
  201.6 0.6 reduce-precision_convert_fusion
  (6 shorter events, 0.1 us)
Async XLA Ops:
  0.0 155.6 %copy-start = (bf16[512,768]{1,0:T(8,128)(2,1)S(1)}, bf16[512,768]{1,0:T(8,128)(2,1)}, u32[]{:S(2)}) copy-start(bf16[512,768]{1,0:T(8,128)(2,1)} %param.13) | copy-start | bytes 2359300
  0.9 5.3 %copy-start.3 = (bf16[768,512]{1,0:T(8,128)(2,1)S(1)}, bf16[768,512]{1,0:T(8,128)(2,1)}, u32[]{:S(2)}) copy-start(bf16[768,512]{1,0:T(8,128)(2,1)} %w.1) | copy-start | bytes 2359300
  0.9 5.3 %copy-start.7 = (bf16[16,768]{1,0:T(8,128)(2,1)S(1)}, bf16[16,768]{1,0:T(8,128)(2,1)}, u32[]{:S(2)}) copy-start(bf16[16,768]{1,0:T(8,128)(2,1)} %x.3) | copy-start | bytes 73732
  2.5 113.0 %copy-start.2 = (bf16[1,96,5,768]{3,1,2,0:T(8,128)(2,1)S(1)}, bf16[1,96,5,768]{3,1,2,0:T(8,128)(2,1)}, u32[]{:S(2)}) copy-start(bf16[1,96,5,768]{3,1,2,0:T(8,128)(2,1)} %param.8) | copy-start | bytes 2211844
  2.5 113.0 %copy-start.4 = (bf16[1,96,512]{2,1,0:T(8,128)(2,1)S(1)}, bf16[1,96,512]{2,1,0:T(8,128)(2,1)}, u32[]{:S(2)}) copy-start(bf16[1,96,512]{2,1,0:T(8,128)(2,1)} %param.12) | copy-start | bytes 294916
  2.5 113.0 %copy-start.5 = (bf16[1,96,512]{2,1,0:T(8,128)(2,1)S(1)}, bf16[1,96,512]{2,1,0:T(8,128)(2,1)}, u32[]{:S(2)}) copy-start(bf16[1,96,512]{2,1,0:T(8,128)(2,1)} %param.11) | copy-start | bytes 294916
  2.5 113.0 %collective-permute-start.4 = (bf16[1152,768]{1,0:T(8,128)(2,1)S(1)}, bf16[1152,768]{1,0:T(8,128)(2,1)S(1)}, u32[]{:S(2)}, u32[]{:S(2)}) collective-permute-start(bf16[1152,768]{1,0:T(8,128)(2,1)S(1)} %fusion.1), channel_id=1, source_target_pairs={{0,16},{16,0},{1,17},{17,1},{2,18},{18,2},{3,19},{19,3},{4,20},{20... | collective-permute-start | bytes 5308424 | tf_op jit(solution)/shard_map/ppermute | solution.py:20
  89.0 10.8 %collective-permute-start = (bf16[256,768]{1,0:T(8,128)(2,1)S(1)}, bf16[256,768]{1,0:T(8,128)(2,1)S(1)}, u32[]{:S(2)}, u32[]{:S(2)}) collective-permute-start(bf16[256,768]{1,0:T(8,128)(2,1)S(1)} %slice.12), channel_id=1, source_target_pairs={{0,1},{1,0},{2,3},{3,2},{4,5},{5,4},{6,7},{7,6},{8,9},{9,8},{10,11... | collective-permute-start | bytes 1179656 | tf_op jit(solution)/shard_map/ppermute | solution.py:20
  91.0 14.9 %collective-permute-start.1 = (bf16[256,768]{1,0:T(8,128)(2,1)S(1)}, bf16[256,768]{1,0:T(8,128)(2,1)S(1)}, u32[]{:S(2)}, u32[]{:S(2)}) collective-permute-start(bf16[256,768]{1,0:T(8,128)(2,1)S(1)} %slice.12), channel_id=1, source_target_pairs={{0,2},{2,0},{1,3},{3,1},{4,6},{6,4},{5,7},{7,5},{8,10},{10,8},{9,1... | collective-permute-start | bytes 1179656 | tf_op jit(solution)/shard_map/ppermute | solution.py:20
  94.0 13.9 %collective-permute-start.2 = (bf16[256,768]{1,0:T(8,128)(2,1)S(1)}, bf16[256,768]{1,0:T(8,128)(2,1)S(1)}, u32[]{:S(2)}, u32[]{:S(2)}) collective-permute-start(bf16[256,768]{1,0:T(8,128)(2,1)S(1)} %slice.12), channel_id=1, source_target_pairs={{0,4},{4,0},{8,12},{12,8},{1,5},{5,1},{9,13},{13,9},{2,6},{6,2},{1... | collective-permute-start | bytes 1179656 | tf_op jit(solution)/shard_map/ppermute | solution.py:20
  96.8 18.7 %collective-permute-start.3 = (bf16[256,768]{1,0:T(8,128)(2,1)S(1)}, bf16[256,768]{1,0:T(8,128)(2,1)S(1)}, u32[]{:S(2)}, u32[]{:S(2)}) collective-permute-start(bf16[256,768]{1,0:T(8,128)(2,1)S(1)} %slice.12), channel_id=1, source_target_pairs={{0,8},{4,12},{8,0},{12,4},{1,9},{5,13},{9,1},{13,5},{2,10},{6,14},... | collective-permute-start | bytes 1179656 | tf_op jit(solution)/shard_map/ppermute | solution.py:20
  115.5 3.8 %copy-start.1 = (bf16[1152,768]{1,0:T(8,128)(2,1)}, bf16[1152,768]{1,0:T(8,128)(2,1)S(1)}, u32[]{:S(2)}) copy-start(bf16[1152,768]{1,0:T(8,128)(2,1)S(1)} %collective-permute-done.4.refs_8_.other_in) | copy-start | bytes 5308420
  119.4 13.8 %copy-start.6 = (bf16[256,192]{1,0:T(8,128)(2,1)}, bf16[256,192]{1,0:T(8,128)(2,1)S(1)}, u32[]{:S(2)}) copy-start(bf16[256,192]{1,0:T(8,128)(2,1)S(1)} %get-tuple-element.12.hidden_in) | copy-start | bytes 294916
  133.9 21.7 %all-to-all-start.2 = ((bf16[16,16,512]{2,1,0:T(8,128)(2,1)}), bf16[16,16,512]{2,1,0:T(8,128)(2,1)S(1)}, u32[]{:S(2)}, u32[]{:S(2)}) async-start(bf16[16,16,512]{2,1,0:T(8,128)(2,1)} %broadcast_in_dim.2), calls=%async_computation.2 | async-start | bytes 524288 | tf_op jit(solution)/shard_map/all_to_all | solution.py:33
  142.8 28.7 %copy-start.8 = (f32[256,768]{1,0:T(8,128)S(1)}, f32[256,768]{1,0:T(8,128)}, u32[]{:S(2)}) copy-start(f32[256,768]{1,0:T(8,128)} %get-tuple-element.13) | copy-start | bytes 2359300
  142.8 13.2 %collective-permute-start.5 = (bf16[256,768]{1,0:T(8,128)(2,1)}, bf16[256,768]{1,0:T(8,128)(2,1)S(1)}, u32[]{:S(2)}, u32[]{:S(2)}) collective-permute-start(bf16[256,768]{1,0:T(8,128)(2,1)} %get-tuple-element.15), channel_id=1, source_target_pairs={{0,1},{1,0},{2,3},{3,2},{4,5},{5,4},{6,7},{7,6},{8,9},{9,8},{10,11... | collective-permute-start | bytes 1179656 | tf_op jit(solution)/shard_map/ppermute | solution.py:20
  145.0 15.0 %collective-permute-start.6 = (bf16[256,768]{1,0:T(8,128)(2,1)}, bf16[256,768]{1,0:T(8,128)(2,1)S(1)}, u32[]{:S(2)}, u32[]{:S(2)}) collective-permute-start(bf16[256,768]{1,0:T(8,128)(2,1)} %get-tuple-element.16), channel_id=1, source_target_pairs={{0,2},{2,0},{1,3},{3,1},{4,6},{6,4},{5,7},{7,5},{8,10},{10,8},{9,1... | collective-permute-start | bytes 1179656 | tf_op jit(solution)/shard_map/ppermute | solution.py:20
  149.8 14.1 %collective-permute-start.7 = (bf16[256,768]{1,0:T(8,128)(2,1)}, bf16[256,768]{1,0:T(8,128)(2,1)S(1)}, u32[]{:S(2)}, u32[]{:S(2)}) collective-permute-start(bf16[256,768]{1,0:T(8,128)(2,1)} %get-tuple-element.17), channel_id=1, source_target_pairs={{0,4},{4,0},{8,12},{12,8},{1,5},{5,1},{9,13},{13,9},{2,6},{6,2},{1... | collective-permute-start | bytes 1179656 | tf_op jit(solution)/shard_map/ppermute | solution.py:20
  152.6 18.8 %collective-permute-start.8 = (bf16[256,768]{1,0:T(8,128)(2,1)}, bf16[256,768]{1,0:T(8,128)(2,1)S(1)}, u32[]{:S(2)}, u32[]{:S(2)}) collective-permute-start(bf16[256,768]{1,0:T(8,128)(2,1)} %get-tuple-element.18), channel_id=1, source_target_pairs={{0,8},{4,12},{8,0},{12,4},{1,9},{5,13},{9,1},{13,5},{2,10},{6,14},... | collective-permute-start | bytes 1179656 | tf_op jit(solution)/shard_map/ppermute | solution.py:20

commit v4 on v3

v4 whole, which is shorter than its diff:
```python
import functools

import jax
import jax.numpy as jnp
from jax import lax
from jax.experimental import pallas as pl
from jax.experimental.pallas import tpu as pltpu
from jax.sharding import Mesh, PartitionSpec as P


F32 = jnp.float32
BF16 = jnp.bfloat16
FEAT = ("x", "yh", "c")
NEAR = 3
UP_MIB = 24
DOWN_MIB = 24
LEVEL_AXES = (("c", 0), ("yh", 0), ("x", 0), ("x", 1))


def swap(array, axis, bit):
    return lax.ppermute(array, axis, [(i, i ^ (1 << bit)) for i in range(lax.axis_size(axis))])


def dot_nt(a, b):
    return lax.dot_general(a, b, (((1,), (1,)), ((), ())), preferred_element_type=F32)


def dot_nn(a, b):
    return lax.dot_general(a, b, (((1,), (0,)), ((), ())), preferred_element_type=F32)


def share(array, axis):
    n = lax.axis_size(axis)
    return lax.all_to_all(jnp.broadcast_to(array[None], (n,) + array.shape), axis, 0, 0, tiled=True)


def total_of(stack):
    return lax.reduce_precision(jnp.sum(stack.astype(F32), axis=0), 8, 7).astype(BF16)


def sum_over_feat(part, n):
    part = lax.all_to_all(part.reshape((n, part.shape[0] // n) + part.shape[1:]), FEAT, 0, 0, tiled=True)
    group = total_of(part)
    whole = share(group, FEAT)
    return whole.reshape((-1,) + group.shape[1:])


def fetch(src, dst, sem, lo, size):
    part = pl.ds(lo, size)
    return pltpu.make_async_copy(src.at[part], dst.at[part], sem)


def pair(mine, other, rows, base, k):
    lo = base + k * rows
    return jnp.concatenate([ref[lo : lo + rows, :] for ref in (mine, other)], axis=0)


def up_body(kinds, rows, rank, *refs):
    n = kinds * rows
    count = kinds + 2
    ins, (hidden_out, back_out) = refs[:count], refs[count : count + 2]
    bufs, (staged, back, sems, out_sems) = refs[count + 2 : -4], refs[-4:]
    xs, (mine, other) = bufs[:kinds], bufs[kinds:]
    db = mine.shape[1]
    head = db - rank

    def whole(i):
        return fetch(ins[i], bufs[i], sems.at[i], 0, ins[i].shape[0])

    first = [whole(0)]
    for i in (kinds, kinds + 1):
        first.append(fetch(ins[i], bufs[i], sems.at[i], 2 * n, 2 * rows))
        first.append(fetch(ins[i], bufs[i], sems.at[i + 2], 0, n))
    partners = [whole(i) for i in range(1, kinds)]
    for copy in first + partners:
        copy.start()
    for copy in first:
        copy.wait()

    def both(lo, hi, at, size):
        return jnp.concatenate([ref[lo:hi, at : at + size] for ref in (mine, other)], axis=0)

    pre = dot_nt(xs[0][:, db:], both(2 * n, 2 * n + rows, 0, rank))
    pre = pre + dot_nt(xs[0][:, :db], pair(mine, other, rows, 0, 0))
    for k in range(1, kinds):
        partners[k - 1].wait()
        pre = pre + dot_nt(xs[k][...], pair(mine, other, rows, 0, k))
    hidden = (0.5 * pre * (1.0 + lax.erf(pre * (0.5**0.5)))).astype(BF16)
    staged[...] = hidden
    stores = [pltpu.make_async_copy(staged, hidden_out, out_sems.at[0])]
    stores[0].start()
    back[:, :head] = dot_nn(hidden, both(2 * n, 2 * n + rows, rank, head)).astype(BF16)
    back[:, head:] = dot_nn(hidden, both(2 * n + rows, 2 * n + 2 * rows, 0, rank - head)).astype(BF16)
    stores.append(pltpu.make_async_copy(back, back_out, out_sems.at[1]))
    stores[1].start()
    for copy in stores:
        copy.wait()


def up_call(gathered, pieces, mine, other, kinds):
    count, width = gathered.shape
    db = mine.shape[1]
    rank = width - db
    rows = mine.shape[0] // (2 * kinds + 2)
    args = (gathered, *pieces, mine, other)
    return pl.pallas_call(
        functools.partial(up_body, kinds, rows, rank),
        out_shape=[pltpu.HBM((count, 2 * rows), BF16), pltpu.HBM((count, rank), BF16)],
        in_specs=[pl.BlockSpec(memory_space=pl.ANY)] * len(args),
        scratch_shapes=[pltpu.VMEM(a.shape, BF16) for a in args]
        + [pltpu.VMEM((count, 2 * rows), BF16), pltpu.VMEM((count, rank), BF16)]
        + [pltpu.SemaphoreType.DMA((len(args) + 2,)), pltpu.SemaphoreType.DMA((2,))],
        compiler_params=pltpu.CompilerParams(vmem_limit_bytes=UP_MIB * 2**20),
        name="ffn_up",
    )(*args)


def down_body(kinds, near, rows, hidden_in, *refs):
    n = kinds * rows
    far = kinds - near
    far_in, (mine_in, other_in), refs = refs[:far], refs[far : far + 2], refs[far + 2 :]
    outs, refs = refs[:near], refs[near:]
    (hidden, *far_hidden), (mine, other), refs = refs[: far + 1], refs[far + 1 : far + 3], refs[far + 3 :]
    stage, (in_sems, out_sems) = refs[:near], refs[near:]
    given = [
        fetch(src, dst, in_sems.at[2 * kinds + i], 0, dst.shape[0])
        for i, (src, dst) in enumerate(zip((hidden_in, *far_in), (hidden, *far_hidden)))
    ]
    loads = {}
    given[0].start()
    for k in (*range(near - 1, -1, -1), *range(near, kinds)):
        loads[k] = (
            fetch(mine_in, mine, in_sems.at[2 * k], n + k * rows, rows),
            fetch(other_in, other, in_sems.at[2 * k + 1], n + k * rows, rows),
        )
        for copy in loads[k]:
            copy.start()
    for copy in given[1:]:
        copy.start()
    given[0].wait()
    stores = []
    for k in range(near - 1, -1, -1):
        for copy in loads[k]:
            copy.wait()
        part = dot_nn(hidden[...], pair(mine, other, rows, n, k))
        if k == 0:
            for i in range(far):
                given[i + 1].wait()
                for copy in loads[near + i]:
                    copy.wait()
                part = part + dot_nn(far_hidden[i][...], pair(mine, other, rows, n, near + i))
        stage[k][...] = part.astype(outs[k].dtype)
        stores.append(pltpu.make_async_copy(stage[k], outs[k], out_sems.at[k]))
        stores[-1].start()
    for copy in stores:
        copy.wait()


def down_call(hidden, far_hidden, mine, other, kinds):
    count, db = hidden.shape[0], mine.shape[1]
    rows = hidden.shape[1] // 2
    near = kinds - len(far_hidden)
    kept = [((count, db), F32)] + [((count, db), BF16)] * (near - 1)
    args = (hidden, *far_hidden, mine, other)
    return pl.pallas_call(
        functools.partial(down_body, kinds, near, rows),
        out_shape=[pltpu.HBM(*a) for a in kept],
        in_specs=[pl.BlockSpec(memory_space=pl.ANY)] * len(args),
        scratch_shapes=[pltpu.VMEM(a.shape, BF16) for a in args]
        + [pltpu.VMEM(*a) for a in kept]
        + [pltpu.SemaphoreType.DMA((2 * kinds + 1 + len(far_hidden),)), pltpu.SemaphoreType.DMA((near,))],
        compiler_params=pltpu.CompilerParams(vmem_limit_bytes=DOWN_MIB * 2**20),
        name="ffn_down",
    )(*args)


def pack_body(near_rows, rank, up, down, *refs):
    far, (right, left), out, sems = refs[:-4], refs[-4:-2], refs[-2], refs[-1]
    n, db = up.shape
    rows = right.shape[0]
    head = db - rank
    moves = [
        (up, out.at[pl.ds(0, n)]),
        (down.at[pl.ds(0, near_rows)], out.at[pl.ds(n, near_rows)]),
        (right, out.at[pl.ds(2 * n, rows), pl.ds(0, rank)]),
        (left.at[:, pl.ds(0, head)], out.at[pl.ds(2 * n, rows), pl.ds(rank, head)]),
        (left.at[:, pl.ds(head, rank - head)], out.at[pl.ds(2 * n + rows, rows), pl.ds(0, rank - head)]),
    ]
    moves += [(piece, out.at[pl.ds(n + near_rows + i * rows, rows)]) for i, piece in enumerate(far)]
    copies = [pltpu.make_async_copy(src, dst, sems.at[i]) for i, (src, dst) in enumerate(moves)]
    for copy in copies:
        copy.start()
    for copy in copies:
        copy.wait()


def pack_call(up, down, far, right, left):
    (n, db), (rows, rank) = up.shape, right.shape
    near_rows = n - len(far) * rows
    args = (up, down, *far, right, left)
    return pl.pallas_call(
        functools.partial(pack_body, near_rows, rank),
        out_shape=pltpu.HBM((2 * n + 2 * rows, db), BF16),
        in_specs=[pl.BlockSpec(memory_space=pl.ANY)] * len(args),
        scratch_shapes=[pltpu.SemaphoreType.DMA((5 + len(far),))],
        compiler_params=pltpu.CompilerParams(vmem_limit_bytes=60 * 2**20),
        name="pack",
    )(*args)


def code_body(x, w, stack):
    part = dot_nn(x[...], w[...]).astype(BF16)
    for i in range(stack.shape[0]):
        stack[i] = part


def code_call(tokens, up_left, n):
    shape = jax.ShapeDtypeStruct((n, tokens.shape[0], up_left.shape[1]), BF16)
    return pl.pallas_call(code_body, out_shape=shape, name="code_part", compiler_params=pltpu.CompilerParams(vmem_limit_bytes=60 * 2**20))(tokens, up_left)


def per_device(tokens, up_weight, down_weight, up_left, up_right, down_left, down_right):
    nz, nf = lax.axis_size("z"), lax.axis_size(FEAT)
    count, db = tokens.shape
    rows, _ = up_right.shape[1:]
    kinds = up_weight.shape[2]
    up = up_weight[0].transpose(1, 0, 2).reshape(kinds * rows, db)
    down = down_weight[0].transpose(1, 0, 2).reshape(kinds * rows, db)

    far = []
    for k in range(NEAR, kinds):
        axis, bit = LEVEL_AXES[k - 1]
        far.append(swap(down[k * rows : (k + 1) * rows], axis, bit))

    packed = pack_call(up, down, far, up_right[0], down_left[0])
    stack = code_call(tokens, up_left, nf)
    stack = lax.all_to_all(stack, FEAT, 0, 0, tiled=True)
    other = swap(packed, "yl", 0)
    mine = jnp.concatenate([tokens, total_of(stack)], axis=1)
    gathered = lax.all_gather(mine, "z", axis=0, tiled=True)
    own = gathered[:, :db]
    pieces = []
    for axis, bit in LEVEL_AXES:
        pieces.append(swap(own, axis, bit))

    hidden, back = up_call(gathered, pieces, packed, other, kinds)
    back = sum_over_feat(back, nf)
    far_hidden = []
    for axis, bit in LEVEL_AXES[NEAR - 1 :]:
        far_hidden.append(swap(hidden, axis, bit))
    own_total, *terms = down_call(hidden, far_hidden, packed, other, kinds)
    sent = []
    for part, (axis, bit) in zip(terms, LEVEL_AXES):
        sent.append(swap(part, axis, bit))
    total = own_total + dot_nn(back, down_right)
    for s in sent:
        total = total + s.astype(F32)
    total = total.astype(BF16)
    total = lax.all_to_all(total.reshape(nz, count, db), "z", 0, 0, tiled=True)
    return total_of(total)


def solution(mesh):
    tok, feat = ("z", "yl"), FEAT
    inner = Mesh(mesh.devices.reshape(16, 2, 4, 2, 2), tok + feat)
    return jax.shard_map(
        per_device,
        mesh=inner,
        in_specs=(
            P(tok, feat),
            P(feat, tok, None, None),
            P(feat, tok, None, None),
            P(feat, None),
            P(feat, tok, None),
            P(feat, tok, None),
            P(None, feat),
        ),
        out_specs=P(tok, feat),
        check_vma=False,
    )
```

time: 204 us -> 210 us (1.029)
  starting transfers between devices: 32.5 us -> 42.4 us
  waiting for transfers between devices: 31.1 us -> 24.5 us
  Pallas kernels: 7.53 us -> 13.8 us
  blocking collectives: 126 us -> 122 us
    ppermute x9 -> x11, starting transfers between devices: 27.2 us -> 37.1 us  [swap(): lax.ppermute(array, axis, [(i, i ^ 1 << bit) for i in range(lax.axis_size...]
    ppermute x9 -> x11, waiting for transfers between devices: 31.1 us -> 24.5 us  [swap(): lax.ppermute(array, axis, [(i, i ^ 1 << bit) for i in range(lax.axis_size...]
    pallas_call x2 -> x3, Pallas kernels: 7.3 us -> 11.7 us  [the longest x1 4.65 us: up_call(): pl.pallas_call(functools.partial(up_body, kinds, rows, rank), out_shape=[...]
    all_to_all x1, blocking collectives: 43.6 us -> 39.3 us  [per_device(): stack = lax.all_to_all(stack, FEAT, 0, 0, tiled=True)]
  transfers between devices with their start and end apart: 10 -> 12, of which waited for: 6 -> 6; matrix products, arithmetic and copies ran while one was open for 0% -> 0% of each run, Pallas kernels for 2% -> 3%
where the time goes in v4:
time: 210 us; the launch traced here: 208 us
  blocking collectives  122 us (58%)
  starting transfers between devices  42.4 us (20%)
  waiting for transfers between devices  24.5 us (12%)
  Pallas kernels  13.8 us (7%)
  local copies, waits for them, and re-layouts  3.42 us (2%)
    all_to_all x1, blocking collectives, per_device(): stack = lax.all_to_all(stack, FEAT, 0, 0, tiled=True)  39.3 us
    all_gather x1, blocking collectives, per_device(): gathered = lax.all_gather(mine, 'z', axis=0, tiled=True)  38.9 us
    ppermute x11, starting transfers between devices, swap(): lax.ppermute(array, axis, [(i, i ^ 1 << bit) for i in range(lax.axis_size...  37.1 us
    all_to_all x1, blocking collectives, per_device(): total = lax.all_to_all(total.reshape(nz, count, db), 'z', 0, 0, tiled=True)  30 us
    ppermute x11, waiting for transfers between devices, swap(): lax.ppermute(array, axis, [(i, i ^ 1 << bit) for i in range(lax.axis_size...  24.5 us
    all_to_all x1, blocking collectives, sum_over_feat(): lax.all_to_all(part.reshape((n, part.shape[0] // n) + part.shape[1:]), FE...  13.9 us
    all_to_all x1, starting transfers between devices, share(): lax.all_to_all(jnp.broadcast_to(array[None], (n,) + array.shape), axis, 0...  5.34 us
    pallas_call x1, Pallas kernels, up_call(): pl.pallas_call(functools.partial(up_body, kinds, rows, rank), out_shape=[...  4.65 us
  transfers between devices with their start and end apart: 12, of which 6 were waited for; matrix products, arithmetic and copies ran while one was open for 0% of the time, Pallas kernels for 3%

profile of v4, /device:TPU:6, one launch (start us, length us, event | category | flops | bytes accessed | tf_op | source)
XLA Modules:
  0.0 207.8 jit_solution(2612755124796796727)
XLA Ops:
  0.0 0.0 copy-start
  0.0 1.1 slice_bitcast_fusion
  1.1 3.3 %collective-permute-start.5 = (bf16[96,768]{1,0:T(8,128)(2,1)S(1)}, bf16[96,768]{1,0:T(8,128)(2,1)S(1)}, u32[]{:S(2)}, u32[]{:S(2)}) collective-permute-start(bf16[96,768]{1,0:T(8,128)(2,1)S(1)} %get-tuple-element.15), channel_id=1, source_target_pairs={{0,8},{4,12},{8,0},{12,4},{1,9},{5,13},{9,1},{13,5},{2,10},{6,14},... | collective-permute-start | bytes 442376 | tf_op jit(solution)/shard_map/ppermute | solution.py:21
  4.4 7.2 %collective-permute-start.4 = (bf16[96,768]{1,0:T(8,128)(2,1)S(1)}, bf16[96,768]{1,0:T(8,128)(2,1)S(1)}, u32[]{:S(2)}, u32[]{:S(2)}) collective-permute-start(bf16[96,768]{1,0:T(8,128)(2,1)S(1)} %get-tuple-element.16), channel_id=1, source_target_pairs={{0,4},{4,0},{8,12},{12,8},{1,5},{5,1},{9,13},{13,9},{2,6},{6,2},{1... | collective-permute-start | bytes 442376 | tf_op jit(solution)/shard_map/ppermute | solution.py:21
  11.6 0.0 collective-permute-done.5.refs_1_
  11.6 0.0 copy-start.4
  11.6 3.1 %collective-permute-done.4.refs_0_ = bf16[96,768]{1,0:T(8,128)(2,1)S(1)} collective-permute-done((bf16[96,768]{1,0:T(8,128)(2,1)S(1)}, bf16[96,768]{1,0:T(8,128)(2,1)S(1)}, u32[]{:S(2)}, u32[]{:S(2)}) %collective-permute-start.4) | collective-permute-done | bytes 147488 | tf_op jit(solution)/shard_map/ppermute | solution.py:21
  14.7 0.0 copy-start.5
  14.7 0.0 copy-done.4
  14.7 0.7 copy-done.5
  15.4 2.6 %pack.1.refs_5_.refs_2_ = bf16[1152,768]{1,0:T(8,128)(2,1)} custom-call(bf16[480,768]{1,0:T(8,128)(2,1)} %bitcast.25, bf16[480,768]{1,0:T(8,128)(2,1)} %bitcast.23, bf16[96,768]{1,0:T(8,128)(2,1)} %copy-done.5, bf16[96,768]{1,0:T(8,128)(2,1)} %copy-done.4, bf16[96,512]{1,0:T(8,128)(2,1)} %bitcast.27, bf16[96,512]{1,0:T(8,128)(2,1)} %bitcast.28), custom_call_target="tpu_custom_call" | custom-call | tf_op jit(solution)/shard_map/pack/pallas_call | solution.py:201
  18.0 0.0 copy-start.6
  18.0 0.0 copy-start.1
  18.0 2.1 collective-permute-start.6
  20.1 2.1 %code_part.1 = bf16[16,16,512]{2,1,0:T(8,128)(2,1)} custom-call(bf16[16,768]{1,0:T(8,128)(2,1)} %x.1, bf16[768,512]{1,0:T(8,128)(2,1)} %w.1), custom_call_target="tpu_custom_call" | custom-call | tf_op jit(solution)/shard_map/code_part/pallas_call | solution.py:219
  22.2 39.3 %all_to_all.20 = bf16[16,16,512]{2,1,0:T(8,128)(2,1)S(1)} all-to-all(bf16[16,16,512]{2,1,0:T(8,128)(2,1)} %code_part.1), channel_id=1, replica_groups=mesh['z'=16,'yl'=2,'x'=4,'yh'=2,'c'=2] {'x','yh','c'}, dimensions={0} | all-to-all | bytes 524288 | tf_op jit(solution)/shard_map/all_to_all | solution.py:237
  61.5 0.0 copy-done.6
  61.6 38.9 %all_gather.3.refs_0_ = bf16[256,1280]{1,0:T(8,128)(2,1)S(1)} all-gather(bf16[16,1280]{1,0:T(8,128)(2,1)S(1)} %pad_maximum_fusion), channel_id=1, replica_groups=mesh['z'=16,'yl'=2,'x'=4,'yh'=2,'c'=2] {'z'}, dimensions={0}, use_global_device_ids=true | all-gather | bytes 696320 | tf_op jit(solution)/shard_map/all_gather | solution.py:240
  100.5 5.4 %collective-permute-start.3 = (bf16[256,768]{1,0:T(8,128)(2,1)S(1)}, bf16[256,768]{1,0:T(8,128)(2,1)S(1)}, u32[]{:S(2)}, u32[]{:S(2)}) collective-permute-start(bf16[256,768]{1,0:T(8,128)(2,1)S(1)} %slice.20), channel_id=1, source_target_pairs={{0,8},{4,12},{8,0},{12,4},{1,9},{5,13},{9,1},{13,5},{2,10},{6,14},... | collective-permute-start | bytes 1179656 | tf_op jit(solution)/shard_map/ppermute | solution.py:21
  106.0 1.9 collective-permute-start.2
  107.9 3.1 %collective-permute-start.1 = (bf16[256,768]{1,0:T(8,128)(2,1)S(1)}, bf16[256,768]{1,0:T(8,128)(2,1)S(1)}, u32[]{:S(2)}, u32[]{:S(2)}) collective-permute-start(bf16[256,768]{1,0:T(8,128)(2,1)S(1)} %slice.20), channel_id=1, source_target_pairs={{0,2},{2,0},{1,3},{3,1},{4,6},{6,4},{5,7},{7,5},{8,10},{10,8},{9,1... | collective-permute-start | bytes 1179656 | tf_op jit(solution)/shard_map/ppermute | solution.py:21
  111.0 1.9 collective-permute-start
  112.9 0.0 collective-permute-done.3.refs_4_
  112.9 3.5 %collective-permute-done.2.refs_3_ = bf16[256,768]{1,0:T(8,128)(2,1)S(1)} collective-permute-done((bf16[256,768]{1,0:T(8,128)(2,1)S(1)}, bf16[256,768]{1,0:T(8,128)(2,1)S(1)}, u32[]{:S(2)}, u32[]{:S(2)}) %collective-permute-start.2) | collective-permute-done | bytes 393248 | tf_op jit(solution)/shard_map/ppermute | solution.py:21
  116.4 2.7 %collective-permute-done.1.refs_2_ = bf16[256,768]{1,0:T(8,128)(2,1)S(1)} collective-permute-done((bf16[256,768]{1,0:T(8,128)(2,1)S(1)}, bf16[256,768]{1,0:T(8,128)(2,1)S(1)}, u32[]{:S(2)}, u32[]{:S(2)}) %collective-permute-start.1) | collective-permute-done | bytes 393248 | tf_op jit(solution)/shard_map/ppermute | solution.py:21
  119.1 0.0 collective-permute-done.refs_1_
  119.1 0.0 collective-permute-done.6.refs_6_.refs_3_
  119.1 0.0 copy-done.1
  119.1 4.6 %ffn_up.1 = (bf16[256,192]{1,0:T(8,128)(2,1)}, bf16[256,512]{1,0:T(8,128)(2,1)}) custom-call(bf16[256,1280]{1,0:T(8,128)(2,1)S(1)} %all_gather.3.refs_0_, bf16[256,768]{1,0:T(8,128)(2,1)S(1)} %collective-permute-done.refs_1_, bf16[256,768]{1,0:T(8,128)(2,1)S(1)} %collective-permute-done.1.refs_2_, bf16[256,768]{1,0:T(8,128)(2,1)S(1)} %collective-permute-done.2.refs_3_, ...), custom_call_target="tpu_custom_call" | custom-call | tf_op jit(solution)/shard_map/ffn_up/pallas_call | solution.py:106
  123.8 13.9 %all_to_all.21 = bf16[16,16,512]{2,1,0:T(8,128)(2,1)S(1)} all-to-all(bf16[16,16,512]{2,1,0:T(8,128)(2,1)} %bitcast.26), channel_id=1, replica_groups=mesh['z'=16,'yl'=2,'x'=4,'yh'=2,'c'=2] {'x','yh','c'}, dimensions={0} | all-to-all | bytes 524288 | tf_op jit(solution)/shard_map/all_to_all | solution.py:42
  137.7 0.7 broadcast_in_dim.2
  138.4 5.3 %all-to-all-start.2 = ((bf16[16,16,512]{2,1,0:T(8,128)(2,1)}), bf16[16,16,512]{2,1,0:T(8,128)(2,1)S(1)}, u32[]{:S(2)}, u32[]{:S(2)}) async-start(bf16[16,16,512]{2,1,0:T(8,128)(2,1)} %broadcast_in_dim.2), calls=%async_computation.2 | async-start | bytes 524288 | tf_op jit(solution)/shard_map/all_to_all | solution.py:34
  143.8 3.3 %collective-permute-start.8 = (bf16[256,192]{1,0:T(8,128)(2,1)}, bf16[256,192]{1,0:T(8,128)(2,1)S(1)}, u32[]{:S(2)}, u32[]{:S(2)}) collective-permute-start(bf16[256,192]{1,0:T(8,128)(2,1)} %get-tuple-element.10.hidden_in), channel_id=1, source_target_pairs={{0,8},{4,12},{8,0},{12,4},{1,9},{5,13},{9,1},{13,5},{2,10},{6,14},... | collective-permute-start | bytes 294920 | tf_op jit(solution)/shard_map/ppermute | solution.py:21
  147.1 1.9 collective-permute-start.7
  149.0 3.9 %collective-permute-done.8.refs_1_ = bf16[256,192]{1,0:T(8,128)(2,1)S(1)} collective-permute-done((bf16[256,192]{1,0:T(8,128)(2,1)}, bf16[256,192]{1,0:T(8,128)(2,1)S(1)}, u32[]{:S(2)}, u32[]{:S(2)}) %collective-permute-start.8) | collective-permute-done | bytes 98336 | tf_op jit(solution)/shard_map/ppermute | solution.py:21
  152.9 1.5 collective-permute-done.7.refs_0_
  154.4 0.0 copy-start.2
  154.4 0.9 copy-done.2
  155.3 4.4 %ffn_down.1 = (f32[256,768]{1,0:T(8,128)}, bf16[256,768]{1,0:T(8,128)(2,1)}, bf16[256,768]{1,0:T(8,128)(2,1)}) custom-call(bf16[256,192]{1,0:T(8,128)(2,1)S(1)} %copy-done.2, bf16[256,192]{1,0:T(8,128)(2,1)S(1)} %collective-permute-done.7.refs_0_, bf16[256,192]{1,0:T(8,128)(2,1)S(1)} %collective-permute-done.8.refs_1_, bf16[1152,768]{1,0:T(8,128)(2,1)S(1)} %copy-done.1, ...), custom_call_target="tpu_custom_call" | custom-call | tf_op jit(solution)/shard_map/ffn_down/pallas_call | solution.py:165
  159.7 0.0 copy-start.3
  159.7 2.1 collective-permute-start.9
  161.8 4.9 %collective-permute-start.10 = (bf16[256,768]{1,0:T(8,128)(2,1)}, bf16[256,768]{1,0:T(8,128)(2,1)S(1)}, u32[]{:S(2)}, u32[]{:S(2)}) collective-permute-start(bf16[256,768]{1,0:T(8,128)(2,1)} %get-tuple-element.14), channel_id=1, source_target_pairs={{0,2},{2,0},{1,3},{3,1},{4,6},{6,4},{5,7},{7,5},{8,10},{10,8},{9,1... | collective-permute-start | bytes 1179656 | tf_op jit(solution)/shard_map/ppermute | solution.py:21
  166.7 0.0 all-to-all-done.2
  166.7 0.0 copy-done
  166.7 0.4 fusion
  167.1 0.0 collective-permute-done.9
  167.1 9.8 %collective-permute-done.10 = bf16[256,768]{1,0:T(8,128)(2,1)S(1)} collective-permute-done((bf16[256,768]{1,0:T(8,128)(2,1)}, bf16[256,768]{1,0:T(8,128)(2,1)S(1)}, u32[]{:S(2)}, u32[]{:S(2)}) %collective-permute-start.10) | collective-permute-done | bytes 393248 | tf_op jit(solution)/shard_map/ppermute | solution.py:21
  176.9 0.0 copy-done.3
  176.9 0.1 add_convert_fusion
  177.1 30.0 %all_to_all.22 = bf16[16,16,768]{2,1,0:T(8,128)(2,1)S(1)} all-to-all(bf16[16,16,768]{2,1,0:T(8,128)(2,1)S(1)} %bitcast.21), channel_id=1, replica_groups=mesh['z'=16,'yl'=2,'x'=4,'yh'=2,'c'=2] {'z'}, dimensions={0} | all-to-all | bytes 786432 | tf_op jit(solution)/shard_map/all_to_all | solution.py:259
  207.1 0.1 convert_reduce_fusion
  207.1 0.6 reduce-precision_convert_fusion
  (6 shorter events, 0.1 us)
Async XLA Ops:
  0.0 166.7 %copy-start = (bf16[512,768]{1,0:T(8,128)(2,1)S(1)}, bf16[512,768]{1,0:T(8,128)(2,1)}, u32[]{:S(2)}) copy-start(bf16[512,768]{1,0:T(8,128)(2,1)} %param.13) | copy-start | bytes 2359300
  1.1 10.5 %collective-permute-start.5 = (bf16[96,768]{1,0:T(8,128)(2,1)S(1)}, bf16[96,768]{1,0:T(8,128)(2,1)S(1)}, u32[]{:S(2)}, u32[]{:S(2)}) collective-permute-start(bf16[96,768]{1,0:T(8,128)(2,1)S(1)} %get-tuple-element.15), channel_id=1, source_target_pairs={{0,8},{4,12},{8,0},{12,4},{1,9},{5,13},{9,1},{13,5},{2,10},{6,14},... | collective-permute-start | bytes 442376 | tf_op jit(solution)/shard_map/ppermute | solution.py:21
  4.4 10.3 %collective-permute-start.4 = (bf16[96,768]{1,0:T(8,128)(2,1)S(1)}, bf16[96,768]{1,0:T(8,128)(2,1)S(1)}, u32[]{:S(2)}, u32[]{:S(2)}) collective-permute-start(bf16[96,768]{1,0:T(8,128)(2,1)S(1)} %get-tuple-element.16), channel_id=1, source_target_pairs={{0,4},{4,0},{8,12},{12,8},{1,5},{5,1},{9,13},{13,9},{2,6},{6,2},{1... | collective-permute-start | bytes 442376 | tf_op jit(solution)/shard_map/ppermute | solution.py:21
  11.6 3.1 %copy-start.4 = (bf16[96,768]{1,0:T(8,128)(2,1)}, bf16[96,768]{1,0:T(8,128)(2,1)S(1)}, u32[]{:S(2)}) copy-start(bf16[96,768]{1,0:T(8,128)(2,1)S(1)} %collective-permute-done.5.refs_1_) | copy-start | bytes 442372
  14.7 0.7 copy-start.5
  18.0 43.5 %copy-start.6 = (bf16[16,768]{1,0:T(8,128)(2,1)S(1)}, bf16[16,768]{1,0:T(8,128)(2,1)}, u32[]{:S(2)}) copy-start(bf16[16,768]{1,0:T(8,128)(2,1)} %x.1) | copy-start | bytes 73732
  18.0 101.1 %copy-start.1 = (bf16[1152,768]{1,0:T(8,128)(2,1)S(1)}, bf16[1152,768]{1,0:T(8,128)(2,1)}, u32[]{:S(2)}) copy-start(bf16[1152,768]{1,0:T(8,128)(2,1)} %pack.1.refs_5_.refs_2_) | copy-start | bytes 5308420
  18.0 101.1 %collective-permute-start.6 = (bf16[1152,768]{1,0:T(8,128)(2,1)}, bf16[1152,768]{1,0:T(8,128)(2,1)}, u32[]{:S(2)}, u32[]{:S(2)}) collective-permute-start(bf16[1152,768]{1,0:T(8,128)(2,1)} %pack.1.refs_5_.refs_2_), channel_id=1, source_target_pairs={{0,16},{16,0},{1,17},{17,1},{2,18},{18,2},{3,19},{19,3},{4,20},{20... | collective-permute-start | bytes 5308424 | tf_op jit(solution)/shard_map/ppermute | solution.py:21
  100.5 12.4 %collective-permute-start.3 = (bf16[256,768]{1,0:T(8,128)(2,1)S(1)}, bf16[256,768]{1,0:T(8,128)(2,1)S(1)}, u32[]{:S(2)}, u32[]{:S(2)}) collective-permute-start(bf16[256,768]{1,0:T(8,128)(2,1)S(1)} %slice.20), channel_id=1, source_target_pairs={{0,8},{4,12},{8,0},{12,4},{1,9},{5,13},{9,1},{13,5},{2,10},{6,14},... | collective-permute-start | bytes 1179656 | tf_op jit(solution)/shard_map/ppermute | solution.py:21
  106.0 10.4 %collective-permute-start.2 = (bf16[256,768]{1,0:T(8,128)(2,1)S(1)}, bf16[256,768]{1,0:T(8,128)(2,1)S(1)}, u32[]{:S(2)}, u32[]{:S(2)}) collective-permute-start(bf16[256,768]{1,0:T(8,128)(2,1)S(1)} %slice.20), channel_id=1, source_target_pairs={{0,4},{4,0},{8,12},{12,8},{1,5},{5,1},{9,13},{13,9},{2,6},{6,2},{1... | collective-permute-start | bytes 1179656 | tf_op jit(solution)/shard_map/ppermute | solution.py:21
  107.9 11.2 %collective-permute-start.1 = (bf16[256,768]{1,0:T(8,128)(2,1)S(1)}, bf16[256,768]{1,0:T(8,128)(2,1)S(1)}, u32[]{:S(2)}, u32[]{:S(2)}) collective-permute-start(bf16[256,768]{1,0:T(8,128)(2,1)S(1)} %slice.20), channel_id=1, source_target_pairs={{0,2},{2,0},{1,3},{3,1},{4,6},{6,4},{5,7},{7,5},{8,10},{10,8},{9,1... | collective-permute-start | bytes 1179656 | tf_op jit(solution)/shard_map/ppermute | solution.py:21
  111.0 8.1 %collective-permute-start = (bf16[256,768]{1,0:T(8,128)(2,1)S(1)}, bf16[256,768]{1,0:T(8,128)(2,1)S(1)}, u32[]{:S(2)}, u32[]{:S(2)}) collective-permute-start(bf16[256,768]{1,0:T(8,128)(2,1)S(1)} %slice.20), channel_id=1, source_target_pairs={{0,1},{1,0},{2,3},{3,2},{4,5},{5,4},{6,7},{7,6},{8,9},{9,8},{10,11... | collective-permute-start | bytes 1179656 | tf_op jit(solution)/shard_map/ppermute | solution.py:21
  138.4 28.3 %all-to-all-start.2 = ((bf16[16,16,512]{2,1,0:T(8,128)(2,1)}), bf16[16,16,512]{2,1,0:T(8,128)(2,1)S(1)}, u32[]{:S(2)}, u32[]{:S(2)}) async-start(bf16[16,16,512]{2,1,0:T(8,128)(2,1)} %broadcast_in_dim.2), calls=%async_computation.2 | async-start | bytes 524288 | tf_op jit(solution)/shard_map/all_to_all | solution.py:34
  143.8 9.1 %collective-permute-start.8 = (bf16[256,192]{1,0:T(8,128)(2,1)}, bf16[256,192]{1,0:T(8,128)(2,1)S(1)}, u32[]{:S(2)}, u32[]{:S(2)}) collective-permute-start(bf16[256,192]{1,0:T(8,128)(2,1)} %get-tuple-element.10.hidden_in), channel_id=1, source_target_pairs={{0,8},{4,12},{8,0},{12,4},{1,9},{5,13},{9,1},{13,5},{2,10},{6,14},... | collective-permute-start | bytes 294920 | tf_op jit(solution)/shard_map/ppermute | solution.py:21
  147.1 7.3 %collective-permute-start.7 = (bf16[256,192]{1,0:T(8,128)(2,1)}, bf16[256,192]{1,0:T(8,128)(2,1)S(1)}, u32[]{:S(2)}, u32[]{:S(2)}) collective-permute-start(bf16[256,192]{1,0:T(8,128)(2,1)} %get-tuple-element.10.hidden_in), channel_id=1, source_target_pairs={{0,4},{4,0},{8,12},{12,8},{1,5},{5,1},{9,13},{13,9},{2,6},{6,2},{1... | collective-permute-start | bytes 294920 | tf_op jit(solution)/shard_map/ppermute | solution.py:21
  154.4 0.9 copy-start.2
  159.7 17.2 %copy-start.3 = (f32[256,768]{1,0:T(8,128)S(1)}, f32[256,768]{1,0:T(8,128)}, u32[]{:S(2)}) copy-start(f32[256,768]{1,0:T(8,128)} %get-tuple-element.11) | copy-start | bytes 2359300
  159.7 7.3 %collective-permute-start.9 = (bf16[256,768]{1,0:T(8,128)(2,1)}, bf16[256,768]{1,0:T(8,128)(2,1)S(1)}, u32[]{:S(2)}, u32[]{:S(2)}) collective-permute-start(bf16[256,768]{1,0:T(8,128)(2,1)} %get-tuple-element.13), channel_id=1, source_target_pairs={{0,1},{1,0},{2,3},{3,2},{4,5},{5,4},{6,7},{7,6},{8,9},{9,8},{10,11... | collective-permute-start | bytes 1179656 | tf_op jit(solution)/shard_map/ppermute | solution.py:21
  161.8 15.1 %collective-permute-start.10 = (bf16[256,768]{1,0:T(8,128)(2,1)}, bf16[256,768]{1,0:T(8,128)(2,1)S(1)}, u32[]{:S(2)}, u32[]{:S(2)}) collective-permute-start(bf16[256,768]{1,0:T(8,128)(2,1)} %get-tuple-element.14), channel_id=1, source_target_pairs={{0,2},{2,0},{1,3},{3,1},{4,6},{6,4},{5,7},{7,5},{8,10},{10,8},{9,1... | collective-permute-start | bytes 1179656 | tf_op jit(solution)/shard_map/ppermute | solution.py:21

commit v5 on v2

v5 whole, which is shorter than its diff:
```python
import functools

import jax
import jax.numpy as jnp
from jax import lax
from jax.experimental import pallas as pl
from jax.experimental.pallas import tpu as pltpu
from jax.sharding import Mesh, PartitionSpec as P


F32 = jnp.float32
BF16 = jnp.bfloat16
FEAT = ("x", "yh", "c")
FFN_MIB = 24
LEVEL_AXES = (("c", 0), ("yh", 0), ("x", 0), ("x", 1))


def swap(array, axis, bit):
    return lax.ppermute(array, axis, [(i, i ^ (1 << bit)) for i in range(lax.axis_size(axis))])


def dot_nt(a, b):
    return lax.dot_general(a, b, (((1,), (1,)), ((), ())), preferred_element_type=F32)


def dot_nn(a, b):
    return lax.dot_general(a, b, (((1,), (0,)), ((), ())), preferred_element_type=F32)


def total_of(stack):
    return lax.reduce_precision(jnp.sum(stack.astype(F32), axis=0), 8, 7).astype(BF16)


def fetch(src, dst, sem, lo, size):
    part = pl.ds(lo, size)
    return pltpu.make_async_copy(src.at[part], dst.at[part], sem)


def ffn_body(kinds, rows, rank, *refs):
    n = kinds * rows
    count = kinds + 2
    ins, outs = refs[:count], refs[count : count + kinds + 1]
    bufs, stage = refs[count + kinds + 1 : 2 * count + kinds + 1], refs[2 * count + kinds + 1 : -2]
    sems, out_sems = refs[-2:]
    xs, (mine, other) = bufs[:kinds], bufs[kinds:]
    db = mine.shape[1]
    head = db - rank

    def part(i, sem, lo, size):
        return fetch(ins[i], bufs[i], sems.at[sem], lo, size)

    def stored(k):
        copy = pltpu.make_async_copy(stage[k], outs[k], out_sems.at[k])
        copy.start()
        return copy

    first = [part(0, 0, 0, xs[0].shape[0])]
    late = []
    for i in (kinds, kinds + 1):
        first.append(part(i, i, 2 * n, 2 * rows))
        first.append(part(i, i + 2, 0, n))
        late.append(part(i, i + 4, n, n))
    partners = [part(i, i, 0, xs[i].shape[0]) for i in range(1, kinds)]
    for copy in first + partners + late:
        copy.start()
    for copy in first:
        copy.wait()

    def both(lo, hi, at, size):
        return jnp.concatenate([ref[lo:hi, at : at + size] for ref in (mine, other)], axis=0)

    pre = dot_nt(xs[0][:, db:], both(2 * n, 2 * n + rows, 0, rank))
    pre = pre + dot_nt(xs[0][:, :db], both(0, rows, 0, db))
    for k in range(1, kinds):
        partners[k - 1].wait()
        pre = pre + dot_nt(xs[k][...], both(k * rows, (k + 1) * rows, 0, db))
    hidden = (0.5 * pre * (1.0 + lax.erf(pre * (0.5**0.5)))).astype(BF16)
    back = stage[kinds]
    back[:, :head] = dot_nn(hidden, both(2 * n, 2 * n + rows, rank, head)).astype(BF16)
    back[:, head:] = dot_nn(hidden, both(2 * n + rows, 2 * n + 2 * rows, 0, rank - head)).astype(BF16)
    stores = [stored(kinds)]
    for copy in late:
        copy.wait()
    for k in range(kinds):
        lo = n + k * rows
        stage[k][...] = dot_nn(hidden, both(lo, lo + rows, 0, db)).astype(outs[k].dtype)
        stores.append(stored(k))
    for copy in stores:
        copy.wait()


def ffn_call(gathered, pieces, mine, other, kinds):
    count, width = gathered.shape
    db = mine.shape[1]
    rank = width - db
    rows = mine.shape[0] // (2 * kinds + 2)
    args = (gathered, *pieces, mine, other)
    outs = [((count, db), F32)] + [((count, db), BF16)] * (kinds - 1) + [((count, rank), BF16)]
    return pl.pallas_call(
        functools.partial(ffn_body, kinds, rows, rank),
        out_shape=[pltpu.HBM(*a) for a in outs],
        in_specs=[pl.BlockSpec(memory_space=pl.ANY)] * len(args),
        scratch_shapes=[pltpu.VMEM(a.shape, BF16) for a in args]
        + [pltpu.VMEM(*a) for a in outs]
        + [pltpu.SemaphoreType.DMA((len(args) + 4,)), pltpu.SemaphoreType.DMA((len(outs),))],
        compiler_params=pltpu.CompilerParams(vmem_limit_bytes=FFN_MIB * 2**20),
        name="ffn",
    )(*args)


def pack_body(rank, up, down, right, left, out, sems):
    n, db = up.shape
    rows = right.shape[0]
    head = db - rank
    moves = (
        (up, out.at[pl.ds(0, n)]),
        (down, out.at[pl.ds(n, n)]),
        (right, out.at[pl.ds(2 * n, rows), pl.ds(0, rank)]),
        (left.at[:, pl.ds(0, head)], out.at[pl.ds(2 * n, rows), pl.ds(rank, head)]),
        (left.at[:, pl.ds(head, rank - head)], out.at[pl.ds(2 * n + rows, rows), pl.ds(0, rank - head)]),
    )
    copies = [pltpu.make_async_copy(src, dst, sems.at[i]) for i, (src, dst) in enumerate(moves)]
    for copy in copies:
        copy.start()
    for copy in copies:
        copy.wait()


def pack_call(up, down, right, left):
    (n, db), (rows, rank) = up.shape, right.shape
    return pl.pallas_call(
        functools.partial(pack_body, rank),
        out_shape=pltpu.HBM((2 * n + 2 * rows, db), BF16),
        in_specs=[pl.BlockSpec(memory_space=pl.ANY)] * 4,
        scratch_shapes=[pltpu.SemaphoreType.DMA((5,))],
        compiler_params=pltpu.CompilerParams(vmem_limit_bytes=60 * 2**20),
        name="pack",
    )(up, down, right, left)


def code_body(x, w, stack):
    part = dot_nn(x[...], w[...]).astype(BF16)
    for i in range(stack.shape[0]):
        stack[i] = part


def code_call(tokens, up_left, n):
    shape = jax.ShapeDtypeStruct((n, tokens.shape[0], up_left.shape[1]), BF16)
    return pl.pallas_call(code_body, out_shape=shape, name="code_part", compiler_params=pltpu.CompilerParams(vmem_limit_bytes=60 * 2**20))(tokens, up_left)


def per_device(tokens, up_weight, down_weight, up_left, up_right, down_left, down_right):
    nz, nf = lax.axis_size("z"), lax.axis_size(FEAT)
    count, db = tokens.shape
    rows, rank = up_right.shape[1:]
    kinds = up_weight.shape[2]
    up = up_weight[0].transpose(1, 0, 2).reshape(kinds * rows, db)
    down = down_weight[0].transpose(1, 0, 2).reshape(kinds * rows, db)

    packed = pack_call(up, down, up_right[0], down_left[0])
    stack = code_call(tokens, up_left, nf)
    stack = lax.all_to_all(stack, FEAT, 0, 0, tiled=True)
    other = swap(packed, "yl", 0)
    mine = jnp.concatenate([tokens, total_of(stack)], axis=1)
    gathered = lax.all_gather(mine, "z", axis=0, tiled=True)
    own = gathered[:, :db]
    pieces = []
    for axis, bit in LEVEL_AXES:
        pieces.append(swap(own, axis, bit))

    own_total, *terms, back = ffn_call(gathered, pieces, packed, other, kinds)
    sent = []
    for part, (axis, bit) in zip(terms, LEVEL_AXES):
        sent.append(swap(part, axis, bit))
    back = lax.all_to_all(back.reshape(nz, count, rank), "z", 0, 0, tiled=True)
    total = own_total
    for s in sent:
        total = total + s.astype(F32)
    total = total.astype(BF16)
    total = lax.all_to_all(total.reshape(nz, count, db), "z", 0, 0, tiled=True)
    back = total_of(back)
    back = lax.all_gather(back, FEAT, axis=0)
    back = total_of(back)
    total = jnp.sum(total.astype(F32), axis=0)
    return (total + dot_nn(back, down_right)).astype(BF16)


def solution(mesh):
    tok, feat = ("z", "yl"), FEAT
    inner = Mesh(mesh.devices.reshape(16, 2, 4, 2, 2), tok + feat)
    return jax.shard_map(
        per_device,
        mesh=inner,
        in_specs=(
            P(tok, feat),
            P(feat, tok, None, None),
            P(feat, tok, None, None),
            P(feat, None),
            P(feat, tok, None),
            P(feat, tok, None),
            P(None, feat),
        ),
        out_specs=P(tok, feat),
        check_vma=False,
    )
```

time: 167 us -> 191 us (1.14)
  the two profiles are of different devices: /device:TPU:6 before, /device:TPU:1 now
where the time goes in v5:
time: 191 us
  blocking collectives  100 us (52%)
  starting transfers between devices  57.2 us (30%)
  waiting for transfers between devices  17.2 us (9%)
  Pallas kernels  12.4 us (6%)
  other arithmetic  2.3 us (1%)
    all_to_all x1, blocking collectives, per_device(): stack = lax.all_to_all(stack, FEAT, 0, 0, tiled=True)  42.5 us
    ppermute x9, starting transfers between devices, swap(): lax.ppermute(array, axis, [(i, i ^ 1 << bit) for i in range(lax.axis_size...  39 us
    all_gather x1, blocking collectives, per_device(): gathered = lax.all_gather(mine, 'z', axis=0, tiled=True)  32.3 us
    all_gather x1, blocking collectives, per_device(): back = lax.all_gather(back, FEAT, axis=0)  25.6 us
    ppermute x9, waiting for transfers between devices, swap(): lax.ppermute(array, axis, [(i, i ^ 1 << bit) for i in range(lax.axis_size...  17.2 us
    all_to_all x1, starting transfers between devices, per_device(): total = lax.all_to_all(total.reshape(nz, count, db), 'z', 0, 0, tiled=True)  11.7 us
    pallas_call x1, Pallas kernels, ffn_call(): pl.pallas_call(functools.partial(ffn_body, kinds, rows, rank), out_shape=...  7.69 us
    all_to_all x1, starting transfers between devices, per_device(): back = lax.all_to_all(back.reshape(nz, count, rank), 'z', 0, 0, tiled=True)  6.39 us
  transfers between devices with their start and end apart: 11, of which 4 were waited for; matrix products, arithmetic and copies ran while one was open for 1% of the time, Pallas kernels for 1%

profile of v5, /device:TPU:1, one launch (start us, length us, event | category | flops | bytes accessed | tf_op | source)
XLA Modules:
  0.0 190.5 jit_solution(10820885796783320528)
XLA Ops:
  0.0 0.0 copy-start
  0.0 2.7 %pack.1.refs_5_ = bf16[1152,768]{1,0:T(8,128)(2,1)} custom-call(bf16[480,768]{1,0:T(8,128)(2,1)} %bitcast.18, bf16[480,768]{1,0:T(8,128)(2,1)} %bitcast.19, bf16[96,512]{1,0:T(8,128)(2,1)} %bitcast.21, bf16[96,512]{1,0:T(8,128)(2,1)} %bitcast.22), custom_call_target="tpu_custom_call" | custom-call | tf_op jit(solution)/shard_map/pack/pallas_call | solution.py:131
  2.7 0.0 copy-start.2
  2.7 0.0 copy-start.1
  2.7 4.2 %collective-permute-start.4 = (bf16[1152,768]{1,0:T(8,128)(2,1)}, bf16[1152,768]{1,0:T(8,128)(2,1)}, u32[]{:S(2)}, u32[]{:S(2)}) collective-permute-start(bf16[1152,768]{1,0:T(8,128)(2,1)} %pack.1.refs_5_), channel_id=1, source_target_pairs={{0,16},{16,0},{1,17},{17,1},{2,18},{18,2},{3,19},{19,3},{4,20},{20... | collective-permute-start | bytes 5308424 | tf_op jit(solution)/shard_map/ppermute | solution.py:19
  6.9 2.1 %code_part.1 = bf16[16,16,512]{2,1,0:T(8,128)(2,1)} custom-call(bf16[16,768]{1,0:T(8,128)(2,1)} %x.1, bf16[768,512]{1,0:T(8,128)(2,1)} %w.1), custom_call_target="tpu_custom_call" | custom-call | tf_op jit(solution)/shard_map/code_part/pallas_call | solution.py:149
  9.0 42.5 %all_to_all.15 = bf16[16,16,512]{2,1,0:T(8,128)(2,1)S(1)} all-to-all(bf16[16,16,512]{2,1,0:T(8,128)(2,1)} %code_part.1), channel_id=1, replica_groups=mesh['z'=16,'yl'=2,'x'=4,'yh'=2,'c'=2] {'x','yh','c'}, dimensions={0} | all-to-all | bytes 524288 | tf_op jit(solution)/shard_map/all_to_all | solution.py:162
  51.5 0.0 copy-done.2
  51.5 32.3 %all_gather.7.refs_0_ = bf16[256,1280]{1,0:T(8,128)(2,1)S(1)} all-gather(bf16[16,1280]{1,0:T(8,128)(2,1)S(1)} %pad_maximum_fusion), channel_id=1, replica_groups=mesh['z'=16,'yl'=2,'x'=4,'yh'=2,'c'=2] {'z'}, dimensions={0}, use_global_device_ids=true | all-gather | bytes 696320 | tf_op jit(solution)/shard_map/all_gather | solution.py:165
  83.8 4.7 %collective-permute-start.3 = (bf16[256,768]{1,0:T(8,128)(2,1)S(1)}, bf16[256,768]{1,0:T(8,128)(2,1)S(1)}, u32[]{:S(2)}, u32[]{:S(2)}) collective-permute-start(bf16[256,768]{1,0:T(8,128)(2,1)S(1)} %slice.4), channel_id=1, source_target_pairs={{0,8},{4,12},{8,0},{12,4},{1,9},{5,13},{9,1},{13,5},{2,10},{6,14},... | collective-permute-start | bytes 1179656 | tf_op jit(solution)/shard_map/ppermute | solution.py:19
  88.5 2.2 %collective-permute-start.2 = (bf16[256,768]{1,0:T(8,128)(2,1)S(1)}, bf16[256,768]{1,0:T(8,128)(2,1)S(1)}, u32[]{:S(2)}, u32[]{:S(2)}) collective-permute-start(bf16[256,768]{1,0:T(8,128)(2,1)S(1)} %slice.4), channel_id=1, source_target_pairs={{0,4},{4,0},{8,12},{12,8},{1,5},{5,1},{9,13},{13,9},{2,6},{6,2},{1... | collective-permute-start | bytes 1179656 | tf_op jit(solution)/shard_map/ppermute | solution.py:19
  90.7 1.9 %collective-permute-start.1 = (bf16[256,768]{1,0:T(8,128)(2,1)S(1)}, bf16[256,768]{1,0:T(8,128)(2,1)S(1)}, u32[]{:S(2)}, u32[]{:S(2)}) collective-permute-start(bf16[256,768]{1,0:T(8,128)(2,1)S(1)} %slice.4), channel_id=1, source_target_pairs={{0,2},{2,0},{1,3},{3,1},{4,6},{6,4},{5,7},{7,5},{8,10},{10,8},{9,1... | collective-permute-start | bytes 1179656 | tf_op jit(solution)/shard_map/ppermute | solution.py:19
  92.6 10.7 %collective-permute-start = (bf16[256,768]{1,0:T(8,128)(2,1)S(1)}, bf16[256,768]{1,0:T(8,128)(2,1)S(1)}, u32[]{:S(2)}, u32[]{:S(2)}) collective-permute-start(bf16[256,768]{1,0:T(8,128)(2,1)S(1)} %slice.4), channel_id=1, source_target_pairs={{0,1},{1,0},{2,3},{3,2},{4,5},{5,4},{6,7},{7,6},{8,9},{9,8},{10,11... | collective-permute-start | bytes 1179656 | tf_op jit(solution)/shard_map/ppermute | solution.py:19
  103.4 0.0 collective-permute-done.3.refs_4_
  103.4 0.0 collective-permute-done.2.refs_3_
  103.4 0.0 collective-permute-done.1.refs_2_
  103.4 1.3 collective-permute-done.refs_1_
  104.7 0.0 collective-permute-done.4.refs_6_
  104.7 0.0 copy-done.1
  104.7 7.7 %ffn.1 = (f32[256,768]{1,0:T(8,128)}, bf16[256,768]{1,0:T(8,128)(2,1)}, bf16[256,768]{1,0:T(8,128)(2,1)}, bf16[256,768]{1,0:T(8,128)(2,1)}, bf16[256,768]{1,0:T(8,128)(2,1)}, /*index=5*/bf16[256,512]{1,0:T(8,128)(2,1)}) custom-call(bf16[256,1280]{1,0:T(8,128)(2,1)S(1)} %all_gather.7.refs_0_, bf16[256,768]{1,0:T(8,128)(2,1)S(1)} %collective-permute-done.refs_1_, ...), custom_call_target="tpu_custom_call" | custom-call | tf_op jit(solution)/shard_map/ffn/pallas_call | solution.py:99
  112.4 6.4 %all-to-all-start.2 = ((bf16[16,16,512]{2,1,0:T(8,128)(2,1)}), bf16[16,16,512]{2,1,0:T(8,128)(2,1)S(1)}, u32[]{:S(2)}, u32[]{:S(2)}) async-start(bf16[16,16,512]{2,1,0:T(8,128)(2,1)} %bitcast.20), calls=%async_computation.2 | async-start | bytes 524288 | tf_op jit(solution)/shard_map/all_to_all | solution.py:175
  118.8 7.8 %collective-permute-start.5 = (bf16[256,768]{1,0:T(8,128)(2,1)}, bf16[256,768]{1,0:T(8,128)(2,1)S(1)}, u32[]{:S(2)}, u32[]{:S(2)}) collective-permute-start(bf16[256,768]{1,0:T(8,128)(2,1)} %get-tuple-element.12), channel_id=1, source_target_pairs={{0,1},{1,0},{2,3},{3,2},{4,5},{5,4},{6,7},{7,6},{8,9},{9,8},{10,11... | collective-permute-start | bytes 1179656 | tf_op jit(solution)/shard_map/ppermute | solution.py:19
  126.6 2.1 %collective-permute-start.6 = (bf16[256,768]{1,0:T(8,128)(2,1)}, bf16[256,768]{1,0:T(8,128)(2,1)S(1)}, u32[]{:S(2)}, u32[]{:S(2)}) collective-permute-start(bf16[256,768]{1,0:T(8,128)(2,1)} %get-tuple-element.13), channel_id=1, source_target_pairs={{0,2},{2,0},{1,3},{3,1},{4,6},{6,4},{5,7},{7,5},{8,10},{10,8},{9,1... | collective-permute-start | bytes 1179656 | tf_op jit(solution)/shard_map/ppermute | solution.py:19
  128.7 3.1 %collective-permute-start.7 = (bf16[256,768]{1,0:T(8,128)(2,1)}, bf16[256,768]{1,0:T(8,128)(2,1)S(1)}, u32[]{:S(2)}, u32[]{:S(2)}) collective-permute-start(bf16[256,768]{1,0:T(8,128)(2,1)} %get-tuple-element.14), channel_id=1, source_target_pairs={{0,4},{4,0},{8,12},{12,8},{1,5},{5,1},{9,13},{13,9},{2,6},{6,2},{1... | collective-permute-start | bytes 1179656 | tf_op jit(solution)/shard_map/ppermute | solution.py:19
  131.7 2.5 %collective-permute-start.8 = (bf16[256,768]{1,0:T(8,128)(2,1)}, bf16[256,768]{1,0:T(8,128)(2,1)S(1)}, u32[]{:S(2)}, u32[]{:S(2)}) collective-permute-start(bf16[256,768]{1,0:T(8,128)(2,1)} %get-tuple-element.15), channel_id=1, source_target_pairs={{0,8},{4,12},{8,0},{12,4},{1,9},{5,13},{9,1},{13,5},{2,10},{6,14},... | collective-permute-start | bytes 1179656 | tf_op jit(solution)/shard_map/ppermute | solution.py:19
  134.2 0.0 collective-permute-done.5
  134.2 6.6 %collective-permute-done.6 = bf16[256,768]{1,0:T(8,128)(2,1)S(1)} collective-permute-done((bf16[256,768]{1,0:T(8,128)(2,1)}, bf16[256,768]{1,0:T(8,128)(2,1)S(1)}, u32[]{:S(2)}, u32[]{:S(2)}) %collective-permute-start.6) | collective-permute-done | bytes 393248 | tf_op jit(solution)/shard_map/ppermute | solution.py:19
  140.9 0.3 collective-permute-done.7
  141.1 9.0 %collective-permute-done.8 = bf16[256,768]{1,0:T(8,128)(2,1)S(1)} collective-permute-done((bf16[256,768]{1,0:T(8,128)(2,1)}, bf16[256,768]{1,0:T(8,128)(2,1)S(1)}, u32[]{:S(2)}, u32[]{:S(2)}) %collective-permute-start.8) | collective-permute-done | bytes 393248 | tf_op jit(solution)/shard_map/ppermute | solution.py:19
  150.1 2.1 %add_convert_fusion = bf16[256,768]{1,0:T(8,128)(2,1)} fusion(bf16[256,768]{1,0:T(8,128)(2,1)S(1)} %collective-permute-done.8, bf16[256,768]{1,0:T(8,128)(2,1)S(1)} %collective-permute-done.7, bf16[256,768]{1,0:T(8,128)(2,1)S(1)} %collective-permute-done.6, f32[256,768]{1,0:T(8,128)} %get-tuple-element.11, bf16[256,768]{1,0:T(8,128)(2,1)S(1)} %collective-permute-done.5), kind=kLoop, calls=%fused_computation.3 | loop fusion | flops 1769472 | bytes 2752512 | tf_op jit(solution)/shard_map/convert_element_type | solution.py:179
  152.2 0.0 all-to-all-done.2
  152.2 11.7 %all-to-all-start.1 = ((bf16[16,16,768]{2,1,0:T(8,128)(2,1)}), bf16[16,16,768]{2,1,0:T(8,128)(2,1)S(1)}, u32[]{:S(2)}, u32[]{:S(2)}) async-start(bf16[16,16,768]{2,1,0:T(8,128)(2,1)} %bitcast.8), calls=%async_computation.1 | async-start | bytes 786432 | tf_op jit(solution)/shard_map/all_to_all | solution.py:180
  164.0 25.6 %all-gather = bf16[256,512]{1,0:T(8,128)(2,1)S(1)} all-gather(bf16[16,512]{1,0:T(8,128)(2,1)S(1)} %reduce-precision_convert_fusion.1), channel_id=2, replica_groups=mesh['z'=16,'yl'=2,'x'=4,'yh'=2,'c'=2] {'x','yh','c'}, dimensions={0}, use_global_device_ids=true | all-gather | bytes 278528 | tf_op jit(solution)/shard_map/all_gather | solution.py:182
  189.6 0.0 all-to-all-done.1
  189.6 0.1 convert_reduce_fusion
  189.7 0.0 copy-done
  189.7 0.8 fusion
  (7 shorter events, 0.2 us)
Async XLA Ops:
  0.0 189.7 %copy-start = (bf16[512,768]{1,0:T(8,128)(2,1)S(1)}, bf16[512,768]{1,0:T(8,128)(2,1)}, u32[]{:S(2)}) copy-start(bf16[512,768]{1,0:T(8,128)(2,1)} %param.13) | copy-start | bytes 2359300
  2.7 48.8 %copy-start.2 = (bf16[16,768]{1,0:T(8,128)(2,1)S(1)}, bf16[16,768]{1,0:T(8,128)(2,1)}, u32[]{:S(2)}) copy-start(bf16[16,768]{1,0:T(8,128)(2,1)} %x.1) | copy-start | bytes 73732
  2.7 102.0 %copy-start.1 = (bf16[1152,768]{1,0:T(8,128)(2,1)S(1)}, bf16[1152,768]{1,0:T(8,128)(2,1)}, u32[]{:S(2)}) copy-start(bf16[1152,768]{1,0:T(8,128)(2,1)} %pack.1.refs_5_) | copy-start | bytes 5308420
  2.7 102.0 %collective-permute-start.4 = (bf16[1152,768]{1,0:T(8,128)(2,1)}, bf16[1152,768]{1,0:T(8,128)(2,1)}, u32[]{:S(2)}, u32[]{:S(2)}) collective-permute-start(bf16[1152,768]{1,0:T(8,128)(2,1)} %pack.1.refs_5_), channel_id=1, source_target_pairs={{0,16},{16,0},{1,17},{17,1},{2,18},{18,2},{3,19},{19,3},{4,20},{20... | collective-permute-start | bytes 5308424 | tf_op jit(solution)/shard_map/ppermute | solution.py:19
  83.8 19.5 %collective-permute-start.3 = (bf16[256,768]{1,0:T(8,128)(2,1)S(1)}, bf16[256,768]{1,0:T(8,128)(2,1)S(1)}, u32[]{:S(2)}, u32[]{:S(2)}) collective-permute-start(bf16[256,768]{1,0:T(8,128)(2,1)S(1)} %slice.4), channel_id=1, source_target_pairs={{0,8},{4,12},{8,0},{12,4},{1,9},{5,13},{9,1},{13,5},{2,10},{6,14},... | collective-permute-start | bytes 1179656 | tf_op jit(solution)/shard_map/ppermute | solution.py:19
  88.5 14.9 %collective-permute-start.2 = (bf16[256,768]{1,0:T(8,128)(2,1)S(1)}, bf16[256,768]{1,0:T(8,128)(2,1)S(1)}, u32[]{:S(2)}, u32[]{:S(2)}) collective-permute-start(bf16[256,768]{1,0:T(8,128)(2,1)S(1)} %slice.4), channel_id=1, source_target_pairs={{0,4},{4,0},{8,12},{12,8},{1,5},{5,1},{9,13},{13,9},{2,6},{6,2},{1... | collective-permute-start | bytes 1179656 | tf_op jit(solution)/shard_map/ppermute | solution.py:19
  90.7 12.7 %collective-permute-start.1 = (bf16[256,768]{1,0:T(8,128)(2,1)S(1)}, bf16[256,768]{1,0:T(8,128)(2,1)S(1)}, u32[]{:S(2)}, u32[]{:S(2)}) collective-permute-start(bf16[256,768]{1,0:T(8,128)(2,1)S(1)} %slice.4), channel_id=1, source_target_pairs={{0,2},{2,0},{1,3},{3,1},{4,6},{6,4},{5,7},{7,5},{8,10},{10,8},{9,1... | collective-permute-start | bytes 1179656 | tf_op jit(solution)/shard_map/ppermute | solution.py:19
  92.6 12.0 %collective-permute-start = (bf16[256,768]{1,0:T(8,128)(2,1)S(1)}, bf16[256,768]{1,0:T(8,128)(2,1)S(1)}, u32[]{:S(2)}, u32[]{:S(2)}) collective-permute-start(bf16[256,768]{1,0:T(8,128)(2,1)S(1)} %slice.4), channel_id=1, source_target_pairs={{0,1},{1,0},{2,3},{3,2},{4,5},{5,4},{6,7},{7,6},{8,9},{9,8},{10,11... | collective-permute-start | bytes 1179656 | tf_op jit(solution)/shard_map/ppermute | solution.py:19
  112.4 39.8 %all-to-all-start.2 = ((bf16[16,16,512]{2,1,0:T(8,128)(2,1)}), bf16[16,16,512]{2,1,0:T(8,128)(2,1)S(1)}, u32[]{:S(2)}, u32[]{:S(2)}) async-start(bf16[16,16,512]{2,1,0:T(8,128)(2,1)} %bitcast.20), calls=%async_computation.2 | async-start | bytes 524288 | tf_op jit(solution)/shard_map/all_to_all | solution.py:175
  118.8 15.4 %collective-permute-start.5 = (bf16[256,768]{1,0:T(8,128)(2,1)}, bf16[256,768]{1,0:T(8,128)(2,1)S(1)}, u32[]{:S(2)}, u32[]{:S(2)}) collective-permute-start(bf16[256,768]{1,0:T(8,128)(2,1)} %get-tuple-element.12), channel_id=1, source_target_pairs={{0,1},{1,0},{2,3},{3,2},{4,5},{5,4},{6,7},{7,6},{8,9},{9,8},{10,11... | collective-permute-start | bytes 1179656 | tf_op jit(solution)/shard_map/ppermute | solution.py:19
  126.6 14.3 %collective-permute-start.6 = (bf16[256,768]{1,0:T(8,128)(2,1)}, bf16[256,768]{1,0:T(8,128)(2,1)S(1)}, u32[]{:S(2)}, u32[]{:S(2)}) collective-permute-start(bf16[256,768]{1,0:T(8,128)(2,1)} %get-tuple-element.13), channel_id=1, source_target_pairs={{0,2},{2,0},{1,3},{3,1},{4,6},{6,4},{5,7},{7,5},{8,10},{10,8},{9,1... | collective-permute-start | bytes 1179656 | tf_op jit(solution)/shard_map/ppermute | solution.py:19
  128.7 12.5 %collective-permute-start.7 = (bf16[256,768]{1,0:T(8,128)(2,1)}, bf16[256,768]{1,0:T(8,128)(2,1)S(1)}, u32[]{:S(2)}, u32[]{:S(2)}) collective-permute-start(bf16[256,768]{1,0:T(8,128)(2,1)} %get-tuple-element.14), channel_id=1, source_target_pairs={{0,4},{4,0},{8,12},{12,8},{1,5},{5,1},{9,13},{13,9},{2,6},{6,2},{1... | collective-permute-start | bytes 1179656 | tf_op jit(solution)/shard_map/ppermute | solution.py:19
  131.7 18.4 %collective-permute-start.8 = (bf16[256,768]{1,0:T(8,128)(2,1)}, bf16[256,768]{1,0:T(8,128)(2,1)S(1)}, u32[]{:S(2)}, u32[]{:S(2)}) collective-permute-start(bf16[256,768]{1,0:T(8,128)(2,1)} %get-tuple-element.15), channel_id=1, source_target_pairs={{0,8},{4,12},{8,0},{12,4},{1,9},{5,13},{9,1},{13,5},{2,10},{6,14},... | collective-permute-start | bytes 1179656 | tf_op jit(solution)/shard_map/ppermute | solution.py:19
  152.2 37.4 %all-to-all-start.1 = ((bf16[16,16,768]{2,1,0:T(8,128)(2,1)}), bf16[16,16,768]{2,1,0:T(8,128)(2,1)S(1)}, u32[]{:S(2)}, u32[]{:S(2)}) async-start(bf16[16,16,768]{2,1,0:T(8,128)(2,1)} %bitcast.8), calls=%async_computation.1 | async-start | bytes 786432 | tf_op jit(solution)/shard_map/all_to_all | solution.py:180

commit v6 on v5

--- a/solution.py
+++ b/solution.py
@@ -34,6 +34,45 @@
 def fetch(src, dst, sem, lo, size):
     part = pl.ds(lo, size)
     return pltpu.make_async_copy(src.at[part], dst.at[part], sem)
+
+
+def both(mine, other, lo, hi, at, size):
+    return jnp.concatenate([ref[lo:hi, at : at + size] for ref in (mine, other)], axis=0)
+
+
+def own_body(kinds, rows, rank, gathered, mine_in, other_in, out, tokens, mine, other, staged, sems):
+    n = kinds * rows
+    db = mine.shape[1]
+    ways = ((mine_in, mine), (other_in, other))
+    head = fetch(gathered, tokens, sems.at[0], 0, tokens.shape[0])
+    right = [fetch(src, dst, sems.at[1 + i], 2 * n, rows) for i, (src, dst) in enumerate(ways)]
+    up = [fetch(src, dst, sems.at[3 + i], 0, rows) for i, (src, dst) in enumerate(ways)]
+    for copy in (head, *right, *up):
+        copy.start()
+    for copy in (head, *right, *up):
+        copy.wait()
+    part = dot_nt(tokens[:, db:], both(mine, other, 2 * n, 2 * n + rows, 0, rank))
+    staged[...] = part + dot_nt(tokens[:, :db], both(mine, other, 0, rows, 0, db))
+    store = pltpu.make_async_copy(staged, out, sems.at[5])
+    store.start()
+    store.wait()
+
+
+def own_call(gathered, mine, other, kinds):
+    count, width = gathered.shape
+    rows = mine.shape[0] // (2 * kinds + 2)
+    args = (gathered, mine, other)
+    out = ((count, 2 * rows), F32)
+    return pl.pallas_call(
+        functools.partial(own_body, kinds, rows, width - mine.shape[1]),
+        out_shape=jax.ShapeDtypeStruct(*out),
+        in_specs=[pl.BlockSpec(memory_space=pl.ANY)] * 3,
+        out_specs=pl.BlockSpec(memory_space=pl.ANY),
+        scratch_shapes=[pltpu.VMEM(a.shape, BF16) for a in args]
+        + [pltpu.VMEM(*out), pltpu.SemaphoreType.DMA((6,))],
+        compiler_params=pltpu.CompilerParams(vmem_limit_bytes=FFN_MIB * 2**20),
+        name="ffn_own",
+    )(*args)
 
 
 def ffn_body(kinds, rows, rank, *refs):
@@ -57,8 +96,8 @@
     first = [part(0, 0, 0, xs[0].shape[0])]
     late = []
     for i in (kinds, kinds + 1):
-        first.append(part(i, i, 2 * n, 2 * rows))
-        first.append(part(i, i + 2, 0, n))
+        first.append(part(i, i, rows, n - rows))
+        late.append(part(i, i + 2, 2 * n, 2 * rows))
         late.append(part(i, i + 4, n, n))
     partners = [part(i, i, 0, xs[i].shape[0]) for i in range(1, kinds)]
     for copy in first + partners + late:
@@ -66,41 +105,36 @@
     for copy in first:
         copy.wait()
 
-    def both(lo, hi, at, size):
-        return jnp.concatenate([ref[lo:hi, at : at + size] for ref in (mine, other)], axis=0)
-
-    pre = dot_nt(xs[0][:, db:], both(2 * n, 2 * n + rows, 0, rank))
-    pre = pre + dot_nt(xs[0][:, :db], both(0, rows, 0, db))
+    pre = xs[0][...]
     for k in range(1, kinds):
         partners[k - 1].wait()
-        pre = pre + dot_nt(xs[k][...], both(k * rows, (k + 1) * rows, 0, db))
+        pre = pre + dot_nt(xs[k][...], both(mine, other, k * rows, (k + 1) * rows, 0, db))
     hidden = (0.5 * pre * (1.0 + lax.erf(pre * (0.5**0.5)))).astype(BF16)
+    for copy in late:
+        copy.wait()
     back = stage[kinds]
-    back[:, :head] = dot_nn(hidden, both(2 * n, 2 * n + rows, rank, head)).astype(BF16)
-    back[:, head:] = dot_nn(hidden, both(2 * n + rows, 2 * n + 2 * rows, 0, rank - head)).astype(BF16)
+    back[:, :head] = dot_nn(hidden, both(mine, other, 2 * n, 2 * n + rows, rank, head)).astype(BF16)
+    back[:, head:] = dot_nn(hidden, both(mine, other, 2 * n + rows, 2 * n + 2 * rows, 0, rank - head)).astype(BF16)
     stores = [stored(kinds)]
-    for copy in late:
-        copy.wait()
     for k in range(kinds):
         lo = n + k * rows
-        stage[k][...] = dot_nn(hidden, both(lo, lo + rows, 0, db)).astype(outs[k].dtype)
+        stage[k][...] = dot_nn(hidden, both(mine, other, lo, lo + rows, 0, db)).astype(outs[k].dtype)
         stores.append(stored(k))
     for copy in stores:
         copy.wait()
 
 
-def ffn_call(gathered, pieces, mine, other, kinds):
-    count, width = gathered.shape
+def ffn_call(own, pieces, mine, other, rank, kinds):
+    count = own.shape[0]
     db = mine.shape[1]
-    rank = width - db
     rows = mine.shape[0] // (2 * kinds + 2)
-    args = (gathered, *pieces, mine, other)
+    args = (own, *pieces, mine, other)
     outs = [((count, db), F32)] + [((count, db), BF16)] * (kinds - 1) + [((count, rank), BF16)]
     return pl.pallas_call(
         functools.partial(ffn_body, kinds, rows, rank),
         out_shape=[pltpu.HBM(*a) for a in outs],
         in_specs=[pl.BlockSpec(memory_space=pl.ANY)] * len(args),
-        scratch_shapes=[pltpu.VMEM(a.shape, BF16) for a in args]
+        scratch_shapes=[pltpu.VMEM(a.shape, a.dtype) for a in args]
         + [pltpu.VMEM(*a) for a in outs]
         + [pltpu.SemaphoreType.DMA((len(args) + 4,)), pltpu.SemaphoreType.DMA((len(outs),))],
         compiler_params=pltpu.CompilerParams(vmem_limit_bytes=FFN_MIB * 2**20),
@@ -168,7 +202,8 @@
     for axis, bit in LEVEL_AXES:
         pieces.append(swap(own, axis, bit))
 
-    own_total, *terms, back = ffn_call(gathered, pieces, packed, other, kinds)
+    own_pre = own_call(gathered, packed, other, kinds)
+    own_total, *terms, back = ffn_call(own_pre, pieces, packed, other, rank, kinds)
     sent = []
     for part, (axis, bit) in zip(terms, LEVEL_AXES):
         sent.append(swap(part, axis, bit))

time: 191 us -> 190 us (level)
    pallas_call x0 -> x1, Pallas kernels: none -> 1.94 us  [own_call(): pl.pallas_call(functools.partial(own_body, kinds, rows, width - mine.shap...]
  transfers between devices with their start and end apart: 11 -> 11, of which waited for: 4 -> 3; matrix products, arithmetic and copies ran while one was open for 1% -> 1% of each run, Pallas kernels for 1% -> 2%
where the time goes in v6:
time: 190 us
  blocking collectives  100 us (53%)
  starting transfers between devices  56.5 us (30%)
  waiting for transfers between devices  15.9 us (8%)
  Pallas kernels  13.5 us (7%)
  other arithmetic  2.3 us (1%)
    all_to_all x1, blocking collectives, per_device(): stack = lax.all_to_all(stack, FEAT, 0, 0, tiled=True)  42.5 us
    ppermute x9, starting transfers between devices, swap(): lax.ppermute(array, axis, [(i, i ^ 1 << bit) for i in range(lax.axis_size...  38.4 us
    all_gather x1, blocking collectives, per_device(): gathered = lax.all_gather(mine, 'z', axis=0, tiled=True)  32.3 us
    all_gather x1, blocking collectives, per_device(): back = lax.all_gather(back, FEAT, axis=0)  25.6 us
    ppermute x9, waiting for transfers between devices, swap(): lax.ppermute(array, axis, [(i, i ^ 1 << bit) for i in range(lax.axis_size...  15.9 us
    all_to_all x1, starting transfers between devices, per_device(): total = lax.all_to_all(total.reshape(nz, count, db), 'z', 0, 0, tiled=True)  11.7 us
    pallas_call x1, Pallas kernels, ffn_call(): pl.pallas_call(functools.partial(ffn_body, kinds, rows, rank), out_shape=...  6.82 us
    all_to_all x1, starting transfers between devices, per_device(): back = lax.all_to_all(back.reshape(nz, count, rank), 'z', 0, 0, tiled=True)  6.39 us
  transfers between devices with their start and end apart: 11, of which 3 were waited for; matrix products, arithmetic and copies ran while one was open for 1% of the time, Pallas kernels for 2%

profile of v6, /device:TPU:1, one launch (start us, length us, event | category | flops | bytes accessed | tf_op | source)
XLA Modules:
  0.0 189.6 jit_solution(6453002980461820985)
XLA Ops:
  0.0 0.0 copy-start
  0.0 2.7 %pack.1.mine_in.refs_5_ = bf16[1152,768]{1,0:T(8,128)(2,1)} custom-call(bf16[480,768]{1,0:T(8,128)(2,1)} %bitcast.18, bf16[480,768]{1,0:T(8,128)(2,1)} %bitcast.19, bf16[96,512]{1,0:T(8,128)(2,1)} %bitcast.21, bf16[96,512]{1,0:T(8,128)(2,1)} %bitcast.22), custom_call_target="tpu_custom_call" | custom-call | tf_op jit(solution)/shard_map/pack/pallas_call | solution.py:165
  2.7 0.0 copy-start.2
  2.7 0.0 copy-start.1
  2.7 4.2 %collective-permute-start = (bf16[1152,768]{1,0:T(8,128)(2,1)}, bf16[1152,768]{1,0:T(8,128)(2,1)}, u32[]{:S(2)}, u32[]{:S(2)}) collective-permute-start(bf16[1152,768]{1,0:T(8,128)(2,1)} %pack.1.mine_in.refs_5_), channel_id=1, source_target_pairs={{0,16},{16,0},{1,17},{17,1},{2,18},{18,2},{3,19},{19,3},{4,20},{20... | collective-permute-start | bytes 5308424 | tf_op jit(solution)/shard_map/ppermute | solution.py:19
  6.9 2.1 %code_part.1 = bf16[16,16,512]{2,1,0:T(8,128)(2,1)} custom-call(bf16[16,768]{1,0:T(8,128)(2,1)} %x.1, bf16[768,512]{1,0:T(8,128)(2,1)} %w.1), custom_call_target="tpu_custom_call" | custom-call | tf_op jit(solution)/shard_map/code_part/pallas_call | solution.py:183
  9.0 42.5 %all_to_all.15 = bf16[16,16,512]{2,1,0:T(8,128)(2,1)S(1)} all-to-all(bf16[16,16,512]{2,1,0:T(8,128)(2,1)} %code_part.1), channel_id=1, replica_groups=mesh['z'=16,'yl'=2,'x'=4,'yh'=2,'c'=2] {'x','yh','c'}, dimensions={0} | all-to-all | bytes 524288 | tf_op jit(solution)/shard_map/all_to_all | solution.py:196
  51.5 0.0 copy-done.2
  51.5 32.3 %all_gather.7.gathered = bf16[256,1280]{1,0:T(8,128)(2,1)S(1)} all-gather(bf16[16,1280]{1,0:T(8,128)(2,1)S(1)} %pad_maximum_fusion), channel_id=1, replica_groups=mesh['z'=16,'yl'=2,'x'=4,'yh'=2,'c'=2] {'z'}, dimensions={0}, use_global_device_ids=true | all-gather | bytes 696320 | tf_op jit(solution)/shard_map/all_gather | solution.py:199
  83.8 4.7 %collective-permute-start.4 = (bf16[256,768]{1,0:T(8,128)(2,1)S(1)}, bf16[256,768]{1,0:T(8,128)(2,1)S(1)}, u32[]{:S(2)}, u32[]{:S(2)}) collective-permute-start(bf16[256,768]{1,0:T(8,128)(2,1)S(1)} %slice.4), channel_id=1, source_target_pairs={{0,8},{4,12},{8,0},{12,4},{1,9},{5,13},{9,1},{13,5},{2,10},{6,14},... | collective-permute-start | bytes 1179656 | tf_op jit(solution)/shard_map/ppermute | solution.py:19
  88.5 2.2 %collective-permute-start.3 = (bf16[256,768]{1,0:T(8,128)(2,1)S(1)}, bf16[256,768]{1,0:T(8,128)(2,1)S(1)}, u32[]{:S(2)}, u32[]{:S(2)}) collective-permute-start(bf16[256,768]{1,0:T(8,128)(2,1)S(1)} %slice.4), channel_id=1, source_target_pairs={{0,4},{4,0},{8,12},{12,8},{1,5},{5,1},{9,13},{13,9},{2,6},{6,2},{1... | collective-permute-start | bytes 1179656 | tf_op jit(solution)/shard_map/ppermute | solution.py:19
  90.7 1.9 %collective-permute-start.2 = (bf16[256,768]{1,0:T(8,128)(2,1)S(1)}, bf16[256,768]{1,0:T(8,128)(2,1)S(1)}, u32[]{:S(2)}, u32[]{:S(2)}) collective-permute-start(bf16[256,768]{1,0:T(8,128)(2,1)S(1)} %slice.4), channel_id=1, source_target_pairs={{0,2},{2,0},{1,3},{3,1},{4,6},{6,4},{5,7},{7,5},{8,10},{10,8},{9,1... | collective-permute-start | bytes 1179656 | tf_op jit(solution)/shard_map/ppermute | solution.py:19
  92.6 10.7 %collective-permute-start.1 = (bf16[256,768]{1,0:T(8,128)(2,1)S(1)}, bf16[256,768]{1,0:T(8,128)(2,1)S(1)}, u32[]{:S(2)}, u32[]{:S(2)}) collective-permute-start(bf16[256,768]{1,0:T(8,128)(2,1)S(1)} %slice.4), channel_id=1, source_target_pairs={{0,1},{1,0},{2,3},{3,2},{4,5},{5,4},{6,7},{7,6},{8,9},{9,8},{10,11... | collective-permute-start | bytes 1179656 | tf_op jit(solution)/shard_map/ppermute | solution.py:19
  103.4 0.0 collective-permute-done.other_in.refs_6_
  103.4 0.0 copy-done.1
  103.4 1.9 %ffn_own.1.refs_0_ = f32[256,192]{1,0:T(8,128)S(1)} custom-call(bf16[256,1280]{1,0:T(8,128)(2,1)S(1)} %all_gather.7.gathered, bf16[1152,768]{1,0:T(8,128)(2,1)S(1)} %copy-done.1, bf16[1152,768]{1,0:T(8,128)(2,1)} %collective-permute-done.other_in.refs_6_), custom_call_target="tpu_custom_call" | custom-call | tf_op jit(solution)/shard_map/ffn_own/pallas_call | solution.py:66
  105.3 0.0 collective-permute-done.4.refs_4_
  105.3 0.0 collective-permute-done.3.refs_3_
  105.3 0.0 collective-permute-done.2.refs_2_
  105.4 0.0 collective-permute-done.1.refs_1_
  105.4 6.8 %ffn.1 = (f32[256,768]{1,0:T(8,128)}, bf16[256,768]{1,0:T(8,128)(2,1)}, bf16[256,768]{1,0:T(8,128)(2,1)}, bf16[256,768]{1,0:T(8,128)(2,1)}, bf16[256,768]{1,0:T(8,128)(2,1)}, /*index=5*/bf16[256,512]{1,0:T(8,128)(2,1)}) custom-call(f32[256,192]{1,0:T(8,128)S(1)} %ffn_own.1.refs_0_, bf16[256,768]{1,0:T(8,128)(2,1)S(1)} %collective-permute-done.1.refs_1_, ...), custom_call_target="tpu_custom_call" | custom-call | tf_op jit(solution)/shard_map/ffn/pallas_call | solution.py:133
  112.2 6.4 %all-to-all-start.2 = ((bf16[16,16,512]{2,1,0:T(8,128)(2,1)}), bf16[16,16,512]{2,1,0:T(8,128)(2,1)S(1)}, u32[]{:S(2)}, u32[]{:S(2)}) async-start(bf16[16,16,512]{2,1,0:T(8,128)(2,1)} %bitcast.20), calls=%async_computation.2 | async-start | bytes 524288 | tf_op jit(solution)/shard_map/all_to_all | solution.py:210
  118.6 7.1 %collective-permute-start.5 = (bf16[256,768]{1,0:T(8,128)(2,1)}, bf16[256,768]{1,0:T(8,128)(2,1)S(1)}, u32[]{:S(2)}, u32[]{:S(2)}) collective-permute-start(bf16[256,768]{1,0:T(8,128)(2,1)} %get-tuple-element.12), channel_id=1, source_target_pairs={{0,1},{1,0},{2,3},{3,2},{4,5},{5,4},{6,7},{7,6},{8,9},{9,8},{10,11... | collective-permute-start | bytes 1179656 | tf_op jit(solution)/shard_map/ppermute | solution.py:19
  125.7 2.1 %collective-permute-start.6 = (bf16[256,768]{1,0:T(8,128)(2,1)}, bf16[256,768]{1,0:T(8,128)(2,1)S(1)}, u32[]{:S(2)}, u32[]{:S(2)}) collective-permute-start(bf16[256,768]{1,0:T(8,128)(2,1)} %get-tuple-element.13), channel_id=1, source_target_pairs={{0,2},{2,0},{1,3},{3,1},{4,6},{6,4},{5,7},{7,5},{8,10},{10,8},{9,1... | collective-permute-start | bytes 1179656 | tf_op jit(solution)/shard_map/ppermute | solution.py:19
  127.7 3.1 %collective-permute-start.7 = (bf16[256,768]{1,0:T(8,128)(2,1)}, bf16[256,768]{1,0:T(8,128)(2,1)S(1)}, u32[]{:S(2)}, u32[]{:S(2)}) collective-permute-start(bf16[256,768]{1,0:T(8,128)(2,1)} %get-tuple-element.14), channel_id=1, source_target_pairs={{0,4},{4,0},{8,12},{12,8},{1,5},{5,1},{9,13},{13,9},{2,6},{6,2},{1... | collective-permute-start | bytes 1179656 | tf_op jit(solution)/shard_map/ppermute | solution.py:19
  130.8 2.5 %collective-permute-start.8 = (bf16[256,768]{1,0:T(8,128)(2,1)}, bf16[256,768]{1,0:T(8,128)(2,1)S(1)}, u32[]{:S(2)}, u32[]{:S(2)}) collective-permute-start(bf16[256,768]{1,0:T(8,128)(2,1)} %get-tuple-element.15), channel_id=1, source_target_pairs={{0,8},{4,12},{8,0},{12,4},{1,9},{5,13},{9,1},{13,5},{2,10},{6,14},... | collective-permute-start | bytes 1179656 | tf_op jit(solution)/shard_map/ppermute | solution.py:19
  133.3 0.0 collective-permute-done.5
  133.3 6.6 %collective-permute-done.6 = bf16[256,768]{1,0:T(8,128)(2,1)S(1)} collective-permute-done((bf16[256,768]{1,0:T(8,128)(2,1)}, bf16[256,768]{1,0:T(8,128)(2,1)S(1)}, u32[]{:S(2)}, u32[]{:S(2)}) %collective-permute-start.6) | collective-permute-done | bytes 393248 | tf_op jit(solution)/shard_map/ppermute | solution.py:19
  140.0 0.3 collective-permute-done.7
  140.2 9.0 %collective-permute-done.8 = bf16[256,768]{1,0:T(8,128)(2,1)S(1)} collective-permute-done((bf16[256,768]{1,0:T(8,128)(2,1)}, bf16[256,768]{1,0:T(8,128)(2,1)S(1)}, u32[]{:S(2)}, u32[]{:S(2)}) %collective-permute-start.8) | collective-permute-done | bytes 393248 | tf_op jit(solution)/shard_map/ppermute | solution.py:19
  149.2 2.1 %add_convert_fusion = bf16[256,768]{1,0:T(8,128)(2,1)} fusion(bf16[256,768]{1,0:T(8,128)(2,1)S(1)} %collective-permute-done.8, bf16[256,768]{1,0:T(8,128)(2,1)S(1)} %collective-permute-done.7, bf16[256,768]{1,0:T(8,128)(2,1)S(1)} %collective-permute-done.6, f32[256,768]{1,0:T(8,128)} %get-tuple-element.11, bf16[256,768]{1,0:T(8,128)(2,1)S(1)} %collective-permute-done.5), kind=kLoop, calls=%fused_computation.3 | loop fusion | flops 1769472 | bytes 2752512 | tf_op jit(solution)/shard_map/convert_element_type | solution.py:214
  151.3 0.0 all-to-all-done.2
  151.3 11.7 %all-to-all-start.1 = ((bf16[16,16,768]{2,1,0:T(8,128)(2,1)}), bf16[16,16,768]{2,1,0:T(8,128)(2,1)S(1)}, u32[]{:S(2)}, u32[]{:S(2)}) async-start(bf16[16,16,768]{2,1,0:T(8,128)(2,1)} %bitcast.8), calls=%async_computation.1 | async-start | bytes 786432 | tf_op jit(solution)/shard_map/all_to_all | solution.py:215
  163.1 25.6 %all-gather = bf16[256,512]{1,0:T(8,128)(2,1)S(1)} all-gather(bf16[16,512]{1,0:T(8,128)(2,1)S(1)} %reduce-precision_convert_fusion.1), channel_id=2, replica_groups=mesh['z'=16,'yl'=2,'x'=4,'yh'=2,'c'=2] {'x','yh','c'}, dimensions={0}, use_global_device_ids=true | all-gather | bytes 278528 | tf_op jit(solution)/shard_map/all_gather | solution.py:217
  188.7 0.0 all-to-all-done.1
  188.7 0.1 convert_reduce_fusion
  188.8 0.0 copy-done
  188.8 0.8 fusion
  (7 shorter events, 0.2 us)
Async XLA Ops:
  0.0 188.8 %copy-start = (bf16[512,768]{1,0:T(8,128)(2,1)S(1)}, bf16[512,768]{1,0:T(8,128)(2,1)}, u32[]{:S(2)}) copy-start(bf16[512,768]{1,0:T(8,128)(2,1)} %param.13) | copy-start | bytes 2359300
  2.7 48.8 %copy-start.2 = (bf16[16,768]{1,0:T(8,128)(2,1)S(1)}, bf16[16,768]{1,0:T(8,128)(2,1)}, u32[]{:S(2)}) copy-start(bf16[16,768]{1,0:T(8,128)(2,1)} %x.1) | copy-start | bytes 73732
  2.7 100.7 %copy-start.1 = (bf16[1152,768]{1,0:T(8,128)(2,1)S(1)}, bf16[1152,768]{1,0:T(8,128)(2,1)}, u32[]{:S(2)}) copy-start(bf16[1152,768]{1,0:T(8,128)(2,1)} %pack.1.mine_in.refs_5_) | copy-start | bytes 5308420
  2.7 100.7 %collective-permute-start = (bf16[1152,768]{1,0:T(8,128)(2,1)}, bf16[1152,768]{1,0:T(8,128)(2,1)}, u32[]{:S(2)}, u32[]{:S(2)}) collective-permute-start(bf16[1152,768]{1,0:T(8,128)(2,1)} %pack.1.mine_in.refs_5_), channel_id=1, source_target_pairs={{0,16},{16,0},{1,17},{17,1},{2,18},{18,2},{3,19},{19,3},{4,20},{20... | collective-permute-start | bytes 5308424 | tf_op jit(solution)/shard_map/ppermute | solution.py:19
  83.8 21.5 %collective-permute-start.4 = (bf16[256,768]{1,0:T(8,128)(2,1)S(1)}, bf16[256,768]{1,0:T(8,128)(2,1)S(1)}, u32[]{:S(2)}, u32[]{:S(2)}) collective-permute-start(bf16[256,768]{1,0:T(8,128)(2,1)S(1)} %slice.4), channel_id=1, source_target_pairs={{0,8},{4,12},{8,0},{12,4},{1,9},{5,13},{9,1},{13,5},{2,10},{6,14},... | collective-permute-start | bytes 1179656 | tf_op jit(solution)/shard_map/ppermute | solution.py:19
  88.5 16.8 %collective-permute-start.3 = (bf16[256,768]{1,0:T(8,128)(2,1)S(1)}, bf16[256,768]{1,0:T(8,128)(2,1)S(1)}, u32[]{:S(2)}, u32[]{:S(2)}) collective-permute-start(bf16[256,768]{1,0:T(8,128)(2,1)S(1)} %slice.4), channel_id=1, source_target_pairs={{0,4},{4,0},{8,12},{12,8},{1,5},{5,1},{9,13},{13,9},{2,6},{6,2},{1... | collective-permute-start | bytes 1179656 | tf_op jit(solution)/shard_map/ppermute | solution.py:19
  90.7 14.6 %collective-permute-start.2 = (bf16[256,768]{1,0:T(8,128)(2,1)S(1)}, bf16[256,768]{1,0:T(8,128)(2,1)S(1)}, u32[]{:S(2)}, u32[]{:S(2)}) collective-permute-start(bf16[256,768]{1,0:T(8,128)(2,1)S(1)} %slice.4), channel_id=1, source_target_pairs={{0,2},{2,0},{1,3},{3,1},{4,6},{6,4},{5,7},{7,5},{8,10},{10,8},{9,1... | collective-permute-start | bytes 1179656 | tf_op jit(solution)/shard_map/ppermute | solution.py:19
  92.6 12.7 %collective-permute-start.1 = (bf16[256,768]{1,0:T(8,128)(2,1)S(1)}, bf16[256,768]{1,0:T(8,128)(2,1)S(1)}, u32[]{:S(2)}, u32[]{:S(2)}) collective-permute-start(bf16[256,768]{1,0:T(8,128)(2,1)S(1)} %slice.4), channel_id=1, source_target_pairs={{0,1},{1,0},{2,3},{3,2},{4,5},{5,4},{6,7},{7,6},{8,9},{9,8},{10,11... | collective-permute-start | bytes 1179656 | tf_op jit(solution)/shard_map/ppermute | solution.py:19
  112.2 39.1 %all-to-all-start.2 = ((bf16[16,16,512]{2,1,0:T(8,128)(2,1)}), bf16[16,16,512]{2,1,0:T(8,128)(2,1)S(1)}, u32[]{:S(2)}, u32[]{:S(2)}) async-start(bf16[16,16,512]{2,1,0:T(8,128)(2,1)} %bitcast.20), calls=%async_computation.2 | async-start | bytes 524288 | tf_op jit(solution)/shard_map/all_to_all | solution.py:210
  118.6 14.7 %collective-permute-start.5 = (bf16[256,768]{1,0:T(8,128)(2,1)}, bf16[256,768]{1,0:T(8,128)(2,1)S(1)}, u32[]{:S(2)}, u32[]{:S(2)}) collective-permute-start(bf16[256,768]{1,0:T(8,128)(2,1)} %get-tuple-element.12), channel_id=1, source_target_pairs={{0,1},{1,0},{2,3},{3,2},{4,5},{5,4},{6,7},{7,6},{8,9},{9,8},{10,11... | collective-permute-start | bytes 1179656 | tf_op jit(solution)/shard_map/ppermute | solution.py:19
  125.7 14.3 %collective-permute-start.6 = (bf16[256,768]{1,0:T(8,128)(2,1)}, bf16[256,768]{1,0:T(8,128)(2,1)S(1)}, u32[]{:S(2)}, u32[]{:S(2)}) collective-permute-start(bf16[256,768]{1,0:T(8,128)(2,1)} %get-tuple-element.13), channel_id=1, source_target_pairs={{0,2},{2,0},{1,3},{3,1},{4,6},{6,4},{5,7},{7,5},{8,10},{10,8},{9,1... | collective-permute-start | bytes 1179656 | tf_op jit(solution)/shard_map/ppermute | solution.py:19
  127.7 12.5 %collective-permute-start.7 = (bf16[256,768]{1,0:T(8,128)(2,1)}, bf16[256,768]{1,0:T(8,128)(2,1)S(1)}, u32[]{:S(2)}, u32[]{:S(2)}) collective-permute-start(bf16[256,768]{1,0:T(8,128)(2,1)} %get-tuple-element.14), channel_id=1, source_target_pairs={{0,4},{4,0},{8,12},{12,8},{1,5},{5,1},{9,13},{13,9},{2,6},{6,2},{1... | collective-permute-start | bytes 1179656 | tf_op jit(solution)/shard_map/ppermute | solution.py:19
  130.8 18.4 %collective-permute-start.8 = (bf16[256,768]{1,0:T(8,128)(2,1)}, bf16[256,768]{1,0:T(8,128)(2,1)S(1)}, u32[]{:S(2)}, u32[]{:S(2)}) collective-permute-start(bf16[256,768]{1,0:T(8,128)(2,1)} %get-tuple-element.15), channel_id=1, source_target_pairs={{0,8},{4,12},{8,0},{12,4},{1,9},{5,13},{9,1},{13,5},{2,10},{6,14},... | collective-permute-start | bytes 1179656 | tf_op jit(solution)/shard_map/ppermute | solution.py:19
  151.3 37.4 %all-to-all-start.1 = ((bf16[16,16,768]{2,1,0:T(8,128)(2,1)}), bf16[16,16,768]{2,1,0:T(8,128)(2,1)S(1)}, u32[]{:S(2)}, u32[]{:S(2)}) async-start(bf16[16,16,768]{2,1,0:T(8,128)(2,1)} %bitcast.8), calls=%async_computation.1 | async-start | bytes 786432 | tf_op jit(solution)/shard_map/all_to_all | solution.py:215

commit v7 on v5

--- a/solution.py
+++ b/solution.py
@@ -27,6 +27,11 @@
     return lax.dot_general(a, b, (((1,), (0,)), ((), ())), preferred_element_type=F32)
 
 
+def share(array, axis):
+    n = lax.axis_size(axis)
+    return lax.all_to_all(jnp.broadcast_to(array[None], (n,) + array.shape), axis, 0, 0, tiled=True)
+
+
 def total_of(stack):
     return lax.reduce_precision(jnp.sum(stack.astype(F32), axis=0), 8, 7).astype(BF16)
 
@@ -38,11 +43,11 @@
 
 def ffn_body(kinds, rows, rank, *refs):
     n = kinds * rows
-    count = kinds + 2
+    count = kinds + 3
     ins, outs = refs[:count], refs[count : count + kinds + 1]
     bufs, stage = refs[count + kinds + 1 : 2 * count + kinds + 1], refs[2 * count + kinds + 1 : -2]
     sems, out_sems = refs[-2:]
-    xs, (mine, other) = bufs[:kinds], bufs[kinds:]
+    xs, (code, mine, other) = bufs[:kinds], bufs[kinds:]
     db = mine.shape[1]
     head = db - rank
 
@@ -56,12 +61,13 @@
 
     first = [part(0, 0, 0, xs[0].shape[0])]
     late = []
-    for i in (kinds, kinds + 1):
-        first.append(part(i, i, 2 * n, 2 * rows))
-        first.append(part(i, i + 2, 0, n))
+    for i in (kinds + 1, kinds + 2):
+        first.append(part(i, i, 0, n))
+        late.append(part(i, i + 2, 2 * n, 2 * rows))
         late.append(part(i, i + 4, n, n))
     partners = [part(i, i, 0, xs[i].shape[0]) for i in range(1, kinds)]
-    for copy in first + partners + late:
+    last = part(kinds, kinds, 0, code.shape[0])
+    for copy in (*first, *partners, *late, last):
         copy.start()
     for copy in first:
         copy.wait()
@@ -69,18 +75,18 @@
     def both(lo, hi, at, size):
         return jnp.concatenate([ref[lo:hi, at : at + size] for ref in (mine, other)], axis=0)
 
-    pre = dot_nt(xs[0][:, db:], both(2 * n, 2 * n + rows, 0, rank))
-    pre = pre + dot_nt(xs[0][:, :db], both(0, rows, 0, db))
+    pre = dot_nt(xs[0][...], both(0, rows, 0, db))
     for k in range(1, kinds):
         partners[k - 1].wait()
         pre = pre + dot_nt(xs[k][...], both(k * rows, (k + 1) * rows, 0, db))
+    for copy in (*late, last):
+        copy.wait()
+    pre = pre + dot_nt(code[...], both(2 * n, 2 * n + rows, 0, rank))
     hidden = (0.5 * pre * (1.0 + lax.erf(pre * (0.5**0.5)))).astype(BF16)
     back = stage[kinds]
     back[:, :head] = dot_nn(hidden, both(2 * n, 2 * n + rows, rank, head)).astype(BF16)
     back[:, head:] = dot_nn(hidden, both(2 * n + rows, 2 * n + 2 * rows, 0, rank - head)).astype(BF16)
     stores = [stored(kinds)]
-    for copy in late:
-        copy.wait()
     for k in range(kinds):
         lo = n + k * rows
         stage[k][...] = dot_nn(hidden, both(lo, lo + rows, 0, db)).astype(outs[k].dtype)
@@ -89,12 +95,11 @@
         copy.wait()
 
 
-def ffn_call(gathered, pieces, mine, other, kinds):
-    count, width = gathered.shape
-    db = mine.shape[1]
-    rank = width - db
+def ffn_call(pieces, code, mine, other):
+    count, rank = code.shape
+    db, kinds = mine.shape[1], len(pieces)
     rows = mine.shape[0] // (2 * kinds + 2)
-    args = (gathered, *pieces, mine, other)
+    args = (*pieces, code, mine, other)
     outs = [((count, db), F32)] + [((count, db), BF16)] * (kinds - 1) + [((count, rank), BF16)]
     return pl.pallas_call(
         functools.partial(ffn_body, kinds, rows, rank),
@@ -138,17 +143,6 @@
     )(up, down, right, left)
 
 
-def code_body(x, w, stack):
-    part = dot_nn(x[...], w[...]).astype(BF16)
-    for i in range(stack.shape[0]):
-        stack[i] = part
-
-
-def code_call(tokens, up_left, n):
-    shape = jax.ShapeDtypeStruct((n, tokens.shape[0], up_left.shape[1]), BF16)
-    return pl.pallas_call(code_body, out_shape=shape, name="code_part", compiler_params=pltpu.CompilerParams(vmem_limit_bytes=60 * 2**20))(tokens, up_left)
-
-
 def per_device(tokens, up_weight, down_weight, up_left, up_right, down_left, down_right):
     nz, nf = lax.axis_size("z"), lax.axis_size(FEAT)
     count, db = tokens.shape
@@ -157,18 +151,18 @@
     up = up_weight[0].transpose(1, 0, 2).reshape(kinds * rows, db)
     down = down_weight[0].transpose(1, 0, 2).reshape(kinds * rows, db)
 
+    own = lax.all_to_all(jnp.broadcast_to(tokens[None], (nz, count, db)), "z", 0, 0, tiled=True)
+    own = own.reshape(nz * count, db)
     packed = pack_call(up, down, up_right[0], down_left[0])
-    stack = code_call(tokens, up_left, nf)
-    stack = lax.all_to_all(stack, FEAT, 0, 0, tiled=True)
     other = swap(packed, "yl", 0)
-    mine = jnp.concatenate([tokens, total_of(stack)], axis=1)
-    gathered = lax.all_gather(mine, "z", axis=0, tiled=True)
-    own = gathered[:, :db]
-    pieces = []
+    part = dot_nn(own, up_left).astype(BF16)
+    part = lax.all_to_all(part.reshape(nf, nz * count // nf, rank), FEAT, 0, 0, tiled=True)
+    group = total_of(part)
+    code = share(group, FEAT).reshape(nz * count, rank)
+    pieces = [own]
     for axis, bit in LEVEL_AXES:
         pieces.append(swap(own, axis, bit))
-
-    own_total, *terms, back = ffn_call(gathered, pieces, packed, other, kinds)
+    own_total, *terms, back = ffn_call(pieces, code, packed, other)
     sent = []
     for part, (axis, bit) in zip(terms, LEVEL_AXES):
         sent.append(swap(part, axis, bit))

time: 191 us -> 171 us (0.90)
  blocking collectives: 100 us -> 25.2 us
  starting transfers between devices: 57.2 us -> 86.7 us
  waiting for transfers between devices: 17.2 us -> 41 us
  local copies, waits for them, and re-layouts: 0.04 us -> 2.34 us
  Pallas kernels: 12.4 us -> 10.2 us
    all_to_all x1 -> x0, blocking collectives: 42.5 us -> none  [per_device(): stack = lax.all_to_all(stack, FEAT, 0, 0, tiled=True)]
    all_to_all x0 -> x3, starting transfers between devices: none -> 34.4 us  [the longest x1 15.7 us: per_device(): lax.all_to_all(jnp.broadcast_to(tokens[None], (nz, count, db)), 'z', 0, 0...]
    all_gather x1 -> x0, blocking collectives: 32.3 us -> none  [per_device(): gathered = lax.all_gather(mine, 'z', axis=0, tiled=True)]
    all_to_all x0 -> x3, waiting for transfers between devices: none -> 25.2 us  [the longest x1 12.1 us: per_device(): lax.all_to_all(jnp.broadcast_to(tokens[None], (nz, count, db)), 'z', 0, 0...]
    ppermute x9, starting transfers between devices: 39 us -> 28.5 us  [swap(): lax.ppermute(array, axis, [(i, i ^ 1 << bit) for i in range(lax.axis_size...]
    all_to_all x1, starting transfers between devices: 6.39 us -> 11.8 us  [per_device(): back = lax.all_to_all(back.reshape(nz, count, rank), 'z', 0, 0, tiled=True)]
    broadcast_in_dim x0 -> x2, local copies, waits for them, and re-layouts: none -> 2.32 us  [the longest x1 1.61 us: per_device(): jnp.broadcast_to(tokens[None], (nz, count, db))]
    pallas_call x1 -> x0, Pallas kernels: 2.1 us -> none  [code_call(): pl.pallas_call(code_body, out_shape=shape, name='code_part', compiler_par...]
  transfers between devices with their start and end apart: 11 -> 14, of which waited for: 4 -> 7; matrix products, arithmetic and copies ran while one was open for 1% -> 2% of each run, Pallas kernels for 1% -> 2%
where the time goes in v7:
time: 171 us; the launch traced here: 170 us
  starting transfers between devices  86.7 us (51%)
  waiting for transfers between devices  41 us (24%)
  blocking collectives  25.2 us (15%)
  Pallas kernels  10.2 us (6%)
  other arithmetic  2.37 us (1%)
  local copies, waits for them, and re-layouts  2.34 us (1%)
  matrix products  1.89 us (1%)
    ppermute x9, starting transfers between devices, swap(): lax.ppermute(array, axis, [(i, i ^ 1 << bit) for i in range(lax.axis_size...  28.5 us
    all_gather x1, blocking collectives, per_device(): back = lax.all_gather(back, FEAT, axis=0)  25.2 us
    ppermute x9, waiting for transfers between devices, swap(): lax.ppermute(array, axis, [(i, i ^ 1 << bit) for i in range(lax.axis_size...  15.8 us
    all_to_all x1, starting transfers between devices, per_device(): lax.all_to_all(jnp.broadcast_to(tokens[None], (nz, count, db)), 'z', 0, 0...  15.7 us
    all_to_all x1, starting transfers between devices, per_device(): lax.all_to_all(part.reshape(nf, nz * count // nf, rank), FEAT, 0, 0, tile...  13.6 us
    all_to_all x1, waiting for transfers between devices, per_device(): lax.all_to_all(jnp.broadcast_to(tokens[None], (nz, count, db)), 'z', 0, 0...  12.1 us
    all_to_all x1, starting transfers between devices, per_device(): total = lax.all_to_all(total.reshape(nz, count, db), 'z', 0, 0, tiled=True)  12 us
    all_to_all x1, starting transfers between devices, per_device(): back = lax.all_to_all(back.reshape(nz, count, rank), 'z', 0, 0, tiled=True)  11.8 us
  transfers between devices with their start and end apart: 14, of which 7 were waited for; matrix products, arithmetic and copies ran while one was open for 2% of the time, Pallas kernels for 2%

profile of v7, /device:TPU:1, one launch (start us, length us, event | category | flops | bytes accessed | tf_op | source)
XLA Modules:
  0.0 169.9 jit_solution(16925747878934665703)
XLA Ops:
  0.0 0.0 copy-start
  0.0 1.6 broadcast_in_dim.4
  1.6 15.7 %all-to-all-start = ((bf16[16,16,768]{2,1,0:T(8,128)(2,1)}), bf16[16,16,768]{2,1,0:T(8,128)(2,1)S(1)}, u32[]{:S(2)}, u32[]{:S(2)}) async-start(bf16[16,16,768]{2,1,0:T(8,128)(2,1)} %broadcast_in_dim.4), calls=%async_computation | async-start | bytes 786432 | tf_op jit(solution)/shard_map/all_to_all | solution.py:154
  17.4 2.6 %pack.1.refs_6_ = bf16[1152,768]{1,0:T(8,128)(2,1)} custom-call(bf16[480,768]{1,0:T(8,128)(2,1)} %bitcast.30, bf16[480,768]{1,0:T(8,128)(2,1)} %bitcast.31, bf16[96,512]{1,0:T(8,128)(2,1)} %bitcast.33, bf16[96,512]{1,0:T(8,128)(2,1)} %bitcast.34), custom_call_target="tpu_custom_call" | custom-call | tf_op jit(solution)/shard_map/pack/pallas_call | solution.py:136
  20.0 0.0 copy-start.1
  20.0 3.3 %collective-permute-start.4 = (bf16[1152,768]{1,0:T(8,128)(2,1)}, bf16[1152,768]{1,0:T(8,128)(2,1)}, u32[]{:S(2)}, u32[]{:S(2)}) collective-permute-start(bf16[1152,768]{1,0:T(8,128)(2,1)} %pack.1.refs_6_), channel_id=1, source_target_pairs={{0,16},{16,0},{1,17},{17,1},{2,18},{18,2},{3,19},{19,3},{4,20},{20... | collective-permute-start | bytes 5308424 | tf_op jit(solution)/shard_map/ppermute | solution.py:19
  23.3 12.1 %all-to-all-done = bf16[16,16,768]{2,1,0:T(8,128)(2,1)S(1)} async-done(((bf16[16,16,768]{2,1,0:T(8,128)(2,1)}), bf16[16,16,768]{2,1,0:T(8,128)(2,1)S(1)}, u32[]{:S(2)}, u32[]{:S(2)}) %all-to-all-start) | async-done | bytes 393248 | tf_op jit(solution)/shard_map/all_to_all | solution.py:154
  35.5 0.0 copy-done
  35.5 1.1 convolution_convert_fusion
  36.5 13.6 %all-to-all-start.1 = ((bf16[16,16,512]{2,1,0:T(8,128)(2,1)}), bf16[16,16,512]{2,1,0:T(8,128)(2,1)S(1)}, u32[]{:S(2)}, u32[]{:S(2)}) async-start(bf16[16,16,512]{2,1,0:T(8,128)(2,1)} %bitcast.1), calls=%async_computation.1 | async-start | bytes 524288 | tf_op jit(solution)/shard_map/all_to_all | solution.py:159
  50.1 4.8 %collective-permute-start.3 = (bf16[256,768]{1,0:T(8,128)(2,1)S(1)}, bf16[256,768]{1,0:T(8,128)(2,1)}, u32[]{:S(2)}, u32[]{:S(2)}) collective-permute-start(bf16[256,768]{1,0:T(8,128)(2,1)S(1)} %bitcast.23), channel_id=1, source_target_pairs={{0,8},{4,12},{8,0},{12,4},{1,9},{5,13},{9,1},{13,5},{2,10},{6,14},... | collective-permute-start | bytes 1179656 | tf_op jit(solution)/shard_map/ppermute | solution.py:19
  54.9 2.2 %collective-permute-start.2 = (bf16[256,768]{1,0:T(8,128)(2,1)S(1)}, bf16[256,768]{1,0:T(8,128)(2,1)}, u32[]{:S(2)}, u32[]{:S(2)}) collective-permute-start(bf16[256,768]{1,0:T(8,128)(2,1)S(1)} %bitcast.24), channel_id=1, source_target_pairs={{0,4},{4,0},{8,12},{12,8},{1,5},{5,1},{9,13},{13,9},{2,6},{6,2},{1... | collective-permute-start | bytes 1179656 | tf_op jit(solution)/shard_map/ppermute | solution.py:19
  57.1 4.6 %collective-permute-start.1 = (bf16[256,768]{1,0:T(8,128)(2,1)S(1)}, bf16[256,768]{1,0:T(8,128)(2,1)}, u32[]{:S(2)}, u32[]{:S(2)}) collective-permute-start(bf16[256,768]{1,0:T(8,128)(2,1)S(1)} %bitcast.25), channel_id=1, source_target_pairs={{0,2},{2,0},{1,3},{3,1},{4,6},{6,4},{5,7},{7,5},{8,10},{10,8},{9,1... | collective-permute-start | bytes 1179656 | tf_op jit(solution)/shard_map/ppermute | solution.py:19
  61.7 3.1 %collective-permute-start = (bf16[256,768]{1,0:T(8,128)(2,1)S(1)}, bf16[256,768]{1,0:T(8,128)(2,1)}, u32[]{:S(2)}, u32[]{:S(2)}) collective-permute-start(bf16[256,768]{1,0:T(8,128)(2,1)S(1)} %bitcast.26), channel_id=1, source_target_pairs={{0,1},{1,0},{2,3},{3,2},{4,5},{5,4},{6,7},{7,6},{8,9},{9,8},{10,11... | collective-permute-start | bytes 1179656 | tf_op jit(solution)/shard_map/ppermute | solution.py:19
  64.8 4.4 %all-to-all-done.1 = bf16[16,16,512]{2,1,0:T(8,128)(2,1)S(1)} async-done(((bf16[16,16,512]{2,1,0:T(8,128)(2,1)}), bf16[16,16,512]{2,1,0:T(8,128)(2,1)S(1)}, u32[]{:S(2)}, u32[]{:S(2)}) %all-to-all-start.1) | async-done | bytes 262176 | tf_op jit(solution)/shard_map/all_to_all | solution.py:159
  69.3 0.7 broadcast_in_dim.5
  70.0 5.1 %all-to-all-start.2 = ((bf16[16,16,512]{2,1,0:T(8,128)(2,1)}), bf16[16,16,512]{2,1,0:T(8,128)(2,1)S(1)}, u32[]{:S(2)}, u32[]{:S(2)}) async-start(bf16[16,16,512]{2,1,0:T(8,128)(2,1)} %broadcast_in_dim.5), calls=%async_computation.2 | async-start | bytes 524288 | tf_op jit(solution)/shard_map/all_to_all | solution.py:32
  75.1 0.0 collective-permute-done.4.refs_7_
  75.1 0.0 collective-permute-done.3.refs_4_
  75.1 0.0 collective-permute-done.2.refs_3_
  75.1 0.1 collective-permute-done.1.refs_2_
  75.2 0.0 collective-permute-done.refs_1_
  75.2 8.7 %all-to-all-done.2 = bf16[16,16,512]{2,1,0:T(8,128)(2,1)S(1)} async-done(((bf16[16,16,512]{2,1,0:T(8,128)(2,1)}), bf16[16,16,512]{2,1,0:T(8,128)(2,1)S(1)}, u32[]{:S(2)}, u32[]{:S(2)}) %all-to-all-start.2) | async-done | bytes 262176 | tf_op jit(solution)/shard_map/all_to_all | solution.py:32
  83.9 0.0 copy-done.1
  83.9 7.6 %ffn.1 = (f32[256,768]{1,0:T(8,128)}, bf16[256,768]{1,0:T(8,128)(2,1)}, bf16[256,768]{1,0:T(8,128)(2,1)}, bf16[256,768]{1,0:T(8,128)(2,1)}, bf16[256,768]{1,0:T(8,128)(2,1)}, /*index=5*/bf16[256,512]{1,0:T(8,128)(2,1)}) custom-call(bf16[256,768]{1,0:T(8,128)(2,1)S(1)} %bitcast.27, bf16[256,768]{1,0:T(8,128)(2,1)} %collective-permute-done.refs_1_, ...), custom_call_target="tpu_custom_call" | custom-call | tf_op jit(solution)/shard_map/ffn/pallas_call | solution.py:104
  91.6 11.8 %all-to-all-start.4 = ((bf16[16,16,512]{2,1,0:T(8,128)(2,1)}), bf16[16,16,512]{2,1,0:T(8,128)(2,1)S(1)}, u32[]{:S(2)}, u32[]{:S(2)}) async-start(bf16[16,16,512]{2,1,0:T(8,128)(2,1)} %bitcast.32), calls=%async_computation.4 | async-start | bytes 524288 | tf_op jit(solution)/shard_map/all_to_all | solution.py:169
  103.3 2.6 %collective-permute-start.5 = (bf16[256,768]{1,0:T(8,128)(2,1)}, bf16[256,768]{1,0:T(8,128)(2,1)S(1)}, u32[]{:S(2)}, u32[]{:S(2)}) collective-permute-start(bf16[256,768]{1,0:T(8,128)(2,1)} %get-tuple-element.12), channel_id=1, source_target_pairs={{0,1},{1,0},{2,3},{3,2},{4,5},{5,4},{6,7},{7,6},{8,9},{9,8},{10,11... | collective-permute-start | bytes 1179656 | tf_op jit(solution)/shard_map/ppermute | solution.py:19
  105.9 2.3 %collective-permute-start.6 = (bf16[256,768]{1,0:T(8,128)(2,1)}, bf16[256,768]{1,0:T(8,128)(2,1)S(1)}, u32[]{:S(2)}, u32[]{:S(2)}) collective-permute-start(bf16[256,768]{1,0:T(8,128)(2,1)} %get-tuple-element.13), channel_id=1, source_target_pairs={{0,2},{2,0},{1,3},{3,1},{4,6},{6,4},{5,7},{7,5},{8,10},{10,8},{9,1... | collective-permute-start | bytes 1179656 | tf_op jit(solution)/shard_map/ppermute | solution.py:19
  108.2 1.9 %collective-permute-start.7 = (bf16[256,768]{1,0:T(8,128)(2,1)}, bf16[256,768]{1,0:T(8,128)(2,1)S(1)}, u32[]{:S(2)}, u32[]{:S(2)}) collective-permute-start(bf16[256,768]{1,0:T(8,128)(2,1)} %get-tuple-element.14), channel_id=1, source_target_pairs={{0,4},{4,0},{8,12},{12,8},{1,5},{5,1},{9,13},{13,9},{2,6},{6,2},{1... | collective-permute-start | bytes 1179656 | tf_op jit(solution)/shard_map/ppermute | solution.py:19
  110.1 3.8 %collective-permute-start.8 = (bf16[256,768]{1,0:T(8,128)(2,1)}, bf16[256,768]{1,0:T(8,128)(2,1)S(1)}, u32[]{:S(2)}, u32[]{:S(2)}) collective-permute-start(bf16[256,768]{1,0:T(8,128)(2,1)} %get-tuple-element.15), channel_id=1, source_target_pairs={{0,8},{4,12},{8,0},{12,4},{1,9},{5,13},{9,1},{13,5},{2,10},{6,14},... | collective-permute-start | bytes 1179656 | tf_op jit(solution)/shard_map/ppermute | solution.py:19
  113.9 0.0 collective-permute-done.5
  113.9 6.3 %collective-permute-done.6 = bf16[256,768]{1,0:T(8,128)(2,1)S(1)} collective-permute-done((bf16[256,768]{1,0:T(8,128)(2,1)}, bf16[256,768]{1,0:T(8,128)(2,1)S(1)}, u32[]{:S(2)}, u32[]{:S(2)}) %collective-permute-start.6) | collective-permute-done | bytes 393248 | tf_op jit(solution)/shard_map/ppermute | solution.py:19
  120.2 0.4 collective-permute-done.7
  120.6 9.0 %collective-permute-done.8 = bf16[256,768]{1,0:T(8,128)(2,1)S(1)} collective-permute-done((bf16[256,768]{1,0:T(8,128)(2,1)}, bf16[256,768]{1,0:T(8,128)(2,1)S(1)}, u32[]{:S(2)}, u32[]{:S(2)}) %collective-permute-start.8) | collective-permute-done | bytes 393248 | tf_op jit(solution)/shard_map/ppermute | solution.py:19
  129.5 0.0 copy-start.2
  129.5 2.2 %add_convert_fusion = bf16[256,768]{1,0:T(8,128)(2,1)} fusion(bf16[256,768]{1,0:T(8,128)(2,1)S(1)} %collective-permute-done.8, bf16[256,768]{1,0:T(8,128)(2,1)S(1)} %collective-permute-done.7, bf16[256,768]{1,0:T(8,128)(2,1)S(1)} %collective-permute-done.6, f32[256,768]{1,0:T(8,128)} %get-tuple-element.11, bf16[256,768]{1,0:T(8,128)(2,1)S(1)} %collective-permute-done.5), kind=kLoop, calls=%fused_computation.4 | loop fusion | flops 1769472 | bytes 2752512 | tf_op jit(solution)/shard_map/convert_element_type | solution.py:173
  131.7 0.0 all-to-all-done.4
  131.7 12.0 %all-to-all-start.3 = ((bf16[16,16,768]{2,1,0:T(8,128)(2,1)}), bf16[16,16,768]{2,1,0:T(8,128)(2,1)S(1)}, u32[]{:S(2)}, u32[]{:S(2)}) async-start(bf16[16,16,768]{2,1,0:T(8,128)(2,1)} %bitcast.11), calls=%async_computation.3 | async-start | bytes 786432 | tf_op jit(solution)/shard_map/all_to_all | solution.py:174
  143.8 25.2 %all-gather = bf16[256,512]{1,0:T(8,128)(2,1)S(1)} all-gather(bf16[16,512]{1,0:T(8,128)(2,1)S(1)} %reduce-precision_convert_fusion.1), channel_id=2, replica_groups=mesh['z'=16,'yl'=2,'x'=4,'yh'=2,'c'=2] {'x','yh','c'}, dimensions={0}, use_global_device_ids=true | all-gather | bytes 278528 | tf_op jit(solution)/shard_map/all_gather | solution.py:176
  169.0 0.0 all-to-all-done.3
  169.0 0.1 convert_reduce_fusion
  169.1 0.0 copy-done.2
  169.1 0.8 fusion
  (5 shorter events, 0.1 us)
Async XLA Ops:
  0.0 35.5 %copy-start = (bf16[768,512]{1,0:T(8,128)(2,1)S(1)}, bf16[768,512]{1,0:T(8,128)(2,1)}, u32[]{:S(2)}) copy-start(bf16[768,512]{1,0:T(8,128)(2,1)} %param.10) | copy-start | bytes 2359300
  1.6 33.8 %all-to-all-start = ((bf16[16,16,768]{2,1,0:T(8,128)(2,1)}), bf16[16,16,768]{2,1,0:T(8,128)(2,1)S(1)}, u32[]{:S(2)}, u32[]{:S(2)}) async-start(bf16[16,16,768]{2,1,0:T(8,128)(2,1)} %broadcast_in_dim.4), calls=%async_computation | async-start | bytes 786432 | tf_op jit(solution)/shard_map/all_to_all | solution.py:154
  20.0 64.0 %copy-start.1 = (bf16[1152,768]{1,0:T(8,128)(2,1)S(1)}, bf16[1152,768]{1,0:T(8,128)(2,1)}, u32[]{:S(2)}) copy-start(bf16[1152,768]{1,0:T(8,128)(2,1)} %pack.1.refs_6_) | copy-start | bytes 5308420
  20.0 55.1 %collective-permute-start.4 = (bf16[1152,768]{1,0:T(8,128)(2,1)}, bf16[1152,768]{1,0:T(8,128)(2,1)}, u32[]{:S(2)}, u32[]{:S(2)}) collective-permute-start(bf16[1152,768]{1,0:T(8,128)(2,1)} %pack.1.refs_6_), channel_id=1, source_target_pairs={{0,16},{16,0},{1,17},{17,1},{2,18},{18,2},{3,19},{19,3},{4,20},{20... | collective-permute-start | bytes 5308424 | tf_op jit(solution)/shard_map/ppermute | solution.py:19
  36.5 32.7 %all-to-all-start.1 = ((bf16[16,16,512]{2,1,0:T(8,128)(2,1)}), bf16[16,16,512]{2,1,0:T(8,128)(2,1)S(1)}, u32[]{:S(2)}, u32[]{:S(2)}) async-start(bf16[16,16,512]{2,1,0:T(8,128)(2,1)} %bitcast.1), calls=%async_computation.1 | async-start | bytes 524288 | tf_op jit(solution)/shard_map/all_to_all | solution.py:159
  50.1 25.0 %collective-permute-start.3 = (bf16[256,768]{1,0:T(8,128)(2,1)S(1)}, bf16[256,768]{1,0:T(8,128)(2,1)}, u32[]{:S(2)}, u32[]{:S(2)}) collective-permute-start(bf16[256,768]{1,0:T(8,128)(2,1)S(1)} %bitcast.23), channel_id=1, source_target_pairs={{0,8},{4,12},{8,0},{12,4},{1,9},{5,13},{9,1},{13,5},{2,10},{6,14},... | collective-permute-start | bytes 1179656 | tf_op jit(solution)/shard_map/ppermute | solution.py:19
  54.9 20.2 %collective-permute-start.2 = (bf16[256,768]{1,0:T(8,128)(2,1)S(1)}, bf16[256,768]{1,0:T(8,128)(2,1)}, u32[]{:S(2)}, u32[]{:S(2)}) collective-permute-start(bf16[256,768]{1,0:T(8,128)(2,1)S(1)} %bitcast.24), channel_id=1, source_target_pairs={{0,4},{4,0},{8,12},{12,8},{1,5},{5,1},{9,13},{13,9},{2,6},{6,2},{1... | collective-permute-start | bytes 1179656 | tf_op jit(solution)/shard_map/ppermute | solution.py:19
  57.1 18.2 %collective-permute-start.1 = (bf16[256,768]{1,0:T(8,128)(2,1)S(1)}, bf16[256,768]{1,0:T(8,128)(2,1)}, u32[]{:S(2)}, u32[]{:S(2)}) collective-permute-start(bf16[256,768]{1,0:T(8,128)(2,1)S(1)} %bitcast.25), channel_id=1, source_target_pairs={{0,2},{2,0},{1,3},{3,1},{4,6},{6,4},{5,7},{7,5},{8,10},{10,8},{9,1... | collective-permute-start | bytes 1179656 | tf_op jit(solution)/shard_map/ppermute | solution.py:19
  61.7 13.6 %collective-permute-start = (bf16[256,768]{1,0:T(8,128)(2,1)S(1)}, bf16[256,768]{1,0:T(8,128)(2,1)}, u32[]{:S(2)}, u32[]{:S(2)}) collective-permute-start(bf16[256,768]{1,0:T(8,128)(2,1)S(1)} %bitcast.26), channel_id=1, source_target_pairs={{0,1},{1,0},{2,3},{3,2},{4,5},{5,4},{6,7},{7,6},{8,9},{9,8},{10,11... | collective-permute-start | bytes 1179656 | tf_op jit(solution)/shard_map/ppermute | solution.py:19
  70.0 13.9 %all-to-all-start.2 = ((bf16[16,16,512]{2,1,0:T(8,128)(2,1)}), bf16[16,16,512]{2,1,0:T(8,128)(2,1)S(1)}, u32[]{:S(2)}, u32[]{:S(2)}) async-start(bf16[16,16,512]{2,1,0:T(8,128)(2,1)} %broadcast_in_dim.5), calls=%async_computation.2 | async-start | bytes 524288 | tf_op jit(solution)/shard_map/all_to_all | solution.py:32
  91.6 40.1 %all-to-all-start.4 = ((bf16[16,16,512]{2,1,0:T(8,128)(2,1)}), bf16[16,16,512]{2,1,0:T(8,128)(2,1)S(1)}, u32[]{:S(2)}, u32[]{:S(2)}) async-start(bf16[16,16,512]{2,1,0:T(8,128)(2,1)} %bitcast.32), calls=%async_computation.4 | async-start | bytes 524288 | tf_op jit(solution)/shard_map/all_to_all | solution.py:169
  103.3 10.5 %collective-permute-start.5 = (bf16[256,768]{1,0:T(8,128)(2,1)}, bf16[256,768]{1,0:T(8,128)(2,1)S(1)}, u32[]{:S(2)}, u32[]{:S(2)}) collective-permute-start(bf16[256,768]{1,0:T(8,128)(2,1)} %get-tuple-element.12), channel_id=1, source_target_pairs={{0,1},{1,0},{2,3},{3,2},{4,5},{5,4},{6,7},{7,6},{8,9},{9,8},{10,11... | collective-permute-start | bytes 1179656 | tf_op jit(solution)/shard_map/ppermute | solution.py:19
  105.9 14.3 %collective-permute-start.6 = (bf16[256,768]{1,0:T(8,128)(2,1)}, bf16[256,768]{1,0:T(8,128)(2,1)S(1)}, u32[]{:S(2)}, u32[]{:S(2)}) collective-permute-start(bf16[256,768]{1,0:T(8,128)(2,1)} %get-tuple-element.13), channel_id=1, source_target_pairs={{0,2},{2,0},{1,3},{3,1},{4,6},{6,4},{5,7},{7,5},{8,10},{10,8},{9,1... | collective-permute-start | bytes 1179656 | tf_op jit(solution)/shard_map/ppermute | solution.py:19
  108.2 12.4 %collective-permute-start.7 = (bf16[256,768]{1,0:T(8,128)(2,1)}, bf16[256,768]{1,0:T(8,128)(2,1)S(1)}, u32[]{:S(2)}, u32[]{:S(2)}) collective-permute-start(bf16[256,768]{1,0:T(8,128)(2,1)} %get-tuple-element.14), channel_id=1, source_target_pairs={{0,4},{4,0},{8,12},{12,8},{1,5},{5,1},{9,13},{13,9},{2,6},{6,2},{1... | collective-permute-start | bytes 1179656 | tf_op jit(solution)/shard_map/ppermute | solution.py:19
  110.1 19.4 %collective-permute-start.8 = (bf16[256,768]{1,0:T(8,128)(2,1)}, bf16[256,768]{1,0:T(8,128)(2,1)S(1)}, u32[]{:S(2)}, u32[]{:S(2)}) collective-permute-start(bf16[256,768]{1,0:T(8,128)(2,1)} %get-tuple-element.15), channel_id=1, source_target_pairs={{0,8},{4,12},{8,0},{12,4},{1,9},{5,13},{9,1},{13,5},{2,10},{6,14},... | collective-permute-start | bytes 1179656 | tf_op jit(solution)/shard_map/ppermute | solution.py:19
  129.5 39.6 %copy-start.2 = (bf16[512,768]{1,0:T(8,128)(2,1)S(1)}, bf16[512,768]{1,0:T(8,128)(2,1)}, u32[]{:S(2)}) copy-start(bf16[512,768]{1,0:T(8,128)(2,1)} %param.13) | copy-start | bytes 2359300
  131.7 37.3 %all-to-all-start.3 = ((bf16[16,16,768]{2,1,0:T(8,128)(2,1)}), bf16[16,16,768]{2,1,0:T(8,128)(2,1)S(1)}, u32[]{:S(2)}, u32[]{:S(2)}) async-start(bf16[16,16,768]{2,1,0:T(8,128)(2,1)} %bitcast.11), calls=%async_computation.3 | async-start | bytes 786432 | tf_op jit(solution)/shard_map/all_to_all | solution.py:174

commit v8 on v5

--- a/solution.py
+++ b/solution.py
@@ -31,56 +31,41 @@
     return lax.reduce_precision(jnp.sum(stack.astype(F32), axis=0), 8, 7).astype(BF16)
 
 
-def fetch(src, dst, sem, lo, size):
-    part = pl.ds(lo, size)
-    return pltpu.make_async_copy(src.at[part], dst.at[part], sem)
-
-
 def ffn_body(kinds, rows, rank, *refs):
     n = kinds * rows
     count = kinds + 2
-    ins, outs = refs[:count], refs[count : count + kinds + 1]
-    bufs, stage = refs[count + kinds + 1 : 2 * count + kinds + 1], refs[2 * count + kinds + 1 : -2]
-    sems, out_sems = refs[-2:]
-    xs, (mine, other) = bufs[:kinds], bufs[kinds:]
+    xs, (mine, other_in), outs = refs[:kinds], refs[kinds:count], refs[count : count + kinds + 1]
+    stage, (other, sems, out_sems) = refs[count + kinds + 1 : -3], refs[-3:]
     db = mine.shape[1]
     head = db - rank
 
-    def part(i, sem, lo, size):
-        return fetch(ins[i], bufs[i], sems.at[sem], lo, size)
+    def fetch(sem, lo, size):
+        rows_of = pl.ds(lo, size)
+        copy = pltpu.make_async_copy(other_in.at[rows_of], other.at[rows_of], sems.at[sem])
+        copy.start()
+        return copy
 
     def stored(k):
         copy = pltpu.make_async_copy(stage[k], outs[k], out_sems.at[k])
         copy.start()
         return copy
 
-    first = [part(0, 0, 0, xs[0].shape[0])]
-    late = []
-    for i in (kinds, kinds + 1):
-        first.append(part(i, i, 2 * n, 2 * rows))
-        first.append(part(i, i + 2, 0, n))
-        late.append(part(i, i + 4, n, n))
-    partners = [part(i, i, 0, xs[i].shape[0]) for i in range(1, kinds)]
-    for copy in first + partners + late:
-        copy.start()
-    for copy in first:
-        copy.wait()
-
     def both(lo, hi, at, size):
         return jnp.concatenate([ref[lo:hi, at : at + size] for ref in (mine, other)], axis=0)
 
+    low_rank, ups, downs = fetch(0, 2 * n, 2 * rows), fetch(1, 0, n), fetch(2, n, n)
+    low_rank.wait()
     pre = dot_nt(xs[0][:, db:], both(2 * n, 2 * n + rows, 0, rank))
+    ups.wait()
     pre = pre + dot_nt(xs[0][:, :db], both(0, rows, 0, db))
     for k in range(1, kinds):
-        partners[k - 1].wait()
         pre = pre + dot_nt(xs[k][...], both(k * rows, (k + 1) * rows, 0, db))
     hidden = (0.5 * pre * (1.0 + lax.erf(pre * (0.5**0.5)))).astype(BF16)
     back = stage[kinds]
     back[:, :head] = dot_nn(hidden, both(2 * n, 2 * n + rows, rank, head)).astype(BF16)
     back[:, head:] = dot_nn(hidden, both(2 * n + rows, 2 * n + 2 * rows, 0, rank - head)).astype(BF16)
     stores = [stored(kinds)]
-    for copy in late:
-        copy.wait()
+    downs.wait()
     for k in range(kinds):
         lo = n + k * rows
         stage[k][...] = dot_nn(hidden, both(lo, lo + rows, 0, db)).astype(outs[k].dtype)
@@ -99,10 +84,10 @@
     return pl.pallas_call(
         functools.partial(ffn_body, kinds, rows, rank),
         out_shape=[pltpu.HBM(*a) for a in outs],
-        in_specs=[pl.BlockSpec(memory_space=pl.ANY)] * len(args),
-        scratch_shapes=[pltpu.VMEM(a.shape, BF16) for a in args]
-        + [pltpu.VMEM(*a) for a in outs]
-        + [pltpu.SemaphoreType.DMA((len(args) + 4,)), pltpu.SemaphoreType.DMA((len(outs),))],
+        out_specs=[pl.BlockSpec(memory_space=pl.ANY)] * len(outs),
+        in_specs=[pl.BlockSpec(memory_space=pltpu.VMEM)] * (len(args) - 1) + [pl.BlockSpec(memory_space=pl.ANY)],
+        scratch_shapes=[pltpu.VMEM(*a) for a in outs]
+        + [pltpu.VMEM(other.shape, BF16), pltpu.SemaphoreType.DMA((3,)), pltpu.SemaphoreType.DMA((len(outs),))],
         compiler_params=pltpu.CompilerParams(vmem_limit_bytes=FFN_MIB * 2**20),
         name="ffn",
     )(*args)

time: 191 us -> 189 us (0.990)
  Pallas kernels: 12.4 us -> 9.85 us
    pallas_call x1, Pallas kernels: 7.69 us -> 5.09 us  [ffn_call(): pl.pallas_call(functools.partial(ffn_body, kinds, rows, rank), out_shape=...]
where the time goes in v8:
time: 189 us; the launch traced here: 188 us
  blocking collectives  100 us (53%)
  starting transfers between devices  57.2 us (30%)
  waiting for transfers between devices  17.2 us (9%)
  Pallas kernels  9.85 us (5%)
  other arithmetic  2.3 us (1%)
    all_to_all x1, blocking collectives, per_device(): stack = lax.all_to_all(stack, FEAT, 0, 0, tiled=True)  42.5 us
    ppermute x9, starting transfers between devices, swap(): lax.ppermute(array, axis, [(i, i ^ 1 << bit) for i in range(lax.axis_size...  39 us
    all_gather x1, blocking collectives, per_device(): gathered = lax.all_gather(mine, 'z', axis=0, tiled=True)  32.3 us
    all_gather x1, blocking collectives, per_device(): back = lax.all_gather(back, FEAT, axis=0)  25.6 us
    ppermute x9, waiting for transfers between devices, swap(): lax.ppermute(array, axis, [(i, i ^ 1 << bit) for i in range(lax.axis_size...  17.2 us
    all_to_all x1, starting transfers between devices, per_device(): total = lax.all_to_all(total.reshape(nz, count, db), 'z', 0, 0, tiled=True)  11.7 us
    all_to_all x1, starting transfers between devices, per_device(): back = lax.all_to_all(back.reshape(nz, count, rank), 'z', 0, 0, tiled=True)  6.4 us
    pallas_call x1, Pallas kernels, ffn_call(): pl.pallas_call(functools.partial(ffn_body, kinds, rows, rank), out_shape=...  5.09 us
  transfers between devices with their start and end apart: 11, of which 4 were waited for; matrix products, arithmetic and copies ran while one was open for 1% of the time, Pallas kernels for 1%

profile of v8, /device:TPU:1, one launch (start us, length us, event | category | flops | bytes accessed | tf_op | source)
XLA Modules:
  0.0 187.9 jit_solution(10366079925014060830)
XLA Ops:
  0.0 0.0 copy-start
  0.0 2.7 %pack.1.refs_5_ = bf16[1152,768]{1,0:T(8,128)(2,1)} custom-call(bf16[480,768]{1,0:T(8,128)(2,1)} %bitcast.18, bf16[480,768]{1,0:T(8,128)(2,1)} %bitcast.19, bf16[96,512]{1,0:T(8,128)(2,1)} %bitcast.21, bf16[96,512]{1,0:T(8,128)(2,1)} %bitcast.22), custom_call_target="tpu_custom_call" | custom-call | tf_op jit(solution)/shard_map/pack/pallas_call | solution.py:116
  2.7 0.0 copy-start.2
  2.7 0.0 copy-start.1
  2.7 4.2 %collective-permute-start.4 = (bf16[1152,768]{1,0:T(8,128)(2,1)}, bf16[1152,768]{1,0:T(8,128)(2,1)}, u32[]{:S(2)}, u32[]{:S(2)}) collective-permute-start(bf16[1152,768]{1,0:T(8,128)(2,1)} %pack.1.refs_5_), channel_id=1, source_target_pairs={{0,16},{16,0},{1,17},{17,1},{2,18},{18,2},{3,19},{19,3},{4,20},{20... | collective-permute-start | bytes 5308424 | tf_op jit(solution)/shard_map/ppermute | solution.py:19
  6.9 2.1 %code_part.1 = bf16[16,16,512]{2,1,0:T(8,128)(2,1)} custom-call(bf16[16,768]{1,0:T(8,128)(2,1)} %x.1, bf16[768,512]{1,0:T(8,128)(2,1)} %w.1), custom_call_target="tpu_custom_call" | custom-call | tf_op jit(solution)/shard_map/code_part/pallas_call | solution.py:134
  9.0 42.5 %all_to_all.15 = bf16[16,16,512]{2,1,0:T(8,128)(2,1)S(1)} all-to-all(bf16[16,16,512]{2,1,0:T(8,128)(2,1)} %code_part.1), channel_id=1, replica_groups=mesh['z'=16,'yl'=2,'x'=4,'yh'=2,'c'=2] {'x','yh','c'}, dimensions={0} | all-to-all | bytes 524288 | tf_op jit(solution)/shard_map/all_to_all | solution.py:147
  51.5 0.0 copy-done.2
  51.5 32.3 %all_gather.7.refs_0_ = bf16[256,1280]{1,0:T(8,128)(2,1)S(1)} all-gather(bf16[16,1280]{1,0:T(8,128)(2,1)S(1)} %pad_maximum_fusion), channel_id=1, replica_groups=mesh['z'=16,'yl'=2,'x'=4,'yh'=2,'c'=2] {'z'}, dimensions={0}, use_global_device_ids=true | all-gather | bytes 696320 | tf_op jit(solution)/shard_map/all_gather | solution.py:150
  83.8 4.7 %collective-permute-start.3 = (bf16[256,768]{1,0:T(8,128)(2,1)S(1)}, bf16[256,768]{1,0:T(8,128)(2,1)S(1)}, u32[]{:S(2)}, u32[]{:S(2)}) collective-permute-start(bf16[256,768]{1,0:T(8,128)(2,1)S(1)} %slice.4), channel_id=1, source_target_pairs={{0,8},{4,12},{8,0},{12,4},{1,9},{5,13},{9,1},{13,5},{2,10},{6,14},... | collective-permute-start | bytes 1179656 | tf_op jit(solution)/shard_map/ppermute | solution.py:19
  88.5 2.2 %collective-permute-start.2 = (bf16[256,768]{1,0:T(8,128)(2,1)S(1)}, bf16[256,768]{1,0:T(8,128)(2,1)S(1)}, u32[]{:S(2)}, u32[]{:S(2)}) collective-permute-start(bf16[256,768]{1,0:T(8,128)(2,1)S(1)} %slice.4), channel_id=1, source_target_pairs={{0,4},{4,0},{8,12},{12,8},{1,5},{5,1},{9,13},{13,9},{2,6},{6,2},{1... | collective-permute-start | bytes 1179656 | tf_op jit(solution)/shard_map/ppermute | solution.py:19
  90.7 1.9 %collective-permute-start.1 = (bf16[256,768]{1,0:T(8,128)(2,1)S(1)}, bf16[256,768]{1,0:T(8,128)(2,1)S(1)}, u32[]{:S(2)}, u32[]{:S(2)}) collective-permute-start(bf16[256,768]{1,0:T(8,128)(2,1)S(1)} %slice.4), channel_id=1, source_target_pairs={{0,2},{2,0},{1,3},{3,1},{4,6},{6,4},{5,7},{7,5},{8,10},{10,8},{9,1... | collective-permute-start | bytes 1179656 | tf_op jit(solution)/shard_map/ppermute | solution.py:19
  92.6 10.7 %collective-permute-start = (bf16[256,768]{1,0:T(8,128)(2,1)S(1)}, bf16[256,768]{1,0:T(8,128)(2,1)S(1)}, u32[]{:S(2)}, u32[]{:S(2)}) collective-permute-start(bf16[256,768]{1,0:T(8,128)(2,1)S(1)} %slice.4), channel_id=1, source_target_pairs={{0,1},{1,0},{2,3},{3,2},{4,5},{5,4},{6,7},{7,6},{8,9},{9,8},{10,11... | collective-permute-start | bytes 1179656 | tf_op jit(solution)/shard_map/ppermute | solution.py:19
  103.4 0.0 collective-permute-done.3.refs_4_
  103.4 0.0 collective-permute-done.2.refs_3_
  103.4 0.0 collective-permute-done.1.refs_2_
  103.4 1.3 collective-permute-done.refs_1_
  104.7 0.0 collective-permute-done.4.refs_6_
  104.7 0.0 copy-done.1
  104.7 5.1 %ffn.1 = (f32[256,768]{1,0:T(8,128)}, bf16[256,768]{1,0:T(8,128)(2,1)}, bf16[256,768]{1,0:T(8,128)(2,1)}, bf16[256,768]{1,0:T(8,128)(2,1)}, bf16[256,768]{1,0:T(8,128)(2,1)}, /*index=5*/bf16[256,512]{1,0:T(8,128)(2,1)}) custom-call(bf16[256,1280]{1,0:T(8,128)(2,1)S(1)} %all_gather.7.refs_0_, bf16[256,768]{1,0:T(8,128)(2,1)S(1)} %collective-permute-done.refs_1_, ...), custom_call_target="tpu_custom_call" | custom-call | tf_op jit(solution)/shard_map/ffn/pallas_call | solution.py:84
  109.8 6.4 %all-to-all-start.2 = ((bf16[16,16,512]{2,1,0:T(8,128)(2,1)}), bf16[16,16,512]{2,1,0:T(8,128)(2,1)S(1)}, u32[]{:S(2)}, u32[]{:S(2)}) async-start(bf16[16,16,512]{2,1,0:T(8,128)(2,1)} %bitcast.20), calls=%async_computation.2 | async-start | bytes 524288 | tf_op jit(solution)/shard_map/all_to_all | solution.py:160
  116.2 7.8 %collective-permute-start.5 = (bf16[256,768]{1,0:T(8,128)(2,1)}, bf16[256,768]{1,0:T(8,128)(2,1)S(1)}, u32[]{:S(2)}, u32[]{:S(2)}) collective-permute-start(bf16[256,768]{1,0:T(8,128)(2,1)} %get-tuple-element.12), channel_id=1, source_target_pairs={{0,1},{1,0},{2,3},{3,2},{4,5},{5,4},{6,7},{7,6},{8,9},{9,8},{10,11... | collective-permute-start | bytes 1179656 | tf_op jit(solution)/shard_map/ppermute | solution.py:19
  124.0 2.1 %collective-permute-start.6 = (bf16[256,768]{1,0:T(8,128)(2,1)}, bf16[256,768]{1,0:T(8,128)(2,1)S(1)}, u32[]{:S(2)}, u32[]{:S(2)}) collective-permute-start(bf16[256,768]{1,0:T(8,128)(2,1)} %get-tuple-element.13), channel_id=1, source_target_pairs={{0,2},{2,0},{1,3},{3,1},{4,6},{6,4},{5,7},{7,5},{8,10},{10,8},{9,1... | collective-permute-start | bytes 1179656 | tf_op jit(solution)/shard_map/ppermute | solution.py:19
  126.0 3.1 %collective-permute-start.7 = (bf16[256,768]{1,0:T(8,128)(2,1)}, bf16[256,768]{1,0:T(8,128)(2,1)S(1)}, u32[]{:S(2)}, u32[]{:S(2)}) collective-permute-start(bf16[256,768]{1,0:T(8,128)(2,1)} %get-tuple-element.14), channel_id=1, source_target_pairs={{0,4},{4,0},{8,12},{12,8},{1,5},{5,1},{9,13},{13,9},{2,6},{6,2},{1... | collective-permute-start | bytes 1179656 | tf_op jit(solution)/shard_map/ppermute | solution.py:19
  129.1 2.5 %collective-permute-start.8 = (bf16[256,768]{1,0:T(8,128)(2,1)}, bf16[256,768]{1,0:T(8,128)(2,1)S(1)}, u32[]{:S(2)}, u32[]{:S(2)}) collective-permute-start(bf16[256,768]{1,0:T(8,128)(2,1)} %get-tuple-element.15), channel_id=1, source_target_pairs={{0,8},{4,12},{8,0},{12,4},{1,9},{5,13},{9,1},{13,5},{2,10},{6,14},... | collective-permute-start | bytes 1179656 | tf_op jit(solution)/shard_map/ppermute | solution.py:19
  131.6 0.0 collective-permute-done.5
  131.6 6.6 %collective-permute-done.6 = bf16[256,768]{1,0:T(8,128)(2,1)S(1)} collective-permute-done((bf16[256,768]{1,0:T(8,128)(2,1)}, bf16[256,768]{1,0:T(8,128)(2,1)S(1)}, u32[]{:S(2)}, u32[]{:S(2)}) %collective-permute-start.6) | collective-permute-done | bytes 393248 | tf_op jit(solution)/shard_map/ppermute | solution.py:19
  138.2 0.3 collective-permute-done.7
  138.5 9.0 %collective-permute-done.8 = bf16[256,768]{1,0:T(8,128)(2,1)S(1)} collective-permute-done((bf16[256,768]{1,0:T(8,128)(2,1)}, bf16[256,768]{1,0:T(8,128)(2,1)S(1)}, u32[]{:S(2)}, u32[]{:S(2)}) %collective-permute-start.8) | collective-permute-done | bytes 393248 | tf_op jit(solution)/shard_map/ppermute | solution.py:19
  147.5 2.1 %add_convert_fusion = bf16[256,768]{1,0:T(8,128)(2,1)} fusion(bf16[256,768]{1,0:T(8,128)(2,1)S(1)} %collective-permute-done.8, bf16[256,768]{1,0:T(8,128)(2,1)S(1)} %collective-permute-done.7, bf16[256,768]{1,0:T(8,128)(2,1)S(1)} %collective-permute-done.6, f32[256,768]{1,0:T(8,128)} %get-tuple-element.11, bf16[256,768]{1,0:T(8,128)(2,1)S(1)} %collective-permute-done.5), kind=kLoop, calls=%fused_computation.3 | loop fusion | flops 1769472 | bytes 2752512 | tf_op jit(solution)/shard_map/convert_element_type | solution.py:164
  149.6 0.0 all-to-all-done.2
  149.6 11.7 %all-to-all-start.1 = ((bf16[16,16,768]{2,1,0:T(8,128)(2,1)}), bf16[16,16,768]{2,1,0:T(8,128)(2,1)S(1)}, u32[]{:S(2)}, u32[]{:S(2)}) async-start(bf16[16,16,768]{2,1,0:T(8,128)(2,1)} %bitcast.8), calls=%async_computation.1 | async-start | bytes 786432 | tf_op jit(solution)/shard_map/all_to_all | solution.py:165
  161.4 25.6 %all-gather = bf16[256,512]{1,0:T(8,128)(2,1)S(1)} all-gather(bf16[16,512]{1,0:T(8,128)(2,1)S(1)} %reduce-precision_convert_fusion.1), channel_id=2, replica_groups=mesh['z'=16,'yl'=2,'x'=4,'yh'=2,'c'=2] {'x','yh','c'}, dimensions={0}, use_global_device_ids=true | all-gather | bytes 278528 | tf_op jit(solution)/shard_map/all_gather | solution.py:167
  187.0 0.0 all-to-all-done.1
  187.0 0.1 convert_reduce_fusion
  187.1 0.0 copy-done
  187.1 0.8 fusion
  (7 shorter events, 0.2 us)
Async XLA Ops:
  0.0 187.1 %copy-start = (bf16[512,768]{1,0:T(8,128)(2,1)S(1)}, bf16[512,768]{1,0:T(8,128)(2,1)}, u32[]{:S(2)}) copy-start(bf16[512,768]{1,0:T(8,128)(2,1)} %param.13) | copy-start | bytes 2359300
  2.7 48.8 %copy-start.2 = (bf16[16,768]{1,0:T(8,128)(2,1)S(1)}, bf16[16,768]{1,0:T(8,128)(2,1)}, u32[]{:S(2)}) copy-start(bf16[16,768]{1,0:T(8,128)(2,1)} %x.1) | copy-start | bytes 73732
  2.7 102.0 %copy-start.1 = (bf16[1152,768]{1,0:T(8,128)(2,1)S(1)}, bf16[1152,768]{1,0:T(8,128)(2,1)}, u32[]{:S(2)}) copy-start(bf16[1152,768]{1,0:T(8,128)(2,1)} %pack.1.refs_5_) | copy-start | bytes 5308420
  2.7 102.0 %collective-permute-start.4 = (bf16[1152,768]{1,0:T(8,128)(2,1)}, bf16[1152,768]{1,0:T(8,128)(2,1)}, u32[]{:S(2)}, u32[]{:S(2)}) collective-permute-start(bf16[1152,768]{1,0:T(8,128)(2,1)} %pack.1.refs_5_), channel_id=1, source_target_pairs={{0,16},{16,0},{1,17},{17,1},{2,18},{18,2},{3,19},{19,3},{4,20},{20... | collective-permute-start | bytes 5308424 | tf_op jit(solution)/shard_map/ppermute | solution.py:19
  83.8 19.5 %collective-permute-start.3 = (bf16[256,768]{1,0:T(8,128)(2,1)S(1)}, bf16[256,768]{1,0:T(8,128)(2,1)S(1)}, u32[]{:S(2)}, u32[]{:S(2)}) collective-permute-start(bf16[256,768]{1,0:T(8,128)(2,1)S(1)} %slice.4), channel_id=1, source_target_pairs={{0,8},{4,12},{8,0},{12,4},{1,9},{5,13},{9,1},{13,5},{2,10},{6,14},... | collective-permute-start | bytes 1179656 | tf_op jit(solution)/shard_map/ppermute | solution.py:19
  88.5 14.9 %collective-permute-start.2 = (bf16[256,768]{1,0:T(8,128)(2,1)S(1)}, bf16[256,768]{1,0:T(8,128)(2,1)S(1)}, u32[]{:S(2)}, u32[]{:S(2)}) collective-permute-start(bf16[256,768]{1,0:T(8,128)(2,1)S(1)} %slice.4), channel_id=1, source_target_pairs={{0,4},{4,0},{8,12},{12,8},{1,5},{5,1},{9,13},{13,9},{2,6},{6,2},{1... | collective-permute-start | bytes 1179656 | tf_op jit(solution)/shard_map/ppermute | solution.py:19
  90.7 12.7 %collective-permute-start.1 = (bf16[256,768]{1,0:T(8,128)(2,1)S(1)}, bf16[256,768]{1,0:T(8,128)(2,1)S(1)}, u32[]{:S(2)}, u32[]{:S(2)}) collective-permute-start(bf16[256,768]{1,0:T(8,128)(2,1)S(1)} %slice.4), channel_id=1, source_target_pairs={{0,2},{2,0},{1,3},{3,1},{4,6},{6,4},{5,7},{7,5},{8,10},{10,8},{9,1... | collective-permute-start | bytes 1179656 | tf_op jit(solution)/shard_map/ppermute | solution.py:19
  92.6 12.0 %collective-permute-start = (bf16[256,768]{1,0:T(8,128)(2,1)S(1)}, bf16[256,768]{1,0:T(8,128)(2,1)S(1)}, u32[]{:S(2)}, u32[]{:S(2)}) collective-permute-start(bf16[256,768]{1,0:T(8,128)(2,1)S(1)} %slice.4), channel_id=1, source_target_pairs={{0,1},{1,0},{2,3},{3,2},{4,5},{5,4},{6,7},{7,6},{8,9},{9,8},{10,11... | collective-permute-start | bytes 1179656 | tf_op jit(solution)/shard_map/ppermute | solution.py:19
  109.8 39.8 %all-to-all-start.2 = ((bf16[16,16,512]{2,1,0:T(8,128)(2,1)}), bf16[16,16,512]{2,1,0:T(8,128)(2,1)S(1)}, u32[]{:S(2)}, u32[]{:S(2)}) async-start(bf16[16,16,512]{2,1,0:T(8,128)(2,1)} %bitcast.20), calls=%async_computation.2 | async-start | bytes 524288 | tf_op jit(solution)/shard_map/all_to_all | solution.py:160
  116.2 15.4 %collective-permute-start.5 = (bf16[256,768]{1,0:T(8,128)(2,1)}, bf16[256,768]{1,0:T(8,128)(2,1)S(1)}, u32[]{:S(2)}, u32[]{:S(2)}) collective-permute-start(bf16[256,768]{1,0:T(8,128)(2,1)} %get-tuple-element.12), channel_id=1, source_target_pairs={{0,1},{1,0},{2,3},{3,2},{4,5},{5,4},{6,7},{7,6},{8,9},{9,8},{10,11... | collective-permute-start | bytes 1179656 | tf_op jit(solution)/shard_map/ppermute | solution.py:19
  124.0 14.3 %collective-permute-start.6 = (bf16[256,768]{1,0:T(8,128)(2,1)}, bf16[256,768]{1,0:T(8,128)(2,1)S(1)}, u32[]{:S(2)}, u32[]{:S(2)}) collective-permute-start(bf16[256,768]{1,0:T(8,128)(2,1)} %get-tuple-element.13), channel_id=1, source_target_pairs={{0,2},{2,0},{1,3},{3,1},{4,6},{6,4},{5,7},{7,5},{8,10},{10,8},{9,1... | collective-permute-start | bytes 1179656 | tf_op jit(solution)/shard_map/ppermute | solution.py:19
  126.0 12.5 %collective-permute-start.7 = (bf16[256,768]{1,0:T(8,128)(2,1)}, bf16[256,768]{1,0:T(8,128)(2,1)S(1)}, u32[]{:S(2)}, u32[]{:S(2)}) collective-permute-start(bf16[256,768]{1,0:T(8,128)(2,1)} %get-tuple-element.14), channel_id=1, source_target_pairs={{0,4},{4,0},{8,12},{12,8},{1,5},{5,1},{9,13},{13,9},{2,6},{6,2},{1... | collective-permute-start | bytes 1179656 | tf_op jit(solution)/shard_map/ppermute | solution.py:19
  129.1 18.4 %collective-permute-start.8 = (bf16[256,768]{1,0:T(8,128)(2,1)}, bf16[256,768]{1,0:T(8,128)(2,1)S(1)}, u32[]{:S(2)}, u32[]{:S(2)}) collective-permute-start(bf16[256,768]{1,0:T(8,128)(2,1)} %get-tuple-element.15), channel_id=1, source_target_pairs={{0,8},{4,12},{8,0},{12,4},{1,9},{5,13},{9,1},{13,5},{2,10},{6,14},... | collective-permute-start | bytes 1179656 | tf_op jit(solution)/shard_map/ppermute | solution.py:19
  149.6 37.4 %all-to-all-start.1 = ((bf16[16,16,768]{2,1,0:T(8,128)(2,1)}), bf16[16,16,768]{2,1,0:T(8,128)(2,1)S(1)}, u32[]{:S(2)}, u32[]{:S(2)}) async-start(bf16[16,16,768]{2,1,0:T(8,128)(2,1)} %bitcast.8), calls=%async_computation.1 | async-start | bytes 786432 | tf_op jit(solution)/shard_map/all_to_all | solution.py:165

commit v9 on v8

--- a/solution.py
+++ b/solution.py
@@ -29,6 +29,38 @@
 
 def total_of(stack):
     return lax.reduce_precision(jnp.sum(stack.astype(F32), axis=0), 8, 7).astype(BF16)
+
+
+def both(mine, other, lo, hi, at, size):
+    return jnp.concatenate([ref[lo:hi, at : at + size] for ref in (mine, other)], axis=0)
+
+
+def own_body(n, rank, gathered, mine, other_in, out, other, sems):
+    rows, db = other.shape[0] // 2, other.shape[1]
+    right = pltpu.make_async_copy(other_in.at[pl.ds(2 * n, rows)], other.at[pl.ds(0, rows)], sems.at[0])
+    up = pltpu.make_async_copy(other_in.at[pl.ds(0, rows)], other.at[pl.ds(rows, rows)], sems.at[1])
+    right.start()
+    up.start()
+    right.wait()
+    weight = jnp.concatenate([mine[2 * n : 2 * n + rows, :rank], other[:rows, :rank]], axis=0)
+    part = dot_nt(gathered[:, db:], weight)
+    up.wait()
+    out[...] = part + dot_nt(gathered[:, :db], jnp.concatenate([mine[:rows, :], other[rows:, :]], axis=0))
+
+
+def own_call(gathered, mine, other, kinds):
+    count, width = gathered.shape
+    db = mine.shape[1]
+    rows = mine.shape[0] // (2 * kinds + 2)
+    vmem = pl.BlockSpec(memory_space=pltpu.VMEM)
+    return pl.pallas_call(
+        functools.partial(own_body, kinds * rows, width - db),
+        out_shape=jax.ShapeDtypeStruct((count, 2 * rows), F32),
+        in_specs=[vmem, vmem, pl.BlockSpec(memory_space=pl.ANY)],
+        scratch_shapes=[pltpu.VMEM((2 * rows, db), BF16), pltpu.SemaphoreType.DMA((2,))],
+        compiler_params=pltpu.CompilerParams(vmem_limit_bytes=FFN_MIB * 2**20),
+        name="ffn_own",
+    )(gathered, mine, other)
 
 
 def ffn_body(kinds, rows, rank, *refs):
@@ -50,36 +82,30 @@
         copy.start()
         return copy
 
-    def both(lo, hi, at, size):
-        return jnp.concatenate([ref[lo:hi, at : at + size] for ref in (mine, other)], axis=0)
-
-    low_rank, ups, downs = fetch(0, 2 * n, 2 * rows), fetch(1, 0, n), fetch(2, n, n)
+    ups, low_rank, downs = fetch(1, rows, n - rows), fetch(0, 2 * n, 2 * rows), fetch(2, n, n)
+    pre = xs[0][...]
+    ups.wait()
+    for k in range(1, kinds):
+        pre = pre + dot_nt(xs[k][...], both(mine, other, k * rows, (k + 1) * rows, 0, db))
+    hidden = (0.5 * pre * (1.0 + lax.erf(pre * (0.5**0.5)))).astype(BF16)
     low_rank.wait()
-    pre = dot_nt(xs[0][:, db:], both(2 * n, 2 * n + rows, 0, rank))
-    ups.wait()
-    pre = pre + dot_nt(xs[0][:, :db], both(0, rows, 0, db))
-    for k in range(1, kinds):
-        pre = pre + dot_nt(xs[k][...], both(k * rows, (k + 1) * rows, 0, db))
-    hidden = (0.5 * pre * (1.0 + lax.erf(pre * (0.5**0.5)))).astype(BF16)
     back = stage[kinds]
-    back[:, :head] = dot_nn(hidden, both(2 * n, 2 * n + rows, rank, head)).astype(BF16)
-    back[:, head:] = dot_nn(hidden, both(2 * n + rows, 2 * n + 2 * rows, 0, rank - head)).astype(BF16)
+    back[:, :head] = dot_nn(hidden, both(mine, other, 2 * n, 2 * n + rows, rank, head)).astype(BF16)
+    back[:, head:] = dot_nn(hidden, both(mine, other, 2 * n + rows, 2 * n + 2 * rows, 0, rank - head)).astype(BF16)
     stores = [stored(kinds)]
     downs.wait()
     for k in range(kinds):
         lo = n + k * rows
-        stage[k][...] = dot_nn(hidden, both(lo, lo + rows, 0, db)).astype(outs[k].dtype)
+        stage[k][...] = dot_nn(hidden, both(mine, other, lo, lo + rows, 0, db)).astype(outs[k].dtype)
         stores.append(stored(k))
     for copy in stores:
         copy.wait()
 
 
-def ffn_call(gathered, pieces, mine, other, kinds):
-    count, width = gathered.shape
-    db = mine.shape[1]
-    rank = width - db
+def ffn_call(own, pieces, mine, other, rank, kinds):
+    count, db = own.shape[0], mine.shape[1]
     rows = mine.shape[0] // (2 * kinds + 2)
-    args = (gathered, *pieces, mine, other)
+    args = (own, *pieces, mine, other)
     outs = [((count, db), F32)] + [((count, db), BF16)] * (kinds - 1) + [((count, rank), BF16)]
     return pl.pallas_call(
         functools.partial(ffn_body, kinds, rows, rank),
@@ -153,7 +179,8 @@
     for axis, bit in LEVEL_AXES:
         pieces.append(swap(own, axis, bit))
 
-    own_total, *terms, back = ffn_call(gathered, pieces, packed, other, kinds)
+    own_pre = own_call(gathered, packed, other, kinds)
+    own_total, *terms, back = ffn_call(own_pre, pieces, packed, other, rank, kinds)
     sent = []
     for part, (axis, bit) in zip(terms, LEVEL_AXES):
         sent.append(swap(part, axis, bit))

time: 189 us -> 188 us (level)
  transfers between devices with their start and end apart: 11 -> 11, of which waited for: 4 -> 3; matrix products, arithmetic and copies ran while one was open for 1% -> 1% of each run, Pallas kernels for 1% -> 2%
where the time goes in v9:
time: 188 us; the launch traced here: 187 us
  blocking collectives  100 us (53%)
  starting transfers between devices  57.1 us (30%)
  waiting for transfers between devices  15.9 us (8%)
  Pallas kernels  10.6 us (6%)
  other arithmetic  2.3 us (1%)
    all_to_all x1, blocking collectives, per_device(): stack = lax.all_to_all(stack, FEAT, 0, 0, tiled=True)  42.5 us
    ppermute x9, starting transfers between devices, swap(): lax.ppermute(array, axis, [(i, i ^ 1 << bit) for i in range(lax.axis_size...  38.9 us
    all_gather x1, blocking collectives, per_device(): gathered = lax.all_gather(mine, 'z', axis=0, tiled=True)  32.3 us
    all_gather x1, blocking collectives, per_device(): back = lax.all_gather(back, FEAT, axis=0)  25.6 us
    ppermute x9, waiting for transfers between devices, swap(): lax.ppermute(array, axis, [(i, i ^ 1 << bit) for i in range(lax.axis_size...  15.9 us
    all_to_all x1, starting transfers between devices, per_device(): total = lax.all_to_all(total.reshape(nz, count, db), 'z', 0, 0, tiled=True)  11.7 us
    all_to_all x1, starting transfers between devices, per_device(): back = lax.all_to_all(back.reshape(nz, count, rank), 'z', 0, 0, tiled=True)  6.38 us
    pallas_call x1, Pallas kernels, ffn_call(): pl.pallas_call(functools.partial(ffn_body, kinds, rows, rank), out_shape=...  4.53 us
  transfers between devices with their start and end apart: 11, of which 3 were waited for; matrix products, arithmetic and copies ran while one was open for 1% of the time, Pallas kernels for 2%

profile of v9, /device:TPU:1, one launch (start us, length us, event | category | flops | bytes accessed | tf_op | source)
XLA Modules:
  0.0 187.3 jit_solution(13463845588654680405)
XLA Ops:
  0.0 0.0 copy-start
  0.0 2.7 %pack.1.mine.refs_5_ = bf16[1152,768]{1,0:T(8,128)(2,1)} custom-call(bf16[480,768]{1,0:T(8,128)(2,1)} %bitcast.18, bf16[480,768]{1,0:T(8,128)(2,1)} %bitcast.19, bf16[96,512]{1,0:T(8,128)(2,1)} %bitcast.21, bf16[96,512]{1,0:T(8,128)(2,1)} %bitcast.22), custom_call_target="tpu_custom_call" | custom-call | tf_op jit(solution)/shard_map/pack/pallas_call | solution.py:142
  2.7 0.0 copy-start.2
  2.7 0.0 copy-start.1
  2.7 4.2 %collective-permute-start = (bf16[1152,768]{1,0:T(8,128)(2,1)}, bf16[1152,768]{1,0:T(8,128)(2,1)}, u32[]{:S(2)}, u32[]{:S(2)}) collective-permute-start(bf16[1152,768]{1,0:T(8,128)(2,1)} %pack.1.mine.refs_5_), channel_id=1, source_target_pairs={{0,16},{16,0},{1,17},{17,1},{2,18},{18,2},{3,19},{19,3},{4,20},{20... | collective-permute-start | bytes 5308424 | tf_op jit(solution)/shard_map/ppermute | solution.py:19
  6.9 2.1 %code_part.1 = bf16[16,16,512]{2,1,0:T(8,128)(2,1)} custom-call(bf16[16,768]{1,0:T(8,128)(2,1)} %x.1, bf16[768,512]{1,0:T(8,128)(2,1)} %w.1), custom_call_target="tpu_custom_call" | custom-call | tf_op jit(solution)/shard_map/code_part/pallas_call | solution.py:160
  9.0 42.5 %all_to_all.15 = bf16[16,16,512]{2,1,0:T(8,128)(2,1)S(1)} all-to-all(bf16[16,16,512]{2,1,0:T(8,128)(2,1)} %code_part.1), channel_id=1, replica_groups=mesh['z'=16,'yl'=2,'x'=4,'yh'=2,'c'=2] {'x','yh','c'}, dimensions={0} | all-to-all | bytes 524288 | tf_op jit(solution)/shard_map/all_to_all | solution.py:173
  51.5 0.0 copy-done.2
  51.5 32.3 %all_gather.7.gathered = bf16[256,1280]{1,0:T(8,128)(2,1)S(1)} all-gather(bf16[16,1280]{1,0:T(8,128)(2,1)S(1)} %pad_maximum_fusion), channel_id=1, replica_groups=mesh['z'=16,'yl'=2,'x'=4,'yh'=2,'c'=2] {'z'}, dimensions={0}, use_global_device_ids=true | all-gather | bytes 696320 | tf_op jit(solution)/shard_map/all_gather | solution.py:176
  83.8 4.7 %collective-permute-start.4 = (bf16[256,768]{1,0:T(8,128)(2,1)S(1)}, bf16[256,768]{1,0:T(8,128)(2,1)S(1)}, u32[]{:S(2)}, u32[]{:S(2)}) collective-permute-start(bf16[256,768]{1,0:T(8,128)(2,1)S(1)} %slice.4), channel_id=1, source_target_pairs={{0,8},{4,12},{8,0},{12,4},{1,9},{5,13},{9,1},{13,5},{2,10},{6,14},... | collective-permute-start | bytes 1179656 | tf_op jit(solution)/shard_map/ppermute | solution.py:19
  88.5 2.2 %collective-permute-start.3 = (bf16[256,768]{1,0:T(8,128)(2,1)S(1)}, bf16[256,768]{1,0:T(8,128)(2,1)S(1)}, u32[]{:S(2)}, u32[]{:S(2)}) collective-permute-start(bf16[256,768]{1,0:T(8,128)(2,1)S(1)} %slice.4), channel_id=1, source_target_pairs={{0,4},{4,0},{8,12},{12,8},{1,5},{5,1},{9,13},{13,9},{2,6},{6,2},{1... | collective-permute-start | bytes 1179656 | tf_op jit(solution)/shard_map/ppermute | solution.py:19
  90.7 1.9 %collective-permute-start.2 = (bf16[256,768]{1,0:T(8,128)(2,1)S(1)}, bf16[256,768]{1,0:T(8,128)(2,1)S(1)}, u32[]{:S(2)}, u32[]{:S(2)}) collective-permute-start(bf16[256,768]{1,0:T(8,128)(2,1)S(1)} %slice.4), channel_id=1, source_target_pairs={{0,2},{2,0},{1,3},{3,1},{4,6},{6,4},{5,7},{7,5},{8,10},{10,8},{9,1... | collective-permute-start | bytes 1179656 | tf_op jit(solution)/shard_map/ppermute | solution.py:19
  92.6 10.7 %collective-permute-start.1 = (bf16[256,768]{1,0:T(8,128)(2,1)S(1)}, bf16[256,768]{1,0:T(8,128)(2,1)S(1)}, u32[]{:S(2)}, u32[]{:S(2)}) collective-permute-start(bf16[256,768]{1,0:T(8,128)(2,1)S(1)} %slice.4), channel_id=1, source_target_pairs={{0,1},{1,0},{2,3},{3,2},{4,5},{5,4},{6,7},{7,6},{8,9},{9,8},{10,11... | collective-permute-start | bytes 1179656 | tf_op jit(solution)/shard_map/ppermute | solution.py:19
  103.4 0.0 collective-permute-done.other_in.refs_6_
  103.4 0.0 copy-done.1
  103.4 1.4 ffn_own.1.refs_0_
  104.7 0.0 collective-permute-done.4.refs_4_
  104.7 0.0 collective-permute-done.3.refs_3_
  104.8 0.0 collective-permute-done.2.refs_2_
  104.8 0.0 collective-permute-done.1.refs_1_
  104.8 4.5 %ffn.1 = (f32[256,768]{1,0:T(8,128)}, bf16[256,768]{1,0:T(8,128)(2,1)}, bf16[256,768]{1,0:T(8,128)(2,1)}, bf16[256,768]{1,0:T(8,128)(2,1)}, bf16[256,768]{1,0:T(8,128)(2,1)}, /*index=5*/bf16[256,512]{1,0:T(8,128)(2,1)}) custom-call(f32[256,192]{1,0:T(8,128)S(1)} %ffn_own.1.refs_0_, bf16[256,768]{1,0:T(8,128)(2,1)S(1)} %collective-permute-done.1.refs_1_, ...), custom_call_target="tpu_custom_call" | custom-call | tf_op jit(solution)/shard_map/ffn/pallas_call | solution.py:110
  109.3 6.4 %all-to-all-start.2 = ((bf16[16,16,512]{2,1,0:T(8,128)(2,1)}), bf16[16,16,512]{2,1,0:T(8,128)(2,1)S(1)}, u32[]{:S(2)}, u32[]{:S(2)}) async-start(bf16[16,16,512]{2,1,0:T(8,128)(2,1)} %bitcast.20), calls=%async_computation.2 | async-start | bytes 524288 | tf_op jit(solution)/shard_map/all_to_all | solution.py:187
  115.7 7.7 %collective-permute-start.5 = (bf16[256,768]{1,0:T(8,128)(2,1)}, bf16[256,768]{1,0:T(8,128)(2,1)S(1)}, u32[]{:S(2)}, u32[]{:S(2)}) collective-permute-start(bf16[256,768]{1,0:T(8,128)(2,1)} %get-tuple-element.12), channel_id=1, source_target_pairs={{0,1},{1,0},{2,3},{3,2},{4,5},{5,4},{6,7},{7,6},{8,9},{9,8},{10,11... | collective-permute-start | bytes 1179656 | tf_op jit(solution)/shard_map/ppermute | solution.py:19
  123.4 2.1 %collective-permute-start.6 = (bf16[256,768]{1,0:T(8,128)(2,1)}, bf16[256,768]{1,0:T(8,128)(2,1)S(1)}, u32[]{:S(2)}, u32[]{:S(2)}) collective-permute-start(bf16[256,768]{1,0:T(8,128)(2,1)} %get-tuple-element.13), channel_id=1, source_target_pairs={{0,2},{2,0},{1,3},{3,1},{4,6},{6,4},{5,7},{7,5},{8,10},{10,8},{9,1... | collective-permute-start | bytes 1179656 | tf_op jit(solution)/shard_map/ppermute | solution.py:19
  125.5 3.1 %collective-permute-start.7 = (bf16[256,768]{1,0:T(8,128)(2,1)}, bf16[256,768]{1,0:T(8,128)(2,1)S(1)}, u32[]{:S(2)}, u32[]{:S(2)}) collective-permute-start(bf16[256,768]{1,0:T(8,128)(2,1)} %get-tuple-element.14), channel_id=1, source_target_pairs={{0,4},{4,0},{8,12},{12,8},{1,5},{5,1},{9,13},{13,9},{2,6},{6,2},{1... | collective-permute-start | bytes 1179656 | tf_op jit(solution)/shard_map/ppermute | solution.py:19
  128.5 2.5 %collective-permute-start.8 = (bf16[256,768]{1,0:T(8,128)(2,1)}, bf16[256,768]{1,0:T(8,128)(2,1)S(1)}, u32[]{:S(2)}, u32[]{:S(2)}) collective-permute-start(bf16[256,768]{1,0:T(8,128)(2,1)} %get-tuple-element.15), channel_id=1, source_target_pairs={{0,8},{4,12},{8,0},{12,4},{1,9},{5,13},{9,1},{13,5},{2,10},{6,14},... | collective-permute-start | bytes 1179656 | tf_op jit(solution)/shard_map/ppermute | solution.py:19
  131.0 0.0 collective-permute-done.5
  131.0 6.6 %collective-permute-done.6 = bf16[256,768]{1,0:T(8,128)(2,1)S(1)} collective-permute-done((bf16[256,768]{1,0:T(8,128)(2,1)}, bf16[256,768]{1,0:T(8,128)(2,1)S(1)}, u32[]{:S(2)}, u32[]{:S(2)}) %collective-permute-start.6) | collective-permute-done | bytes 393248 | tf_op jit(solution)/shard_map/ppermute | solution.py:19
  137.7 0.3 collective-permute-done.7
  137.9 9.0 %collective-permute-done.8 = bf16[256,768]{1,0:T(8,128)(2,1)S(1)} collective-permute-done((bf16[256,768]{1,0:T(8,128)(2,1)}, bf16[256,768]{1,0:T(8,128)(2,1)S(1)}, u32[]{:S(2)}, u32[]{:S(2)}) %collective-permute-start.8) | collective-permute-done | bytes 393248 | tf_op jit(solution)/shard_map/ppermute | solution.py:19
  146.9 2.1 %add_convert_fusion = bf16[256,768]{1,0:T(8,128)(2,1)} fusion(bf16[256,768]{1,0:T(8,128)(2,1)S(1)} %collective-permute-done.8, bf16[256,768]{1,0:T(8,128)(2,1)S(1)} %collective-permute-done.7, bf16[256,768]{1,0:T(8,128)(2,1)S(1)} %collective-permute-done.6, f32[256,768]{1,0:T(8,128)} %get-tuple-element.11, bf16[256,768]{1,0:T(8,128)(2,1)S(1)} %collective-permute-done.5), kind=kLoop, calls=%fused_computation.3 | loop fusion | flops 1769472 | bytes 2752512 | tf_op jit(solution)/shard_map/convert_element_type | solution.py:191
  149.0 0.0 all-to-all-done.2
  149.0 11.7 %all-to-all-start.1 = ((bf16[16,16,768]{2,1,0:T(8,128)(2,1)}), bf16[16,16,768]{2,1,0:T(8,128)(2,1)S(1)}, u32[]{:S(2)}, u32[]{:S(2)}) async-start(bf16[16,16,768]{2,1,0:T(8,128)(2,1)} %bitcast.8), calls=%async_computation.1 | async-start | bytes 786432 | tf_op jit(solution)/shard_map/all_to_all | solution.py:192
  160.8 25.6 %all-gather = bf16[256,512]{1,0:T(8,128)(2,1)S(1)} all-gather(bf16[16,512]{1,0:T(8,128)(2,1)S(1)} %reduce-precision_convert_fusion.1), channel_id=2, replica_groups=mesh['z'=16,'yl'=2,'x'=4,'yh'=2,'c'=2] {'x','yh','c'}, dimensions={0}, use_global_device_ids=true | all-gather | bytes 278528 | tf_op jit(solution)/shard_map/all_gather | solution.py:194
  186.4 0.0 all-to-all-done.1
  186.4 0.1 convert_reduce_fusion
  186.5 0.0 copy-done
  186.5 0.8 fusion
  (7 shorter events, 0.2 us)
Async XLA Ops:
  0.0 186.5 %copy-start = (bf16[512,768]{1,0:T(8,128)(2,1)S(1)}, bf16[512,768]{1,0:T(8,128)(2,1)}, u32[]{:S(2)}) copy-start(bf16[512,768]{1,0:T(8,128)(2,1)} %param.13) | copy-start | bytes 2359300
  2.7 48.8 %copy-start.2 = (bf16[16,768]{1,0:T(8,128)(2,1)S(1)}, bf16[16,768]{1,0:T(8,128)(2,1)}, u32[]{:S(2)}) copy-start(bf16[16,768]{1,0:T(8,128)(2,1)} %x.1) | copy-start | bytes 73732
  2.7 100.7 %copy-start.1 = (bf16[1152,768]{1,0:T(8,128)(2,1)S(1)}, bf16[1152,768]{1,0:T(8,128)(2,1)}, u32[]{:S(2)}) copy-start(bf16[1152,768]{1,0:T(8,128)(2,1)} %pack.1.mine.refs_5_) | copy-start | bytes 5308420
  2.7 100.7 %collective-permute-start = (bf16[1152,768]{1,0:T(8,128)(2,1)}, bf16[1152,768]{1,0:T(8,128)(2,1)}, u32[]{:S(2)}, u32[]{:S(2)}) collective-permute-start(bf16[1152,768]{1,0:T(8,128)(2,1)} %pack.1.mine.refs_5_), channel_id=1, source_target_pairs={{0,16},{16,0},{1,17},{17,1},{2,18},{18,2},{3,19},{19,3},{4,20},{20... | collective-permute-start | bytes 5308424 | tf_op jit(solution)/shard_map/ppermute | solution.py:19
  83.8 20.9 %collective-permute-start.4 = (bf16[256,768]{1,0:T(8,128)(2,1)S(1)}, bf16[256,768]{1,0:T(8,128)(2,1)S(1)}, u32[]{:S(2)}, u32[]{:S(2)}) collective-permute-start(bf16[256,768]{1,0:T(8,128)(2,1)S(1)} %slice.4), channel_id=1, source_target_pairs={{0,8},{4,12},{8,0},{12,4},{1,9},{5,13},{9,1},{13,5},{2,10},{6,14},... | collective-permute-start | bytes 1179656 | tf_op jit(solution)/shard_map/ppermute | solution.py:19
  88.5 16.3 %collective-permute-start.3 = (bf16[256,768]{1,0:T(8,128)(2,1)S(1)}, bf16[256,768]{1,0:T(8,128)(2,1)S(1)}, u32[]{:S(2)}, u32[]{:S(2)}) collective-permute-start(bf16[256,768]{1,0:T(8,128)(2,1)S(1)} %slice.4), channel_id=1, source_target_pairs={{0,4},{4,0},{8,12},{12,8},{1,5},{5,1},{9,13},{13,9},{2,6},{6,2},{1... | collective-permute-start | bytes 1179656 | tf_op jit(solution)/shard_map/ppermute | solution.py:19
  90.7 14.0 %collective-permute-start.2 = (bf16[256,768]{1,0:T(8,128)(2,1)S(1)}, bf16[256,768]{1,0:T(8,128)(2,1)S(1)}, u32[]{:S(2)}, u32[]{:S(2)}) collective-permute-start(bf16[256,768]{1,0:T(8,128)(2,1)S(1)} %slice.4), channel_id=1, source_target_pairs={{0,2},{2,0},{1,3},{3,1},{4,6},{6,4},{5,7},{7,5},{8,10},{10,8},{9,1... | collective-permute-start | bytes 1179656 | tf_op jit(solution)/shard_map/ppermute | solution.py:19
  92.6 12.1 %collective-permute-start.1 = (bf16[256,768]{1,0:T(8,128)(2,1)S(1)}, bf16[256,768]{1,0:T(8,128)(2,1)S(1)}, u32[]{:S(2)}, u32[]{:S(2)}) collective-permute-start(bf16[256,768]{1,0:T(8,128)(2,1)S(1)} %slice.4), channel_id=1, source_target_pairs={{0,1},{1,0},{2,3},{3,2},{4,5},{5,4},{6,7},{7,6},{8,9},{9,8},{10,11... | collective-permute-start | bytes 1179656 | tf_op jit(solution)/shard_map/ppermute | solution.py:19
  109.3 39.7 %all-to-all-start.2 = ((bf16[16,16,512]{2,1,0:T(8,128)(2,1)}), bf16[16,16,512]{2,1,0:T(8,128)(2,1)S(1)}, u32[]{:S(2)}, u32[]{:S(2)}) async-start(bf16[16,16,512]{2,1,0:T(8,128)(2,1)} %bitcast.20), calls=%async_computation.2 | async-start | bytes 524288 | tf_op jit(solution)/shard_map/all_to_all | solution.py:187
  115.7 15.3 %collective-permute-start.5 = (bf16[256,768]{1,0:T(8,128)(2,1)}, bf16[256,768]{1,0:T(8,128)(2,1)S(1)}, u32[]{:S(2)}, u32[]{:S(2)}) collective-permute-start(bf16[256,768]{1,0:T(8,128)(2,1)} %get-tuple-element.12), channel_id=1, source_target_pairs={{0,1},{1,0},{2,3},{3,2},{4,5},{5,4},{6,7},{7,6},{8,9},{9,8},{10,11... | collective-permute-start | bytes 1179656 | tf_op jit(solution)/shard_map/ppermute | solution.py:19
  123.4 14.3 %collective-permute-start.6 = (bf16[256,768]{1,0:T(8,128)(2,1)}, bf16[256,768]{1,0:T(8,128)(2,1)S(1)}, u32[]{:S(2)}, u32[]{:S(2)}) collective-permute-start(bf16[256,768]{1,0:T(8,128)(2,1)} %get-tuple-element.13), channel_id=1, source_target_pairs={{0,2},{2,0},{1,3},{3,1},{4,6},{6,4},{5,7},{7,5},{8,10},{10,8},{9,1... | collective-permute-start | bytes 1179656 | tf_op jit(solution)/shard_map/ppermute | solution.py:19
  125.5 12.5 %collective-permute-start.7 = (bf16[256,768]{1,0:T(8,128)(2,1)}, bf16[256,768]{1,0:T(8,128)(2,1)S(1)}, u32[]{:S(2)}, u32[]{:S(2)}) collective-permute-start(bf16[256,768]{1,0:T(8,128)(2,1)} %get-tuple-element.14), channel_id=1, source_target_pairs={{0,4},{4,0},{8,12},{12,8},{1,5},{5,1},{9,13},{13,9},{2,6},{6,2},{1... | collective-permute-start | bytes 1179656 | tf_op jit(solution)/shard_map/ppermute | solution.py:19
  128.5 18.4 %collective-permute-start.8 = (bf16[256,768]{1,0:T(8,128)(2,1)}, bf16[256,768]{1,0:T(8,128)(2,1)S(1)}, u32[]{:S(2)}, u32[]{:S(2)}) collective-permute-start(bf16[256,768]{1,0:T(8,128)(2,1)} %get-tuple-element.15), channel_id=1, source_target_pairs={{0,8},{4,12},{8,0},{12,4},{1,9},{5,13},{9,1},{13,5},{2,10},{6,14},... | collective-permute-start | bytes 1179656 | tf_op jit(solution)/shard_map/ppermute | solution.py:19
  149.0 37.4 %all-to-all-start.1 = ((bf16[16,16,768]{2,1,0:T(8,128)(2,1)}), bf16[16,16,768]{2,1,0:T(8,128)(2,1)S(1)}, u32[]{:S(2)}, u32[]{:S(2)}) async-start(bf16[16,16,768]{2,1,0:T(8,128)(2,1)} %bitcast.8), calls=%async_computation.1 | async-start | bytes 786432 | tf_op jit(solution)/shard_map/all_to_all | solution.py:192

commit v10 on v9

--- a/solution.py
+++ b/solution.py
@@ -149,15 +149,42 @@
     )(up, down, right, left)
 
 
-def code_body(x, w, stack):
-    part = dot_nn(x[...], w[...]).astype(BF16)
-    for i in range(stack.shape[0]):
-        stack[i] = part
+def code_body(chunks, x, w_in, stack, w, part, sems, out_sems):
+    size = w.shape[0] // chunks
+    loads = []
+    for i in range(chunks):
+        piece = pl.ds(i * size, size)
+        loads.append(pltpu.make_async_copy(w_in.at[piece], w.at[piece], sems.at[i]))
+        loads[i].start()
+    total = jnp.zeros(part.shape, F32)
+    for i in range(chunks):
+        loads[i].wait()
+        total = total + dot_nn(x[:, i * size : (i + 1) * size], w[i * size : (i + 1) * size, :])
+    part[...] = total.astype(BF16)
+    stores = [pltpu.make_async_copy(part, stack.at[i], out_sems.at[i]) for i in range(stack.shape[0])]
+    for copy in stores:
+        copy.start()
+    for copy in stores:
+        copy.wait()
 
 
 def code_call(tokens, up_left, n):
-    shape = jax.ShapeDtypeStruct((n, tokens.shape[0], up_left.shape[1]), BF16)
-    return pl.pallas_call(code_body, out_shape=shape, name="code_part", compiler_params=pltpu.CompilerParams(vmem_limit_bytes=60 * 2**20))(tokens, up_left)
+    count, rank = tokens.shape[0], up_left.shape[1]
+    chunks = 3
+    return pl.pallas_call(
+        functools.partial(code_body, chunks),
+        out_shape=pltpu.HBM((n, count, rank), BF16),
+        in_specs=[pl.BlockSpec(memory_space=pltpu.VMEM), pl.BlockSpec(memory_space=pl.ANY)],
+        out_specs=pl.BlockSpec(memory_space=pl.ANY),
+        scratch_shapes=[
+            pltpu.VMEM(up_left.shape, BF16),
+            pltpu.VMEM((count, rank), BF16),
+            pltpu.SemaphoreType.DMA((chunks,)),
+            pltpu.SemaphoreType.DMA((n,)),
+        ],
+        name="code_part",
+        compiler_params=pltpu.CompilerParams(vmem_limit_bytes=60 * 2**20),
+    )(tokens, up_left)
 
 
 def per_device(tokens, up_weight, down_weight, up_left, up_right, down_left, down_right):

time: 188 us -> 188 us (level)
  no operation moved by 1% of the time
where the time goes in v10:
time: 188 us; the launch traced here: 187 us
  blocking collectives  99.5 us (53%)
  starting transfers between devices  57.1 us (30%)
  waiting for transfers between devices  15.9 us (8%)
  Pallas kernels  11.4 us (6%)
  other arithmetic  2.3 us (1%)
    all_to_all x1, blocking collectives, per_device(): stack = lax.all_to_all(stack, FEAT, 0, 0, tiled=True)  41.7 us
    ppermute x9, starting transfers between devices, swap(): lax.ppermute(array, axis, [(i, i ^ 1 << bit) for i in range(lax.axis_size...  38.9 us
    all_gather x1, blocking collectives, per_device(): gathered = lax.all_gather(mine, 'z', axis=0, tiled=True)  32.3 us
    all_gather x1, blocking collectives, per_device(): back = lax.all_gather(back, FEAT, axis=0)  25.6 us
    ppermute x9, waiting for transfers between devices, swap(): lax.ppermute(array, axis, [(i, i ^ 1 << bit) for i in range(lax.axis_size...  15.9 us
    all_to_all x1, starting transfers between devices, per_device(): total = lax.all_to_all(total.reshape(nz, count, db), 'z', 0, 0, tiled=True)  11.7 us
    all_to_all x1, starting transfers between devices, per_device(): back = lax.all_to_all(back.reshape(nz, count, rank), 'z', 0, 0, tiled=True)  6.38 us
    pallas_call x1, Pallas kernels, ffn_call(): pl.pallas_call(functools.partial(ffn_body, kinds, rows, rank), out_shape=...  4.53 us
  transfers between devices with their start and end apart: 11, of which 3 were waited for; matrix products, arithmetic and copies ran while one was open for 1% of the time, Pallas kernels for 2%

profile of v10, /device:TPU:1, one launch (start us, length us, event | category | flops | bytes accessed | tf_op | source)
XLA Modules:
  0.0 187.3 jit_solution(8558519284565880494)
XLA Ops:
  0.0 0.0 copy-start
  0.0 2.7 %pack.1.mine.refs_5_ = bf16[1152,768]{1,0:T(8,128)(2,1)} custom-call(bf16[480,768]{1,0:T(8,128)(2,1)} %bitcast.18, bf16[480,768]{1,0:T(8,128)(2,1)} %bitcast.19, bf16[96,512]{1,0:T(8,128)(2,1)} %bitcast.21, bf16[96,512]{1,0:T(8,128)(2,1)} %bitcast.22), custom_call_target="tpu_custom_call" | custom-call | tf_op jit(solution)/shard_map/pack/pallas_call | solution.py:142
  2.7 0.0 copy-start.2
  2.7 0.0 copy-start.1
  2.7 4.2 %collective-permute-start = (bf16[1152,768]{1,0:T(8,128)(2,1)}, bf16[1152,768]{1,0:T(8,128)(2,1)}, u32[]{:S(2)}, u32[]{:S(2)}) collective-permute-start(bf16[1152,768]{1,0:T(8,128)(2,1)} %pack.1.mine.refs_5_), channel_id=1, source_target_pairs={{0,16},{16,0},{1,17},{17,1},{2,18},{18,2},{3,19},{19,3},{4,20},{20... | collective-permute-start | bytes 5308424 | tf_op jit(solution)/shard_map/ppermute | solution.py:19
  6.9 2.9 %code_part.1 = bf16[16,16,512]{2,1,0:T(8,128)(2,1)} custom-call(bf16[16,768]{1,0:T(8,128)(2,1)} %x.1, bf16[768,512]{1,0:T(8,128)(2,1)} %w_in.1), custom_call_target="tpu_custom_call" | custom-call | tf_op jit(solution)/shard_map/code_part/pallas_call | solution.py:174
  9.7 41.7 %all_to_all.15 = bf16[16,16,512]{2,1,0:T(8,128)(2,1)S(1)} all-to-all(bf16[16,16,512]{2,1,0:T(8,128)(2,1)} %code_part.1), channel_id=1, replica_groups=mesh['z'=16,'yl'=2,'x'=4,'yh'=2,'c'=2] {'x','yh','c'}, dimensions={0} | all-to-all | bytes 524288 | tf_op jit(solution)/shard_map/all_to_all | solution.py:200
  51.5 0.0 copy-done.2
  51.5 32.3 %all_gather.7.gathered = bf16[256,1280]{1,0:T(8,128)(2,1)S(1)} all-gather(bf16[16,1280]{1,0:T(8,128)(2,1)S(1)} %pad_maximum_fusion), channel_id=1, replica_groups=mesh['z'=16,'yl'=2,'x'=4,'yh'=2,'c'=2] {'z'}, dimensions={0}, use_global_device_ids=true | all-gather | bytes 696320 | tf_op jit(solution)/shard_map/all_gather | solution.py:203
  83.8 4.7 %collective-permute-start.4 = (bf16[256,768]{1,0:T(8,128)(2,1)S(1)}, bf16[256,768]{1,0:T(8,128)(2,1)S(1)}, u32[]{:S(2)}, u32[]{:S(2)}) collective-permute-start(bf16[256,768]{1,0:T(8,128)(2,1)S(1)} %slice.4), channel_id=1, source_target_pairs={{0,8},{4,12},{8,0},{12,4},{1,9},{5,13},{9,1},{13,5},{2,10},{6,14},... | collective-permute-start | bytes 1179656 | tf_op jit(solution)/shard_map/ppermute | solution.py:19
  88.5 2.2 %collective-permute-start.3 = (bf16[256,768]{1,0:T(8,128)(2,1)S(1)}, bf16[256,768]{1,0:T(8,128)(2,1)S(1)}, u32[]{:S(2)}, u32[]{:S(2)}) collective-permute-start(bf16[256,768]{1,0:T(8,128)(2,1)S(1)} %slice.4), channel_id=1, source_target_pairs={{0,4},{4,0},{8,12},{12,8},{1,5},{5,1},{9,13},{13,9},{2,6},{6,2},{1... | collective-permute-start | bytes 1179656 | tf_op jit(solution)/shard_map/ppermute | solution.py:19
  90.7 1.9 %collective-permute-start.2 = (bf16[256,768]{1,0:T(8,128)(2,1)S(1)}, bf16[256,768]{1,0:T(8,128)(2,1)S(1)}, u32[]{:S(2)}, u32[]{:S(2)}) collective-permute-start(bf16[256,768]{1,0:T(8,128)(2,1)S(1)} %slice.4), channel_id=1, source_target_pairs={{0,2},{2,0},{1,3},{3,1},{4,6},{6,4},{5,7},{7,5},{8,10},{10,8},{9,1... | collective-permute-start | bytes 1179656 | tf_op jit(solution)/shard_map/ppermute | solution.py:19
  92.6 10.7 %collective-permute-start.1 = (bf16[256,768]{1,0:T(8,128)(2,1)S(1)}, bf16[256,768]{1,0:T(8,128)(2,1)S(1)}, u32[]{:S(2)}, u32[]{:S(2)}) collective-permute-start(bf16[256,768]{1,0:T(8,128)(2,1)S(1)} %slice.4), channel_id=1, source_target_pairs={{0,1},{1,0},{2,3},{3,2},{4,5},{5,4},{6,7},{7,6},{8,9},{9,8},{10,11... | collective-permute-start | bytes 1179656 | tf_op jit(solution)/shard_map/ppermute | solution.py:19
  103.4 0.0 collective-permute-done.other_in.refs_6_
  103.4 0.0 copy-done.1
  103.4 1.4 ffn_own.1.refs_0_
  104.7 0.0 collective-permute-done.4.refs_4_
  104.7 0.0 collective-permute-done.3.refs_3_
  104.8 0.0 collective-permute-done.2.refs_2_
  104.8 0.0 collective-permute-done.1.refs_1_
  104.8 4.5 %ffn.1 = (f32[256,768]{1,0:T(8,128)}, bf16[256,768]{1,0:T(8,128)(2,1)}, bf16[256,768]{1,0:T(8,128)(2,1)}, bf16[256,768]{1,0:T(8,128)(2,1)}, bf16[256,768]{1,0:T(8,128)(2,1)}, /*index=5*/bf16[256,512]{1,0:T(8,128)(2,1)}) custom-call(f32[256,192]{1,0:T(8,128)S(1)} %ffn_own.1.refs_0_, bf16[256,768]{1,0:T(8,128)(2,1)S(1)} %collective-permute-done.1.refs_1_, ...), custom_call_target="tpu_custom_call" | custom-call | tf_op jit(solution)/shard_map/ffn/pallas_call | solution.py:110
  109.3 6.4 %all-to-all-start.2 = ((bf16[16,16,512]{2,1,0:T(8,128)(2,1)}), bf16[16,16,512]{2,1,0:T(8,128)(2,1)S(1)}, u32[]{:S(2)}, u32[]{:S(2)}) async-start(bf16[16,16,512]{2,1,0:T(8,128)(2,1)} %bitcast.20), calls=%async_computation.2 | async-start | bytes 524288 | tf_op jit(solution)/shard_map/all_to_all | solution.py:214
  115.7 7.7 %collective-permute-start.5 = (bf16[256,768]{1,0:T(8,128)(2,1)}, bf16[256,768]{1,0:T(8,128)(2,1)S(1)}, u32[]{:S(2)}, u32[]{:S(2)}) collective-permute-start(bf16[256,768]{1,0:T(8,128)(2,1)} %get-tuple-element.12), channel_id=1, source_target_pairs={{0,1},{1,0},{2,3},{3,2},{4,5},{5,4},{6,7},{7,6},{8,9},{9,8},{10,11... | collective-permute-start | bytes 1179656 | tf_op jit(solution)/shard_map/ppermute | solution.py:19
  123.4 2.1 %collective-permute-start.6 = (bf16[256,768]{1,0:T(8,128)(2,1)}, bf16[256,768]{1,0:T(8,128)(2,1)S(1)}, u32[]{:S(2)}, u32[]{:S(2)}) collective-permute-start(bf16[256,768]{1,0:T(8,128)(2,1)} %get-tuple-element.13), channel_id=1, source_target_pairs={{0,2},{2,0},{1,3},{3,1},{4,6},{6,4},{5,7},{7,5},{8,10},{10,8},{9,1... | collective-permute-start | bytes 1179656 | tf_op jit(solution)/shard_map/ppermute | solution.py:19
  125.5 3.1 %collective-permute-start.7 = (bf16[256,768]{1,0:T(8,128)(2,1)}, bf16[256,768]{1,0:T(8,128)(2,1)S(1)}, u32[]{:S(2)}, u32[]{:S(2)}) collective-permute-start(bf16[256,768]{1,0:T(8,128)(2,1)} %get-tuple-element.14), channel_id=1, source_target_pairs={{0,4},{4,0},{8,12},{12,8},{1,5},{5,1},{9,13},{13,9},{2,6},{6,2},{1... | collective-permute-start | bytes 1179656 | tf_op jit(solution)/shard_map/ppermute | solution.py:19
  128.5 2.5 %collective-permute-start.8 = (bf16[256,768]{1,0:T(8,128)(2,1)}, bf16[256,768]{1,0:T(8,128)(2,1)S(1)}, u32[]{:S(2)}, u32[]{:S(2)}) collective-permute-start(bf16[256,768]{1,0:T(8,128)(2,1)} %get-tuple-element.15), channel_id=1, source_target_pairs={{0,8},{4,12},{8,0},{12,4},{1,9},{5,13},{9,1},{13,5},{2,10},{6,14},... | collective-permute-start | bytes 1179656 | tf_op jit(solution)/shard_map/ppermute | solution.py:19
  131.0 0.0 collective-permute-done.5
  131.0 6.6 %collective-permute-done.6 = bf16[256,768]{1,0:T(8,128)(2,1)S(1)} collective-permute-done((bf16[256,768]{1,0:T(8,128)(2,1)}, bf16[256,768]{1,0:T(8,128)(2,1)S(1)}, u32[]{:S(2)}, u32[]{:S(2)}) %collective-permute-start.6) | collective-permute-done | bytes 393248 | tf_op jit(solution)/shard_map/ppermute | solution.py:19
  137.7 0.3 collective-permute-done.7
  137.9 9.0 %collective-permute-done.8 = bf16[256,768]{1,0:T(8,128)(2,1)S(1)} collective-permute-done((bf16[256,768]{1,0:T(8,128)(2,1)}, bf16[256,768]{1,0:T(8,128)(2,1)S(1)}, u32[]{:S(2)}, u32[]{:S(2)}) %collective-permute-start.8) | collective-permute-done | bytes 393248 | tf_op jit(solution)/shard_map/ppermute | solution.py:19
  146.9 2.1 %add_convert_fusion = bf16[256,768]{1,0:T(8,128)(2,1)} fusion(bf16[256,768]{1,0:T(8,128)(2,1)S(1)} %collective-permute-done.8, bf16[256,768]{1,0:T(8,128)(2,1)S(1)} %collective-permute-done.7, bf16[256,768]{1,0:T(8,128)(2,1)S(1)} %collective-permute-done.6, f32[256,768]{1,0:T(8,128)} %get-tuple-element.11, bf16[256,768]{1,0:T(8,128)(2,1)S(1)} %collective-permute-done.5), kind=kLoop, calls=%fused_computation.3 | loop fusion | flops 1769472 | bytes 2752512 | tf_op jit(solution)/shard_map/convert_element_type | solution.py:218
  149.0 0.0 all-to-all-done.2
  149.0 11.7 %all-to-all-start.1 = ((bf16[16,16,768]{2,1,0:T(8,128)(2,1)}), bf16[16,16,768]{2,1,0:T(8,128)(2,1)S(1)}, u32[]{:S(2)}, u32[]{:S(2)}) async-start(bf16[16,16,768]{2,1,0:T(8,128)(2,1)} %bitcast.8), calls=%async_computation.1 | async-start | bytes 786432 | tf_op jit(solution)/shard_map/all_to_all | solution.py:219
  160.8 25.6 %all-gather = bf16[256,512]{1,0:T(8,128)(2,1)S(1)} all-gather(bf16[16,512]{1,0:T(8,128)(2,1)S(1)} %reduce-precision_convert_fusion.1), channel_id=2, replica_groups=mesh['z'=16,'yl'=2,'x'=4,'yh'=2,'c'=2] {'x','yh','c'}, dimensions={0}, use_global_device_ids=true | all-gather | bytes 278528 | tf_op jit(solution)/shard_map/all_gather | solution.py:221
  186.4 0.0 all-to-all-done.1
  186.4 0.1 convert_reduce_fusion
  186.5 0.0 copy-done
  186.5 0.8 fusion
  (7 shorter events, 0.2 us)
Async XLA Ops:
  0.0 186.5 %copy-start = (bf16[512,768]{1,0:T(8,128)(2,1)S(1)}, bf16[512,768]{1,0:T(8,128)(2,1)}, u32[]{:S(2)}) copy-start(bf16[512,768]{1,0:T(8,128)(2,1)} %param.13) | copy-start | bytes 2359300
  2.7 48.8 %copy-start.2 = (bf16[16,768]{1,0:T(8,128)(2,1)S(1)}, bf16[16,768]{1,0:T(8,128)(2,1)}, u32[]{:S(2)}) copy-start(bf16[16,768]{1,0:T(8,128)(2,1)} %x.1) | copy-start | bytes 73732
  2.7 100.7 %copy-start.1 = (bf16[1152,768]{1,0:T(8,128)(2,1)S(1)}, bf16[1152,768]{1,0:T(8,128)(2,1)}, u32[]{:S(2)}) copy-start(bf16[1152,768]{1,0:T(8,128)(2,1)} %pack.1.mine.refs_5_) | copy-start | bytes 5308420
  2.7 100.7 %collective-permute-start = (bf16[1152,768]{1,0:T(8,128)(2,1)}, bf16[1152,768]{1,0:T(8,128)(2,1)}, u32[]{:S(2)}, u32[]{:S(2)}) collective-permute-start(bf16[1152,768]{1,0:T(8,128)(2,1)} %pack.1.mine.refs_5_), channel_id=1, source_target_pairs={{0,16},{16,0},{1,17},{17,1},{2,18},{18,2},{3,19},{19,3},{4,20},{20... | collective-permute-start | bytes 5308424 | tf_op jit(solution)/shard_map/ppermute | solution.py:19
  83.8 20.9 %collective-permute-start.4 = (bf16[256,768]{1,0:T(8,128)(2,1)S(1)}, bf16[256,768]{1,0:T(8,128)(2,1)S(1)}, u32[]{:S(2)}, u32[]{:S(2)}) collective-permute-start(bf16[256,768]{1,0:T(8,128)(2,1)S(1)} %slice.4), channel_id=1, source_target_pairs={{0,8},{4,12},{8,0},{12,4},{1,9},{5,13},{9,1},{13,5},{2,10},{6,14},... | collective-permute-start | bytes 1179656 | tf_op jit(solution)/shard_map/ppermute | solution.py:19
  88.5 16.3 %collective-permute-start.3 = (bf16[256,768]{1,0:T(8,128)(2,1)S(1)}, bf16[256,768]{1,0:T(8,128)(2,1)S(1)}, u32[]{:S(2)}, u32[]{:S(2)}) collective-permute-start(bf16[256,768]{1,0:T(8,128)(2,1)S(1)} %slice.4), channel_id=1, source_target_pairs={{0,4},{4,0},{8,12},{12,8},{1,5},{5,1},{9,13},{13,9},{2,6},{6,2},{1... | collective-permute-start | bytes 1179656 | tf_op jit(solution)/shard_map/ppermute | solution.py:19
  90.7 14.0 %collective-permute-start.2 = (bf16[256,768]{1,0:T(8,128)(2,1)S(1)}, bf16[256,768]{1,0:T(8,128)(2,1)S(1)}, u32[]{:S(2)}, u32[]{:S(2)}) collective-permute-start(bf16[256,768]{1,0:T(8,128)(2,1)S(1)} %slice.4), channel_id=1, source_target_pairs={{0,2},{2,0},{1,3},{3,1},{4,6},{6,4},{5,7},{7,5},{8,10},{10,8},{9,1... | collective-permute-start | bytes 1179656 | tf_op jit(solution)/shard_map/ppermute | solution.py:19
  92.6 12.1 %collective-permute-start.1 = (bf16[256,768]{1,0:T(8,128)(2,1)S(1)}, bf16[256,768]{1,0:T(8,128)(2,1)S(1)}, u32[]{:S(2)}, u32[]{:S(2)}) collective-permute-start(bf16[256,768]{1,0:T(8,128)(2,1)S(1)} %slice.4), channel_id=1, source_target_pairs={{0,1},{1,0},{2,3},{3,2},{4,5},{5,4},{6,7},{7,6},{8,9},{9,8},{10,11... | collective-permute-start | bytes 1179656 | tf_op jit(solution)/shard_map/ppermute | solution.py:19
  109.3 39.7 %all-to-all-start.2 = ((bf16[16,16,512]{2,1,0:T(8,128)(2,1)}), bf16[16,16,512]{2,1,0:T(8,128)(2,1)S(1)}, u32[]{:S(2)}, u32[]{:S(2)}) async-start(bf16[16,16,512]{2,1,0:T(8,128)(2,1)} %bitcast.20), calls=%async_computation.2 | async-start | bytes 524288 | tf_op jit(solution)/shard_map/all_to_all | solution.py:214
  115.7 15.3 %collective-permute-start.5 = (bf16[256,768]{1,0:T(8,128)(2,1)}, bf16[256,768]{1,0:T(8,128)(2,1)S(1)}, u32[]{:S(2)}, u32[]{:S(2)}) collective-permute-start(bf16[256,768]{1,0:T(8,128)(2,1)} %get-tuple-element.12), channel_id=1, source_target_pairs={{0,1},{1,0},{2,3},{3,2},{4,5},{5,4},{6,7},{7,6},{8,9},{9,8},{10,11... | collective-permute-start | bytes 1179656 | tf_op jit(solution)/shard_map/ppermute | solution.py:19
  123.4 14.3 %collective-permute-start.6 = (bf16[256,768]{1,0:T(8,128)(2,1)}, bf16[256,768]{1,0:T(8,128)(2,1)S(1)}, u32[]{:S(2)}, u32[]{:S(2)}) collective-permute-start(bf16[256,768]{1,0:T(8,128)(2,1)} %get-tuple-element.13), channel_id=1, source_target_pairs={{0,2},{2,0},{1,3},{3,1},{4,6},{6,4},{5,7},{7,5},{8,10},{10,8},{9,1... | collective-permute-start | bytes 1179656 | tf_op jit(solution)/shard_map/ppermute | solution.py:19
  125.5 12.5 %collective-permute-start.7 = (bf16[256,768]{1,0:T(8,128)(2,1)}, bf16[256,768]{1,0:T(8,128)(2,1)S(1)}, u32[]{:S(2)}, u32[]{:S(2)}) collective-permute-start(bf16[256,768]{1,0:T(8,128)(2,1)} %get-tuple-element.14), channel_id=1, source_target_pairs={{0,4},{4,0},{8,12},{12,8},{1,5},{5,1},{9,13},{13,9},{2,6},{6,2},{1... | collective-permute-start | bytes 1179656 | tf_op jit(solution)/shard_map/ppermute | solution.py:19
  128.5 18.4 %collective-permute-start.8 = (bf16[256,768]{1,0:T(8,128)(2,1)}, bf16[256,768]{1,0:T(8,128)(2,1)S(1)}, u32[]{:S(2)}, u32[]{:S(2)}) collective-permute-start(bf16[256,768]{1,0:T(8,128)(2,1)} %get-tuple-element.15), channel_id=1, source_target_pairs={{0,8},{4,12},{8,0},{12,4},{1,9},{5,13},{9,1},{13,5},{2,10},{6,14},... | collective-permute-start | bytes 1179656 | tf_op jit(solution)/shard_map/ppermute | solution.py:19
  149.0 37.4 %all-to-all-start.1 = ((bf16[16,16,768]{2,1,0:T(8,128)(2,1)}), bf16[16,16,768]{2,1,0:T(8,128)(2,1)S(1)}, u32[]{:S(2)}, u32[]{:S(2)}) async-start(bf16[16,16,768]{2,1,0:T(8,128)(2,1)} %bitcast.8), calls=%async_computation.1 | async-start | bytes 786432 | tf_op jit(solution)/shard_map/all_to_all | solution.py:219
